TPU v7x, 512 devices: a whole 4x4x16 slice. The times are simulated.
512 devices in a mesh: dp: 32 (over z, core), shard: 16 (over y, x).
Axes of the slice: x: 4, y: 4, z: 16, core: 2. Of those that a mesh axis runs over, the one named last changes fastest.
Arguments:
- tokens: bfloat16 [196608, 512], P(('dp', 'shard')), may hold values from -24 to 24
- w_proj: bfloat16 [512, 2048], P(None, 'shard'), may hold values from -0.25 to 0.25
- w_out: bfloat16 [512, 512], replicated, may hold values from -0.25 to 0.25
- item_rows: bfloat16 [16384, 512], P('shard'), may hold values from -1.5 to 1.5
- lengths: int32 [512, 4], P(('dp', 'shard')), may hold values from 1 to 192, 384 in all within a row
- target_owner: int32 [196608, 1], P(('dp', 'shard')), may hold values from 0 to 15; in each aligned block of 384 rows (0 to 383, 384 to 767, ...) at most 48 rows name the same one
- target_row: int32 [196608], P(('dp', 'shard')), may hold values from 0 to 1023
- negative_rows: int32 [1024], P('shard'), may hold values from 0 to 1023
Outputs:
- grad_tokens: bfloat16 [196608, 512], P(('dp', 'shard'))
- weight_grads: float32 [512, 512], replicated
- item_grads: float32 [16384, 512], P('shard')
Inputs may be any that keep to these rules, and one draw needn't show every extreme that they name: `target_owner`: in the rows of one device no owner is named more than 48 times, a bound that some block reaches.
All inputs are finite; a program needn't handle non-finite values.
Results may differ from a plain program's by a relative error of at most 0.02.
Values may be sent and summed in bfloat16 or wider, within the bound.
No kernel may reach another device: no remote copies, remote signals or barrier semaphores. Data moves between devices by JAX's collectives and lax.ppermute only.
A program may use at most 64 MiB of HBM per device.

v0:
```python
import jax
import jax.numpy as jnp
from jax import lax
from jax.sharding import PartitionSpec as P

D = 512
HEADS = 4
DH = 128
MAXLEN = 192


epsilon = 1e-06
logit_divisor = 0.015625
loss_scale = 512.0


def reduce_last_dimension(operand, other_side):
    return lax.dot_general(
        operand, other_side, (((1,), (1,)), ((), ())), preferred_element_type=jnp.float32
    )


def contract_first(operand, other_side):
    return lax.dot_general(
        operand, other_side, (((0,), (0,)), ((), ())), preferred_element_type=jnp.float32
    )


def silu_slope(values):
    sigmoid = jax.nn.sigmoid(values)
    return sigmoid * (1.0 + values * (1.0 - sigmoid))


def history_mask(lengths_row, rows_count):
    history_ends = jnp.cumsum(lengths_row)
    positions = jnp.arange(rows_count, dtype=jnp.int32)
    history_ids = jnp.sum((positions[:, None] >= history_ends[None, :-1]).astype(jnp.int32), axis=1)
    visible = (history_ids[:, None] == history_ids[None, :]) & (
        positions[None, :] <= positions[:, None]
    )
    return jnp.where(visible, 1.0, 0.0).astype(jnp.float32)


def head_columns(activated, section, head_index):
    first_col = section * D + head_index * DH
    return activated[:, first_col : first_col + DH]


def head_scores(queries, key_rows):
    return reduce_last_dimension(queries, key_rows) * DH ** (-0.5)


def head_weights(scores, visible):
    return (jax.nn.silu(scores) * visible * (1.0 / MAXLEN)).astype(jnp.bfloat16)


def forward_layer(tokens, project, w_out, visible):
    wide_tokens = tokens.astype(jnp.float32)
    input_scale = lax.rsqrt(jnp.mean(wide_tokens * wide_tokens, axis=1, keepdims=True) + epsilon)
    normed = (wide_tokens * input_scale).astype(jnp.bfloat16)
    pre_act = project(normed)
    activated = lax.optimization_barrier(jax.nn.silu(pre_act).astype(jnp.bfloat16))
    heads_out = []
    for head_index in range(HEADS):
        queries = head_columns(activated, 2, head_index)
        key_rows = head_columns(activated, 3, head_index)
        value_rows = head_columns(activated, 1, head_index)
        weights = head_weights(head_scores(queries, key_rows), visible)
        heads_out.append(jnp.dot(weights, value_rows, preferred_element_type=jnp.float32))
    joined = lax.optimization_barrier(jnp.concatenate(heads_out, axis=1).astype(jnp.bfloat16))
    joined_wide = joined.astype(jnp.float32)
    middle_scale = lax.rsqrt(jnp.mean(joined_wide * joined_wide, axis=1, keepdims=True) + epsilon)
    gate_wide = activated[:, :D].astype(jnp.float32)
    gated = (joined_wide * middle_scale * gate_wide).astype(jnp.bfloat16)
    layer_out = wide_tokens + jnp.dot(gated, w_out, preferred_element_type=jnp.float32)
    return (layer_out, (wide_tokens, input_scale, pre_act, activated, joined, middle_scale, gated))


def loss_head(layer_out, clicked_product_vectors, sampled_decoys):
    out_scale = lax.rsqrt(jnp.sum(layer_out * layer_out, axis=1, keepdims=True) + epsilon)
    normalized_example_vectors = lax.optimization_barrier(
        (layer_out * out_scale).astype(jnp.bfloat16)
    )
    normalized_complete_embedding = normalized_example_vectors.astype(jnp.float32)
    correct_logit_entry = (
        jnp.sum(normalized_complete_embedding * clicked_product_vectors.astype(jnp.float32), axis=1)
        / logit_divisor
    )
    decoy_logit_entries = (
        reduce_last_dimension(normalized_example_vectors, sampled_decoys) / logit_divisor
    )
    target_exp = jnp.exp(correct_logit_entry)
    negative_exp = jnp.exp(decoy_logit_entries)
    totals = target_exp + jnp.sum(negative_exp, axis=1)
    target_prob = target_exp / totals
    negative_probs = (loss_scale * negative_exp / totals[:, None]).astype(jnp.bfloat16)
    target_coef = (loss_scale * (target_prob - 1.0))[:, None]
    grad_unit = target_coef * clicked_product_vectors.astype(jnp.float32) + jnp.dot(
        negative_probs, sampled_decoys, preferred_element_type=jnp.float32
    )
    grad_out = out_scale * grad_unit - layer_out * out_scale**3 * jnp.sum(
        layer_out * grad_unit, axis=1, keepdims=True
    )
    grad_target = target_coef * normalized_complete_embedding
    return (grad_out, grad_target, negative_probs, normalized_example_vectors)


def backward_layer(grad_out, saved_state, project_back, w_out, visible):
    wide_tokens, input_scale, pre_act, activated, joined, middle_scale, gated = saved_state
    grad_out_b = grad_out.astype(jnp.bfloat16)
    weight_part = contract_first(gated, grad_out_b)
    grad_gated = reduce_last_dimension(grad_out_b, w_out)
    joined_wide = joined.astype(jnp.float32)
    gate_wide = activated[:, :D].astype(jnp.float32)
    grad_gate = grad_gated * joined_wide * middle_scale
    grad_norm = grad_gated * gate_wide
    grad_joined = middle_scale * grad_norm - joined_wide * middle_scale**3 * jnp.mean(
        joined_wide * grad_norm, axis=1, keepdims=True
    )
    grad_joined_b = grad_joined.astype(jnp.bfloat16)
    grad_values = []
    grad_queries = []
    grad_keys = []
    for head_index in range(HEADS):
        queries = head_columns(activated, 2, head_index)
        key_rows = head_columns(activated, 3, head_index)
        value_rows = head_columns(activated, 1, head_index)
        scores = head_scores(queries, key_rows)
        weights = head_weights(scores, visible)
        grad_head = grad_joined_b[:, head_index * DH : (head_index + 1) * DH]
        grad_weights = reduce_last_dimension(grad_head, value_rows)
        grad_values.append(contract_first(weights, grad_head))
        grad_scores = (
            grad_weights * visible * (1.0 / MAXLEN) * silu_slope(scores) * DH ** (-0.5)
        ).astype(jnp.bfloat16)
        grad_queries.append(jnp.dot(grad_scores, key_rows, preferred_element_type=jnp.float32))
        grad_keys.append(contract_first(grad_scores, queries))
    grad_act = jnp.concatenate([grad_gate] + grad_values + grad_queries + grad_keys, axis=1)
    grad_pre = (grad_act * silu_slope(pre_act)).astype(jnp.bfloat16)
    grad_normed = project_back(grad_pre)
    grad_input = input_scale * grad_normed - wide_tokens * input_scale**3 * jnp.mean(
        wide_tokens * grad_normed, axis=1, keepdims=True
    )
    return ((grad_out + grad_input).astype(jnp.bfloat16), weight_part)


def finish_rows(grad_items, rows_wide):
    item_scale = lax.rsqrt(jnp.sum(rows_wide * rows_wide, axis=1, keepdims=True) + epsilon)
    return (
        item_scale * grad_items
        - rows_wide * item_scale**3 * jnp.sum(rows_wide * grad_items, axis=1, keepdims=True)
    ) / loss_scale


def shards(tokens, w_proj, w_out, item_rows, lengths, target_owner, target_row, negative_rows):
    tok_rows = tokens.shape[0]
    model_width = tokens.shape[1]
    shard_count = lax.axis_size("shard")
    capacity = 2 * tok_rows // shard_count
    visible = history_mask(lengths[0], tok_rows)

    def project(normed):
        return jnp.dot(
            normed,
            lax.all_gather(w_proj, "shard", axis=1, tiled=True),
            preferred_element_type=jnp.float32,
        )

    def project_back(grad_pre):
        return reduce_last_dimension(grad_pre, lax.all_gather(w_proj, "shard", axis=1, tiled=True))

    rows_wide = item_rows.astype(jnp.float32)
    item_scale = lax.rsqrt(jnp.sum(rows_wide * rows_wide, axis=1, keepdims=True) + epsilon)
    unit_items = (rows_wide * item_scale).astype(jnp.bfloat16)
    owners = target_owner[:, 0]
    owner_hits = (owners[:, None] == jnp.arange(shard_count, dtype=jnp.int32)[None, :]).astype(
        jnp.int32
    )
    earlier = jnp.cumsum(owner_hits, axis=0) - owner_hits
    slot_index = jnp.sum(earlier * owner_hits, axis=1)
    position = owners * capacity + slot_index
    requests = jnp.zeros((shard_count * capacity,), jnp.int32).at[position].set(target_row)
    asked_rows = lax.all_to_all(
        requests.reshape(shard_count, capacity), "shard", split_axis=0, concat_axis=0, tiled=True
    )
    asked_flat = asked_rows.reshape(-1)
    served = jnp.take(unit_items, asked_flat, axis=0).reshape(shard_count, capacity, model_width)
    fetched = lax.all_to_all(served, "shard", split_axis=0, concat_axis=0, tiled=True)
    clicked_product_vectors = jnp.take(
        fetched.reshape(shard_count * capacity, model_width), position, axis=0
    )
    sampled_decoys = lax.all_gather(
        jnp.take(unit_items, negative_rows, axis=0), "shard", axis=0, tiled=True
    )
    layer_out, saved_state = forward_layer(tokens, project, w_out, visible)
    grad_out, grad_target, negative_probs, normalized_example_vectors = loss_head(
        layer_out, clicked_product_vectors, sampled_decoys
    )
    grad_tokens, weight_part = backward_layer(grad_out, saved_state, project_back, w_out, visible)
    outgoing = (
        jnp.zeros((shard_count * capacity, model_width), jnp.float32).at[position].set(grad_target)
    )
    returned = lax.all_to_all(
        outgoing.reshape(shard_count, capacity, model_width).astype(jnp.bfloat16),
        "shard",
        split_axis=0,
        concat_axis=0,
        tiled=True,
    ).astype(jnp.float32)
    grad_items = (
        jnp.zeros((item_rows.shape[0], model_width), jnp.float32)
        .at[asked_flat]
        .add(returned.reshape(-1, model_width))
    )
    own_negatives = lax.psum_scatter(
        contract_first(negative_probs, normalized_example_vectors).astype(jnp.bfloat16),
        "shard",
        scatter_dimension=0,
        tiled=True,
    ).astype(jnp.float32)
    grad_items = grad_items.at[negative_rows].add(own_negatives)
    grad_items = lax.psum(grad_items.astype(jnp.bfloat16), "dp").astype(jnp.float32)
    item_grads = finish_rows(grad_items, rows_wide)
    weight_grads = lax.psum(weight_part, ("dp", "shard")) / loss_scale
    return (grad_tokens, weight_grads, item_grads)


def solution(mesh):
    in_specs = (
        P(("dp", "shard"), None),
        P(None, "shard"),
        P(),
        P("shard", None),
        P(("dp", "shard"), None),
        P(("dp", "shard"), None),
        P(("dp", "shard")),
        P("shard"),
    )
    out_specs = (P(("dp", "shard"), None), P(), P("shard", None))
    return jax.shard_map(shards, mesh=mesh, in_specs=in_specs, out_specs=out_specs, check_vma=False)
```

profile of v0, /device:TPU:1, one launch (start us, length us, event | category | flops | bytes accessed | tf_op | source)
XLA Modules:
  0.0 947.1 jit_solution(13287930997406279915)
XLA Ops:
  9.9 1.2 and_reduce_fusion
  11.1 3.1 scatter_custom_fusion
  14.9 7.6 all-to-all-start
  23.3 1.2 fusion.29
  24.4 1.5 fusion.2
  27.0 1.8 all-to-all-done
  30.1 2.7 gather_fusion
  32.9 1.1 broadcast_select_fusion
  33.9 4.9 all-to-all-start.1
  41.2 9.7 %all-to-all-done.1 = bf16[16,48,512]{2,1,0:T(8,128)(2,1)S(1)} async-done(((bf16[16,48,512]{2,1,0:T(8,128)(2,1)}), bf16[16,48,512]{2,1,0:T(8,128)(2,1)S(1)}, u32[]{:S(2)}, u32[]{:S(2)}) %all-to-all-start.1) | async-done | bytes 786464 | tf_op jit(solution)/shard_map/all_to_all | solution.py:188
  50.9 2.6 gather_fusion.1
  53.4 26.8 %all-gather.3.cloned.1.call-done = bf16[512,2048]{1,0:T(8,128)(2,1)} async-done(((bf16[512,128]{1,0:T(8,128)(2,1)}), bf16[512,2048]{1,0:T(8,128)(2,1)}) %all-gather.3.cloned.1.call-update) | async-done | bytes 2097168 | tf_op jit(solution)/shard_map/all_gather | solution.py:165
  80.3 4.5 multiply_convert_fusion.1
  85.6 1.6 fusion.45
  91.4 49.3 %all-gather.5.cloned.1.call-done = bf16[1024,512]{1,0:T(8,128)(2,1)} async-done(((bf16[64,512]{1,0:T(8,128)(2,1)}), bf16[1024,512]{1,0:T(8,128)(2,1)}) %all-gather.5.cloned.1.call-update) | async-done | bytes 1048592 | tf_op jit(solution)/shard_map/all_gather | solution.py:192
  140.7 1.9 fusion.106
  143.9 1.9 convolution_convert_fusion
  145.7 2.4 multiply_reduce_fusion
  148.2 1.5 multiply_subtract_fusion
  150.4 1.2 fusion.41
  151.6 1.1 fusion.23
  152.8 1.1 fusion.22
  154.0 3.3 scatter_custom_fusion.1
  157.2 2.4 convert_element_type.136
  159.6 4.4 all-to-all-start.2
  164.4 1.7 fusion.24
  166.1 1.0 convolution_dynamic-update-slice_fusion.11
  167.1 1.0 convolution_dynamic-update-slice_fusion.10
  168.1 1.0 convolution_dynamic-update-slice_fusion.9
  169.1 1.0 convolution_dynamic-update-slice_fusion.8
  171.0 1.0 convolution_dynamic-update-slice_fusion.6
  173.4 1.0 convolution_dynamic-update-slice_fusion.4
  174.3 1.0 convolution_dynamic-update-slice_fusion.3
  175.3 1.0 convolution_dynamic-update-slice_fusion.2
  176.3 1.0 convolution_dynamic-update-slice_fusion.1
  177.3 1.0 convolution_dynamic-update-slice_fusion
  178.3 1.5 fusion.57
  179.9 5.8 fusion.35
  186.2 8.6 scatter_custom_fusion.2
  194.9 48.8 %reduce-scatter.2.cloned.1.call-done = bf16[64,512]{1,0:T(8,128)(2,1)} async-done(((bf16[1024,512]{1,0:T(8,128)(2,1)}), bf16[64,512]{1,0:T(8,128)(2,1)}) %reduce-scatter.2.cloned.1.call-update) | async-done | bytes 65552 | tf_op jit(solution)/shard_map/reduce_scatter | solution.py:215
  243.6 4.1 scatter_custom_fusion.3
  247.8 2.8 convert_element_type.140
  250.7 1.7 fusion.34
  252.4 472.2 %all-reduce.3.cloned.1.call-done = f32[512,512]{1,0:T(8,128)} async-done(((f32[512,512]{1,0:T(8,128)}), f32[512,512]{1,0:T(8,128)}) %all-reduce.3.cloned.1.call-update) | async-done | bytes 1048592 | tf_op jit(solution)/shard_map/psum | solution.py:224
  724.5 2.3 broadcast_multiply_fusion
  726.8 210.2 %all-reduce.5.cloned.1.call-done = bf16[1024,512]{1,0:T(8,128)(2,1)} async-done(((bf16[1024,512]{1,0:T(8,128)(2,1)}), bf16[1024,512]{1,0:T(8,128)(2,1)}) %all-reduce.5.cloned.1.call-update) | async-done | bytes 1048592 | tf_op jit(solution)/shard_map/psum | solution.py:222
  937.0 1.7 fusion.5
  938.7 1.9 fusion.1
  (151 shorter events, 18.9 us)
Async XLA Ops:
  7.2 81.9 %copy-start = (bf16[512,512]{1,0:T(8,128)(2,1)S(1)}, bf16[512,512]{1,0:T(8,128)(2,1)}, u32[]{:S(2)}) copy-start(bf16[512,512]{1,0:T(8,128)(2,1)} %param.10) | copy-start | bytes 1572868
  7.2 19.4 %copy-start.1 = (bf16[1024,512]{1,0:T(8,128)(2,1)S(1)}, bf16[1024,512]{1,0:T(8,128)(2,1)}, u32[]{:S(2)}) copy-start(bf16[1024,512]{1,0:T(8,128)(2,1)} %param.11) | copy-start | bytes 3145732
  7.2 73.1 %all-gather.3.cloned.1.call-start = ((), (), s32[]{:S(2)}) async-start(), calls=%async_computation.4 | async-start | bytes 2228224 | tf_op jit(solution)/shard_map/all_gather | solution.py:165
  11.1 27.7 %copy-start.35 = (s32[384]{0:T(512)}, s32[384]{0:T(512)S(1)}, u32[]{:S(2)}) copy-start(s32[384]{0:T(512)S(1)} %reduce.4) | copy-start | bytes 4612
  14.9 13.9 %all-to-all-start = ((s32[16,1,48]{2,1,0:T(1,128)}), s32[16,1,48]{2,1,0:T(1,128)S(1)}, u32[]{:S(2)}, u32[]{:S(2)}) async-start(s32[16,1,48]{2,1,0:T(1,128)} %all_to_all.12), calls=%async_computation | async-start | bytes 16384 | tf_op jit(solution)/shard_map/all_to_all | solution.py:183
  26.6 6.2 copy-start.45
  27.0 58.6 %copy-start.40 = (s32[384]{0:T(512)}, s32[384]{0:T(512)S(1)}, u32[]{:S(2)}) copy-start(s32[384]{0:T(512)S(1)} %convert_reduce_fusion) | copy-start | bytes 4612
  30.1 2.7 copy-start.31
  32.8 6.0 copy-start.46
  33.9 17.0 %all-to-all-start.1 = ((bf16[16,48,512]{2,1,0:T(8,128)(2,1)}), bf16[16,48,512]{2,1,0:T(8,128)(2,1)S(1)}, u32[]{:S(2)}, u32[]{:S(2)}) async-start(bf16[16,48,512]{2,1,0:T(8,128)(2,1)} %broadcast_select_fusion), calls=%async_computation.1 | async-start | bytes 1572864 | tf_op jit(solution)/shard_map/all_to_all | solution.py:188
  38.8 101.9 %all-gather.5.cloned.1.call-start = ((), (), s32[]{:S(2)}) async-start(), calls=%async_computation.5 | async-start | bytes 1114112 | tf_op jit(solution)/shard_map/all_gather | solution.py:192
  39.5 40.8 %copy-start.37 = (f32[384]{0:T(512)}, f32[384]{0:T(512)S(1)}, u32[]{:S(2)}) copy-start(f32[384]{0:T(512)S(1)} %get-tuple-element.12) | copy-start | bytes 4612
  40.2 40.1 %copy-start.11 = (bf16[384,512]{1,0:T(8,128)(2,1)S(1)}, bf16[384,512]{1,0:T(8,128)(2,1)}, u32[]{:S(2)}) copy-start(bf16[384,512]{1,0:T(8,128)(2,1)} %param.8) | copy-start | bytes 1179652
  40.9 202.7 %reduce-scatter.2.cloned.1.call-start = ((), (), s32[]{:S(2)}) async-start(), calls=%async_computation.7 | async-start | bytes 1114112 | tf_op jit(solution)/shard_map/reduce_scatter | solution.py:215
  84.7 4.4 copy-start.2
  85.0 2.2 copy-start.25
  85.3 1.9 copy-start.27
  85.6 1.6 copy-start.29
  87.2 2.4 copy-start.16
  87.2 2.4 copy-start.18
  87.2 2.4 copy-start.20
  87.2 2.4 copy-start.22
  87.2 1.9 copy-start.12
  88.3 2.2 copy-start.10
  88.3 2.1 copy-start.44
  89.7 56.1 %copy-start.6 = (f32[384,512]{1,0:T(8,128)}, f32[384,512]{1,0:T(8,128)S(1)}, u32[]{:S(2)}) copy-start(f32[384,512]{1,0:T(8,128)S(1)} %get-tuple-element.25) | copy-start | bytes 2359300
  140.7 2.0 copy-start.34
  145.7 2.4 copy-start.39
  148.2 1.6 copy-start.3
  148.2 2.2 copy-start.32
  157.2 7.1 copy-start.42
  159.6 26.6 %all-to-all-start.2 = ((bf16[16,48,512]{2,1,0:T(8,128)(2,1)}), bf16[16,48,512]{2,1,0:T(8,128)(2,1)S(1)}, u32[]{:S(2)}, u32[]{:S(2)}) async-start(bf16[16,48,512]{2,1,0:T(8,128)(2,1)} %bitcast.59), calls=%async_computation.2 | async-start | bytes 1572864 | tf_op jit(solution)/shard_map/all_to_all | solution.py:203
  164.0 560.5 %all-reduce.3.cloned.1.call-start = ((), (), s32[]{:S(2)}) async-start(), calls=%async_computation.6 | async-start | bytes 2097152 | tf_op jit(solution)/shard_map/psum | solution.py:224
  164.3 1.8 copy-start.8
  164.3 1.8 copy-start.23
  164.3 2.8 copy-start.21
  164.3 3.8 copy-start.19
  164.3 4.7 copy-start.17
  166.0 4.0 copy-start.4
  166.1 5.0 copy-start.15
  166.1 5.9 copy-start.14
  166.1 6.9 copy-start.26
  179.8 757.2 %all-reduce.5.cloned.1.call-start = ((), (), s32[]{:S(2)}) async-start(), calls=%async_computation.8 | async-start | bytes 2097152 | tf_op jit(solution)/shard_map/psum | solution.py:222
  247.8 2.9 copy-start.13
  247.8 2.9 copy-start.24
  247.8 2.9 copy-start.36
  247.8 2.9 copy-start.38
  937.0 1.7 copy-start.5
  (7 other events, 7.7 us)
Sparse Core Ops, SparseCore 0:
  11.0 69.2 all-gather.2
  83.8 56.8 all-gather.4
  154.1 89.5 reduce-scatter.1
  249.5 474.9 all-reduce.2
  726.7 210.2 all-reduce.4
where the time goes:
time: 948 us; the launch traced here: 947 us
  waiting for transfers between devices  820 us (86%)
  other arithmetic  45.7 us (5%)
  matrix products  38.5 us (4%)
  starting transfers between devices  17.4 us (2%)
  between operations  14.4 us (2%)
  local copies, waits for them, and re-layouts  11.5 us (1%)
    psum x1, waiting for transfers between devices, shards(): weight_grads = lax.psum(weight_part, ('dp', 'shard')) / loss_scale  472 us
    psum x1, waiting for transfers between devices, shards(): lax.psum(grad_items.astype(jnp.bfloat16), 'dp').astype(jnp.float32)  210 us
    all_gather x1, waiting for transfers between devices, shards(): lax.all_gather(jnp.take(unit_items, negative_rows, axis=0), 'shard', axis...  49.3 us
    reduce_scatter x1, waiting for transfers between devices, shards(): lax.psum_scatter(contract_first(negative_probs, normalized_example_vector...  48.8 us
    all_gather x1, waiting for transfers between devices, project(): lax.all_gather(w_proj, 'shard', axis=1, tiled=True)  26.8 us
  transfers between devices with their start and end apart: 8, of which 7 were waited for; matrix products, arithmetic and copies ran while one was open for 8% of the time, Pallas kernels for 0%

commit v1 on v0

v1 whole, which is shorter than its diff:
```python
import jax
import jax.numpy as jnp
from jax import lax
from jax.sharding import PartitionSpec as P

D = 512
HEADS = 4
DH = 128
MAXLEN = 192
SECTIONS = 4 * HEADS

epsilon = 1e-06
logit_divisor = 0.015625
loss_scale = 512.0

F32 = jnp.float32
BF16 = jnp.bfloat16


def dot(a, b, contract, batch=((), ())):
    return lax.dot_general(a, b, (contract, batch), preferred_element_type=F32)


def silu_slope(values):
    sigmoid = jax.nn.sigmoid(values)
    return sigmoid * (1.0 + values * (1.0 - sigmoid))


def history_mask(lengths_row, rows_count):
    history_ends = jnp.cumsum(lengths_row)
    positions = jnp.arange(rows_count, dtype=jnp.int32)
    history_ids = jnp.sum((positions[:, None] >= history_ends[None, :-1]).astype(jnp.int32), axis=1)
    return (history_ids[:, None] == history_ids[None, :]) & (
        positions[None, :] <= positions[:, None]
    )


def exchange(pieces, axis, groups=None):
    return lax.all_to_all(
        pieces, axis, split_axis=0, concat_axis=0, tiled=True, axis_index_groups=groups
    )


def gather_from(piece, axis, count, groups=None):
    return exchange(jnp.broadcast_to(piece[None], (count,) + piece.shape), axis, groups)


def add_up(received):
    return jnp.sum(received.astype(F32), axis=0)


def shards(tokens, w_proj, w_out, item_rows, lengths, target_owner, target_row, negative_rows):
    tok_rows = tokens.shape[0]
    width = tokens.shape[1]
    item_count = item_rows.shape[0]
    dp = lax.axis_size("dp")
    owners_count = lax.axis_size("shard")
    capacity = 2 * tok_rows // owners_count
    slots = owners_count * capacity
    own_negs = negative_rows.shape[0]
    negs = owners_count * own_negs
    zs = dp // 2
    lo = 4
    hi = zs // lo
    pair = [[2 * z, 2 * z + 1] for z in range(zs)]
    near = [[2 * (lo * h + l) + c for l in range(lo)] for h in range(hi) for c in range(2)]
    far = [[2 * (lo * h + l) + c for h in range(hi)] for l in range(lo) for c in range(2)]

    owners = target_owner
    hits = owners == lax.broadcasted_iota(jnp.int32, (tok_rows, owners_count), 1)
    t_row = lax.broadcasted_iota(jnp.int32, (tok_rows, tok_rows), 0)
    t_col = lax.broadcasted_iota(jnp.int32, (tok_rows, tok_rows), 1)
    before = dot((t_col < t_row).astype(BF16), hits.astype(BF16), ((1,), (0,)))
    slot_index = jnp.sum(jnp.where(hits, before, 0.0), axis=1, keepdims=True).astype(jnp.int32)
    position = owners * capacity + slot_index
    placed = position == lax.broadcasted_iota(jnp.int32, (tok_rows, slots), 1)
    requests = jnp.sum(jnp.where(placed, target_row[:, None], 0), axis=0)
    placed = placed.astype(BF16)
    asked = exchange(requests.reshape(owners_count, capacity), "shard").reshape(slots, 1)

    w_all = gather_from(w_proj, "shard", owners_count)

    rows_wide = item_rows.astype(F32)
    item_scale = lax.rsqrt(jnp.sum(rows_wide * rows_wide, axis=1, keepdims=True) + epsilon)
    unit_items = (rows_wide * item_scale).astype(BF16)
    own_pick = (
        negative_rows[:, None] == lax.broadcasted_iota(jnp.int32, (own_negs, item_count), 1)
    ).astype(BF16)
    decoys = gather_from(
        dot(own_pick, unit_items, ((1,), (0,))).astype(BF16), "shard", owners_count
    ).reshape(negs, width)
    asked_pick = (asked == lax.broadcasted_iota(jnp.int32, (slots, item_count), 1)).astype(BF16)
    served = dot(asked_pick, unit_items, ((1,), (0,))).astype(BF16)
    fetched = exchange(served.reshape(owners_count, capacity, width), "shard").reshape(slots, width)

    visible = history_mask(lengths[0], tok_rows)[None]
    wide_tokens = tokens.astype(F32)
    input_scale = lax.rsqrt(jnp.mean(wide_tokens * wide_tokens, axis=1, keepdims=True) + epsilon)
    normed = (wide_tokens * input_scale).astype(BF16)
    normed_s = jnp.broadcast_to(normed[None], (SECTIONS, tok_rows, width))
    pre_act = dot(normed_s, w_all, ((2,), (1,)), ((0,), (0,)))
    activated = jax.nn.silu(pre_act).astype(BF16)
    gate, values, queries, keys = (activated[i * HEADS : (i + 1) * HEADS] for i in range(4))
    scores = dot(queries, keys, ((2,), (2,)), ((0,), (0,))) * DH ** (-0.5)
    score_sig = jax.nn.sigmoid(scores)
    weights = jnp.where(visible, scores * score_sig * (1.0 / MAXLEN), 0.0).astype(BF16)
    joined = dot(weights, values, ((2,), (1,)), ((0,), (0,))).astype(BF16)
    joined_wide = joined.astype(F32)
    middle_scale = lax.rsqrt(
        jnp.sum(joined_wide * joined_wide, axis=(0, 2), keepdims=True) / width + epsilon
    )
    gate_wide = gate.astype(F32)
    gated = (joined_wide * middle_scale * gate_wide).astype(BF16)
    w_out_h = w_out.reshape(HEADS, DH, width)
    layer_out = wide_tokens + jnp.sum(dot(gated, w_out_h, ((2,), (1,)), ((0,), (0,))), axis=0)

    clicked = dot(placed, fetched, ((1,), (0,)))
    out_scale = lax.rsqrt(jnp.sum(layer_out * layer_out, axis=1, keepdims=True) + epsilon)
    unit_b = (layer_out * out_scale).astype(BF16)
    unit_wide = unit_b.astype(F32)
    target_logit = jnp.sum(unit_wide * clicked, axis=1, keepdims=True) / logit_divisor
    negative_logits = dot(unit_b, decoys, ((1,), (1,))) / logit_divisor
    target_exp = jnp.exp(target_logit)
    negative_exp = jnp.exp(negative_logits)
    totals = target_exp + jnp.sum(negative_exp, axis=1, keepdims=True)
    negative_probs = (negative_exp * (loss_scale / totals)).astype(BF16)
    target_coef = loss_scale * (target_exp / totals - 1.0)
    grad_target = (target_coef * unit_wide).astype(BF16)
    outgoing = dot(placed, grad_target, ((0,), (0,))).astype(BF16)
    grad_negs = dot(negative_probs, unit_b, ((0,), (0,))).astype(BF16)
    grad_unit = target_coef * clicked + dot(negative_probs, decoys, ((1,), (0,)))
    grad_out = out_scale * grad_unit - layer_out * out_scale**3 * jnp.sum(
        layer_out * grad_unit, axis=1, keepdims=True
    )
    grad_out_b = grad_out.astype(BF16)
    weight_part = dot(gated, grad_out_b, ((1,), (0,))).astype(BF16).reshape(width, width)

    halves = jnp.concatenate(
        [
            grad_negs.reshape(owners_count, 2, own_negs // 2, width),
            weight_part.reshape(owners_count, 2, width // owners_count // 2, width),
        ],
        axis=2,
    ).transpose(1, 0, 2, 3)
    of_pair = add_up(exchange(halves, "dp", pair)).astype(BF16)
    back = exchange(
        jnp.concatenate([outgoing.reshape(owners_count, capacity, width), of_pair], axis=1), "shard"
    )
    half_negs = own_negs // 2
    returned = back[:, :capacity].reshape(slots, width)
    neg_and_w = add_up(back[:, capacity:])
    neg_half = neg_and_w[:half_negs].astype(BF16)
    w_part = neg_and_w[half_negs:].astype(BF16)
    core = lax.rem(lax.axis_index("dp"), 2)
    half_rows = lax.dynamic_slice_in_dim(negative_rows, core * half_negs, half_negs)
    half_pick = (
        lax.broadcasted_iota(jnp.int32, (item_count, half_negs), 0) == half_rows[None, :]
    ).astype(BF16)
    dense = dot(asked_pick, returned, ((0,), (0,))) + dot(half_pick, neg_half, ((1,), (0,)))
    part = add_up(exchange(dense.astype(BF16).reshape(2, item_count // 2, width), "dp", pair))

    def with_w(rows, w_rows, count):
        pieces = rows.astype(BF16).reshape(count, -1, width)
        shared = jnp.broadcast_to(w_rows.astype(BF16)[None], (count,) + w_rows.shape)
        got = add_up(exchange(jnp.concatenate([pieces, shared], axis=1), "dp", near if count == lo and rows.shape[0] == item_count // 2 else far))
        own = pieces.shape[1]
        return got[:own], got[own:]

    part, w_part = with_w(part, w_part, lo)
    part, w_part = with_w(part, w_part, hi)
    part = gather_from(part.astype(BF16), "dp", hi, far).reshape(-1, width)
    part = gather_from(part, "dp", lo, near).reshape(-1, width)
    w_half = gather_from(w_part.astype(BF16), "shard", owners_count)
    both = gather_from(
        jnp.concatenate([part, w_half.reshape(-1, width)], axis=0), "dp", 2, pair
    )
    grad_items = both[:, : item_count // 2].reshape(item_count, width).astype(F32)
    w_sum = both[:, item_count // 2 :].reshape(2, owners_count, -1, width)
    weight_grads = w_sum.transpose(1, 0, 2, 3).reshape(width, width).astype(F32) / loss_scale
    item_grads = (
        item_scale * grad_items
        - rows_wide * item_scale**3 * jnp.sum(rows_wide * grad_items, axis=1, keepdims=True)
    ) / loss_scale

    grad_gated = dot(
        jnp.broadcast_to(grad_out_b[None], (HEADS, tok_rows, width)),
        w_out_h,
        ((2,), (2,)),
        ((0,), (0,)),
    )
    grad_gate = grad_gated * joined_wide * middle_scale
    grad_norm = grad_gated * gate_wide
    grad_joined = middle_scale * grad_norm - joined_wide * middle_scale**3 * (
        jnp.sum(joined_wide * grad_norm, axis=(0, 2), keepdims=True) / width
    )
    grad_joined_b = grad_joined.astype(BF16)
    grad_weights = dot(grad_joined_b, values, ((2,), (2,)), ((0,), (0,)))
    grad_values = dot(weights, grad_joined_b, ((1,), (1,)), ((0,), (0,)))
    slope = score_sig * (1.0 + scores * (1.0 - score_sig))
    grad_scores = jnp.where(
        visible, grad_weights * (1.0 / MAXLEN) * slope * DH ** (-0.5), 0.0
    ).astype(BF16)
    grad_queries = dot(grad_scores, keys, ((2,), (1,)), ((0,), (0,)))
    grad_keys = dot(grad_scores, queries, ((1,), (1,)), ((0,), (0,)))
    grad_act = jnp.concatenate([grad_gate, grad_values, grad_queries, grad_keys], axis=0)
    grad_pre = (grad_act * silu_slope(pre_act)).astype(BF16)
    grad_normed = jnp.sum(dot(grad_pre, w_all, ((2,), (2,)), ((0,), (0,))), axis=0)
    grad_input = input_scale * grad_normed - wide_tokens * input_scale**3 * jnp.mean(
        wide_tokens * grad_normed, axis=1, keepdims=True
    )
    grad_tokens = (grad_out + grad_input).astype(BF16)
    return (grad_tokens, weight_grads, item_grads)


def solution(mesh):
    in_specs = (
        P(("dp", "shard"), None),
        P(None, "shard"),
        P(),
        P("shard", None),
        P(("dp", "shard"), None),
        P(("dp", "shard"), None),
        P(("dp", "shard")),
        P("shard"),
    )
    out_specs = (P(("dp", "shard"), None), P(), P("shard", None))
    return jax.shard_map(shards, mesh=mesh, in_specs=in_specs, out_specs=out_specs, check_vma=False)
```

time: 948 us -> 264 us (0.28)
  waiting for transfers between devices: 820 us -> 83.1 us
  blocking collectives: 0 us -> 48.4 us
  starting transfers between devices: 17.4 us -> 55.6 us
  other arithmetic: 45.7 us -> 22 us
  between operations: 14.4 us -> 1.19 us
    psum x2 -> x0, waiting for transfers between devices: 682 us -> none  [the longest x1 472 us: shards(): weight_grads = lax.psum(weight_part, ('dp', 'shard')) / loss_scale]
    all_gather x2 -> x0, waiting for transfers between devices: 76.2 us -> none  [the longest x1 49.3 us: shards(): lax.all_gather(jnp.take(unit_items, negative_rows, axis=0), 'shard', axis...]
    all_to_all x3 -> x9, waiting for transfers between devices: 11.5 us -> 83.1 us  [exchange(): lax.all_to_all(pieces, axis, split_axis=0, concat_axis=0, tiled=True, axi...]
    reduce_scatter x1 -> x0, waiting for transfers between devices: 48.8 us -> none  [shards(): lax.psum_scatter(contract_first(negative_probs, normalized_example_vector...]
    all_to_all x0 -> x4, blocking collectives: none -> 48.4 us  [exchange(): lax.all_to_all(pieces, axis, split_axis=0, concat_axis=0, tiled=True, axi...]
    all_to_all x3 -> x9, starting transfers between devices: 16.8 us -> 55.6 us  [exchange(): lax.all_to_all(pieces, axis, split_axis=0, concat_axis=0, tiled=True, axi...]
    scatter-add x2 -> x0, other arithmetic: 12.8 us -> none  [the longest x1 8.62 us: shards(): grad_items = jnp.zeros((item_rows.shape[0], model_width), jnp.float32).at...]
    dot_general x32 -> x21, matrix products: 38.5 us -> 39.4 us  [dot(): return lax.dot_general(a, b, (contract, batch), preferred_element_type=F32)]
  transfers between devices with their start and end apart: 8 -> 9, of which waited for: 7 -> 9; matrix products, arithmetic and copies ran while one was open for 8% -> 15% of each run, Pallas kernels for 0% -> 0%
where the time goes in v1:
time: 264 us; the launch traced here: 263 us
  waiting for transfers between devices  83.1 us (31%)
  starting transfers between devices  55.6 us (21%)
  blocking collectives  48.4 us (18%)
  matrix products  39.4 us (15%)
  other arithmetic  22 us (8%)
  local copies, waits for them, and re-layouts  13 us (5%)
    all_to_all x9, waiting for transfers between devices, exchange(): lax.all_to_all(pieces, axis, split_axis=0, concat_axis=0, tiled=True, axi...  83.1 us
    all_to_all x9, starting transfers between devices, exchange(): lax.all_to_all(pieces, axis, split_axis=0, concat_axis=0, tiled=True, axi...  55.6 us
    all_to_all x4, blocking collectives, exchange(): lax.all_to_all(pieces, axis, split_axis=0, concat_axis=0, tiled=True, axi...  48.4 us
    dot_general x21, matrix products, dot(): return lax.dot_general(a, b, (contract, batch), preferred_element_type=F32)  39.4 us
    broadcast_in_dim x6, local copies, waits for them, and re-layouts, gather_from(): jnp.broadcast_to(piece[None], (count,) + piece.shape)  6.64 us
  transfers between devices with their start and end apart: 9, of which 9 were waited for; matrix products, arithmetic and copies ran while one was open for 15% of the time, Pallas kernels for 0%

profile of v1, /device:TPU:1, one launch (start us, length us, event | category | flops | bytes accessed | tf_op | source)
XLA Modules:
  0.0 262.7 jit_solution(5197701088065852757)
XLA Ops:
  3.9 7.6 %all-to-all-start.1 = ((s32[16,1,48]{2,1,0:T(1,128)}), s32[16,1,48]{2,1,0:T(1,128)S(1)}, u32[]{:S(2)}, u32[]{:S(2)}) async-start(s32[16,1,48]{2,1,0:T(1,128)} %all_to_all.43), calls=%async_computation.1 | async-start | bytes 16384 | tf_op jit(solution)/shard_map/all_to_all | solution.py:39
  13.3 4.5 %all-to-all-done.1 = s32[16,1,48]{2,1,0:T(1,128)S(1)} async-done(((s32[16,1,48]{2,1,0:T(1,128)}), s32[16,1,48]{2,1,0:T(1,128)S(1)}, u32[]{:S(2)}, u32[]{:S(2)}) %all-to-all-start.1) | async-done | bytes 3104 | tf_op jit(solution)/shard_map/all_to_all | solution.py:39
  17.8 1.5 broadcast_in_dim.56
  19.3 4.6 %all-to-all-start = ((bf16[16,512,128]{1,2,0:T(8,128)(2,1)}), bf16[16,512,128]{1,2,0:T(8,128)(2,1)}, u32[]{:S(2)}, u32[]{:S(2)}) async-start(bf16[16,512,128]{1,2,0:T(8,128)(2,1)} %broadcast_in_dim.56), calls=%async_computation | async-start | bytes 4194304 | tf_op jit(solution)/shard_map/all_to_all | solution.py:39
  27.6 2.0 fusion.15
  29.6 19.2 %all-to-all-done = bf16[16,512,128]{1,2,0:T(8,128)(2,1)} async-done(((bf16[16,512,128]{1,2,0:T(8,128)(2,1)}), bf16[16,512,128]{1,2,0:T(8,128)(2,1)}, u32[]{:S(2)}, u32[]{:S(2)}) %all-to-all-start) | async-done | bytes 2097184 | tf_op jit(solution)/shard_map/all_to_all | solution.py:39
  48.8 7.7 %all-to-all-start.2 = ((bf16[16,48,512]{2,1,0:T(8,128)(2,1)}), bf16[16,48,512]{2,1,0:T(8,128)(2,1)S(1)}, u32[]{:S(2)}, u32[]{:S(2)}) async-start(bf16[16,48,512]{2,1,0:T(8,128)(2,1)} %bitcast.4), calls=%async_computation.2 | async-start | bytes 1572864 | tf_op jit(solution)/shard_map/all_to_all | solution.py:39
  56.4 5.2 %multiply_convert_fusion = (bf16[16,384,128]{1,2,0:T(8,128)(2,1)S(1)}, f32[16,384,128]{1,2,0:T(8,128)}) fusion(bf16[16,512,128]{1,2,0:T(8,128)(2,1)} %all-to-all-done, bf16[384,512]{1,0:T(8,128)(2,1)S(1)} %fusion.25), kind=kOutput, calls=%fused_computation.9 | convolution fusion | flops 809238528 | bytes 7208960 | tf_op jit(solution)/shard_map/dot_general | solution.py:21
  61.7 2.6 select_convert_fusion.1
  65.2 1.3 fusion.31
  66.5 2.0 all-to-all-done.2
  68.5 1.1 broadcast_in_dim.61
  69.6 4.7 %all-to-all-start.3 = ((bf16[16,64,512]{2,1,0:T(8,128)(2,1)}), bf16[16,64,512]{2,1,0:T(8,128)(2,1)S(1)}, u32[]{:S(2)}, u32[]{:S(2)}) async-start(bf16[16,64,512]{2,1,0:T(8,128)(2,1)} %broadcast_in_dim.61), calls=%async_computation.3 | async-start | bytes 2097152 | tf_op jit(solution)/shard_map/all_to_all | solution.py:39
  74.4 1.8 multiply_reduce_fusion.1
  76.2 1.5 fusion.22
  77.7 10.9 %all-to-all-done.3 = bf16[16,64,512]{2,1,0:T(8,128)(2,1)S(1)} async-done(((bf16[16,64,512]{2,1,0:T(8,128)(2,1)}), bf16[16,64,512]{2,1,0:T(8,128)(2,1)S(1)}, u32[]{:S(2)}, u32[]{:S(2)}) %all-to-all-start.3) | async-done | bytes 1048608 | tf_op jit(solution)/shard_map/all_to_all | solution.py:39
  88.6 1.8 fusion.66
  90.4 1.7 convolution_convert_fusion.1
  94.9 1.6 convolution_convert_fusion.2
  96.7 9.7 %all_to_all.69 = bf16[2,16,48,512]{3,2,1,0:T(8,128)(2,1)} all-to-all(bf16[2,16,48,512]{3,2,1,0:T(8,128)(2,1)S(1)} %copy_bitcast_fusion), channel_id=1, replica_groups={{0,16},{32,48},{64,80},{96,112},{128,144},{160,176},{192,208},{224,240}..., dimensions={0} | all-to-all | bytes 3145728 | tf_op jit(solution)/shard_map/all_to_all | solution.py:39
  106.4 1.8 reduce_sum.188
  108.1 2.4 pad_maximum_fusion.1
  110.6 4.6 %all-to-all-start.5 = ((bf16[16,96,512]{2,1,0:T(8,128)(2,1)}), bf16[16,96,512]{2,1,0:T(8,128)(2,1)}, u32[]{:S(2)}, u32[]{:S(2)}) async-start(bf16[16,96,512]{2,1,0:T(8,128)(2,1)} %pad_maximum_fusion.1), calls=%async_computation.5 | async-start | bytes 3145728 | tf_op jit(solution)/shard_map/all_to_all | solution.py:39
  115.3 24.8 %all-to-all-done.5 = bf16[16,96,512]{2,1,0:T(8,128)(2,1)} async-done(((bf16[16,96,512]{2,1,0:T(8,128)(2,1)}), bf16[16,96,512]{2,1,0:T(8,128)(2,1)}, u32[]{:S(2)}, u32[]{:S(2)}) %all-to-all-start.5) | async-done | bytes 1572896 | tf_op jit(solution)/shard_map/all_to_all | solution.py:39
  140.0 1.5 fusion.65
  142.0 1.2 add_convert_fusion
  143.2 5.4 %all_to_all.70 = bf16[2,512,512]{2,1,0:T(8,128)(2,1)S(1)} all-to-all(bf16[2,512,512]{2,1,0:T(8,128)(2,1)S(1)} %bitcast.62), channel_id=1, replica_groups={{0,16},{32,48},{64,80},{96,112},{128,144},{160,176},{192,208},{224,240}..., dimensions={0} | all-to-all | bytes 2097152 | tf_op jit(solution)/shard_map/all_to_all | solution.py:39
  150.9 21.8 %all_to_all.71 = bf16[4,144,512]{2,1,0:T(8,128)(2,1)S(1)} all-to-all(bf16[4,144,512]{2,1,0:T(8,128)(2,1)S(1)} %pad_maximum_fusion.3), channel_id=1, replica_groups={{0,32,64,96},{16,48,80,112},{128,160,192,224},{144,176,208,240},{256,28..., dimensions={0} | all-to-all | bytes 1179648 | tf_op jit(solution)/shard_map/all_to_all | solution.py:39
  173.5 12.1 %all-to-all-start.8 = ((bf16[4,48,512]{2,1,0:T(8,128)(2,1)}), bf16[4,48,512]{2,1,0:T(8,128)(2,1)S(1)}, u32[]{:S(2)}, u32[]{:S(2)}) async-start(bf16[4,48,512]{2,1,0:T(8,128)(2,1)} %pad_maximum_fusion.4), calls=%async_computation.8 | async-start | bytes 393216 | tf_op jit(solution)/shard_map/all_to_all | solution.py:39
  185.6 1.7 fusion.36
  187.4 2.3 fusion.32
  189.6 8.4 %all-to-all-done.8 = bf16[4,48,512]{2,1,0:T(8,128)(2,1)S(1)} async-done(((bf16[4,48,512]{2,1,0:T(8,128)(2,1)}), bf16[4,48,512]{2,1,0:T(8,128)(2,1)S(1)}, u32[]{:S(2)}, u32[]{:S(2)}) %all-to-all-start.8) | async-done | bytes 196640 | tf_op jit(solution)/shard_map/all_to_all | solution.py:39
  198.8 4.2 %all-to-all-start.11 = ((bf16[16,16,512]{2,1,0:T(8,128)(2,1)}), bf16[16,16,512]{2,1,0:T(8,128)(2,1)}, u32[]{:S(2)}, u32[]{:S(2)}) async-start(bf16[16,16,512]{2,1,0:T(8,128)(2,1)} %broadcast_in_dim.68), calls=%async_computation.11 | async-start | bytes 524288 | tf_op jit(solution)/shard_map/all_to_all | solution.py:39
  203.0 3.4 %select_convert_fusion = bf16[4,384,384]{2,1,0:T(8,128)(2,1)S(1)} fusion(f32[4,384,384]{2,1,0:T(8,128)} %get-tuple-element.22, bf16[4,384,128]{1,2,0:T(8,128)(2,1)} %get-tuple-element.8, pred[384,384]{1,0:T(8,128)(4,1)} %copy-done.19, bf16[16,384,128]{1,2,0:T(8,128)(2,1)} %copy-done.11), kind=kOutput, calls=%fused_computation.14 | convolution fusion | flops 158662656 | bytes 4472832 | tf_op jit(solution)/shard_map/dot_general | solution.py:21
  207.0 3.5 %all-to-all-done.11 = bf16[16,16,512]{2,1,0:T(8,128)(2,1)} async-done(((bf16[16,16,512]{2,1,0:T(8,128)(2,1)}), bf16[16,16,512]{2,1,0:T(8,128)(2,1)}, u32[]{:S(2)}, u32[]{:S(2)}) %all-to-all-start.11) | async-done | bytes 262176 | tf_op jit(solution)/shard_map/all_to_all | solution.py:39
  210.6 1.4 broadcast_in_dim.65
  212.0 6.1 %all-to-all-start.9 = ((bf16[4,32,512]{2,1,0:T(8,128)(2,1)}), bf16[4,32,512]{2,1,0:T(8,128)(2,1)}, u32[]{:S(2)}, u32[]{:S(2)}) async-start(bf16[4,32,512]{2,1,0:T(8,128)(2,1)} %broadcast_in_dim.65), calls=%async_computation.9 | async-start | bytes 262144 | tf_op jit(solution)/shard_map/all_to_all | solution.py:39
  218.1 2.7 %fusion.67 = f32[4,384,128]{1,2,0:T(8,128)} fusion(bf16[4,384,128]{1,2,0:T(8,128)(2,1)} %get-tuple-element.8, bf16[4,384,384]{2,1,0:T(8,128)(2,1)} %copy-done.10), kind=kOutput, calls=%fused_computation.132 | convolution fusion | flops 150994944 | bytes 2359296 | tf_op jit(solution)/shard_map/dot_general | solution.py:21
  220.8 2.3 fusion.46
  223.1 7.9 %all-to-all-done.9 = bf16[4,32,512]{2,1,0:T(8,128)(2,1)} async-done(((bf16[4,32,512]{2,1,0:T(8,128)(2,1)}), bf16[4,32,512]{2,1,0:T(8,128)(2,1)}, u32[]{:S(2)}, u32[]{:S(2)}) %all-to-all-start.9) | async-done | bytes 131104 | tf_op jit(solution)/shard_map/all_to_all | solution.py:39
  230.9 1.7 broadcast_in_dim.67
  232.7 4.1 %all-to-all-start.10 = ((bf16[4,128,512]{2,1,0:T(8,128)(2,1)}), bf16[4,128,512]{2,1,0:T(8,128)(2,1)}, u32[]{:S(2)}, u32[]{:S(2)}) async-start(bf16[4,128,512]{2,1,0:T(8,128)(2,1)} %broadcast_in_dim.67), calls=%async_computation.10 | async-start | bytes 1048576 | tf_op jit(solution)/shard_map/all_to_all | solution.py:39
  236.9 1.6 fusion.52
  238.6 4.5 %fusion.30 = (f32[384]{0:T(512)S(1)}, f32[384,512]{1,0:T(8,128)S(1)}) fusion(bf16[384,512]{1,0:T(8,128)(2,1)S(1)} %copy-done.6, bf16[16,512,128]{1,2,0:T(8,128)(2,1)} %all-to-all-done, f32[4,384,128]{1,2,0:T(8,128)} %fusion.46, f32[4,384,128]{1,2,0:T(8,128)S(1)} %fusion.52, f32[4,384,128]{1,2,0:T(8,128)S(1)} %copy-done.13, ...), kind=kOutput, calls=%fused_computation.70 | convolution fusion | flops 815332992 | bytes 9569792 | tf_op jit(solution)/shard_map/dot_general | solution.py:21
  244.2 1.9 all-to-all-done.10
  246.1 1.2 pad_maximum_fusion.2
  247.4 11.5 %all_to_all.72 = bf16[2,768,512]{2,1,0:T(8,128)(2,1)S(1)} all-to-all(bf16[2,768,512]{2,1,0:T(8,128)(2,1)S(1)} %broadcast_in_dim.69), channel_id=1, replica_groups={{0,16},{32,48},{64,80},{96,112},{128,144},{160,176},{192,208},{224,240}..., dimensions={0} | all-to-all | bytes 3145728 | tf_op jit(solution)/shard_map/all_to_all | solution.py:39
  260.8 1.9 fusion.6
  (100 shorter events, 20.7 us)
Async XLA Ops:
  0.6 73.7 %copy-start = (bf16[512,512]{1,0:T(8,128)(2,1)S(1)}, bf16[512,512]{1,0:T(8,128)(2,1)}, u32[]{:S(2)}) copy-start(bf16[512,512]{1,0:T(8,128)(2,1)} %param.10) | copy-start | bytes 1572868
  3.9 13.9 %all-to-all-start.1 = ((s32[16,1,48]{2,1,0:T(1,128)}), s32[16,1,48]{2,1,0:T(1,128)S(1)}, u32[]{:S(2)}, u32[]{:S(2)}) async-start(s32[16,1,48]{2,1,0:T(1,128)} %all_to_all.43), calls=%async_computation.1 | async-start | bytes 16384 | tf_op jit(solution)/shard_map/all_to_all | solution.py:39
  19.3 4.7 %copy-start.5 = (bf16[384,512]{1,0:T(8,128)(2,1)S(1)}, bf16[384,512]{1,0:T(8,128)(2,1)}, u32[]{:S(2)}) copy-start(bf16[384,512]{1,0:T(8,128)(2,1)} %param.8) | copy-start | bytes 1179652
  19.3 4.9 %copy-start.1 = (bf16[1024,512]{1,0:T(8,128)(2,1)S(1)}, bf16[1024,512]{1,0:T(8,128)(2,1)}, u32[]{:S(2)}) copy-start(bf16[1024,512]{1,0:T(8,128)(2,1)} %param.11) | copy-start | bytes 3145732
  19.3 29.4 %all-to-all-start = ((bf16[16,512,128]{1,2,0:T(8,128)(2,1)}), bf16[16,512,128]{1,2,0:T(8,128)(2,1)}, u32[]{:S(2)}, u32[]{:S(2)}) async-start(bf16[16,512,128]{1,2,0:T(8,128)(2,1)} %broadcast_in_dim.56), calls=%async_computation | async-start | bytes 4194304 | tf_op jit(solution)/shard_map/all_to_all | solution.py:39
  23.9 2.0 copy-start.24
  25.6 3.9 %copy-start.21 = (f32[1024]{0:T(1024)}, f32[1024]{0:T(1024)S(1)}, u32[]{:S(2)}) copy-start(f32[1024]{0:T(1024)S(1)} %get-tuple-element.10) | copy-start | bytes 12292
  25.8 35.9 %copy-start.19 = (pred[384,384]{1,0:T(8,128)(4,1)}, pred[384,384]{1,0:T(8,128)(4,1)S(1)}, u32[]{:S(2)}) copy-start(pred[384,384]{1,0:T(8,128)(4,1)S(1)} %fusion.41) | copy-start | bytes 442372
  48.8 19.7 %all-to-all-start.2 = ((bf16[16,48,512]{2,1,0:T(8,128)(2,1)}), bf16[16,48,512]{2,1,0:T(8,128)(2,1)S(1)}, u32[]{:S(2)}, u32[]{:S(2)}) async-start(bf16[16,48,512]{2,1,0:T(8,128)(2,1)} %bitcast.4), calls=%async_computation.2 | async-start | bytes 1572864 | tf_op jit(solution)/shard_map/all_to_all | solution.py:39
  61.7 2.6 copy-start.11
  64.2 1.0 copy-start.10
  68.5 5.9 %copy-start.7 = (bf16[16,48,512]{2,1,0:T(8,128)(2,1)}, bf16[16,48,512]{2,1,0:T(8,128)(2,1)S(1)}, u32[]{:S(2)}) copy-start(bf16[16,48,512]{2,1,0:T(8,128)(2,1)S(1)} %all-to-all-done.2) | copy-start | bytes 2359300
  69.6 19.0 %all-to-all-start.3 = ((bf16[16,64,512]{2,1,0:T(8,128)(2,1)}), bf16[16,64,512]{2,1,0:T(8,128)(2,1)S(1)}, u32[]{:S(2)}, u32[]{:S(2)}) async-start(bf16[16,64,512]{2,1,0:T(8,128)(2,1)} %broadcast_in_dim.61), calls=%async_computation.3 | async-start | bytes 2097152 | tf_op jit(solution)/shard_map/all_to_all | solution.py:39
  74.3 1.8 copy-start.8
  88.6 1.8 copy-start.4
  90.4 2.6 copy-start.9
  93.0 1.9 copy-start.14
  93.8 0.9 copy-start.2
  94.9 1.6 copy-start.16
  110.6 29.4 %all-to-all-start.5 = ((bf16[16,96,512]{2,1,0:T(8,128)(2,1)}), bf16[16,96,512]{2,1,0:T(8,128)(2,1)}, u32[]{:S(2)}, u32[]{:S(2)}) async-start(bf16[16,96,512]{2,1,0:T(8,128)(2,1)} %pad_maximum_fusion.1), calls=%async_computation.5 | async-start | bytes 3145728 | tf_op jit(solution)/shard_map/all_to_all | solution.py:39
  149.8 35.9 %copy-start.15 = (bf16[4,384,128]{1,2,0:T(8,128)(2,1)S(1)}, bf16[4,384,128]{1,2,0:T(8,128)(2,1)}, u32[]{:S(2)}) copy-start(bf16[4,384,128]{1,2,0:T(8,128)(2,1)} %get-tuple-element.24) | copy-start | bytes 1179652
  173.5 24.5 %all-to-all-start.8 = ((bf16[4,48,512]{2,1,0:T(8,128)(2,1)}), bf16[4,48,512]{2,1,0:T(8,128)(2,1)S(1)}, u32[]{:S(2)}, u32[]{:S(2)}) async-start(bf16[4,48,512]{2,1,0:T(8,128)(2,1)} %pad_maximum_fusion.4), calls=%async_computation.8 | async-start | bytes 393216 | tf_op jit(solution)/shard_map/all_to_all | solution.py:39
  198.1 4.9 %copy-start.17 = (bf16[48,512]{1,0:T(8,128)(2,1)}, bf16[48,512]{1,0:T(8,128)(2,1)S(1)}, u32[]{:S(2)}) copy-start(bf16[48,512]{1,0:T(8,128)(2,1)S(1)} %reduce.4) | copy-start | bytes 147460
  198.8 11.7 %all-to-all-start.11 = ((bf16[16,16,512]{2,1,0:T(8,128)(2,1)}), bf16[16,16,512]{2,1,0:T(8,128)(2,1)}, u32[]{:S(2)}, u32[]{:S(2)}) async-start(bf16[16,16,512]{2,1,0:T(8,128)(2,1)} %broadcast_in_dim.68), calls=%async_computation.11 | async-start | bytes 524288 | tf_op jit(solution)/shard_map/all_to_all | solution.py:39
  203.0 3.4 %copy-start.18 = (bf16[48,512]{1,0:T(8,128)(2,1)S(1)}, bf16[48,512]{1,0:T(8,128)(2,1)}, u32[]{:S(2)}) copy-start(bf16[48,512]{1,0:T(8,128)(2,1)} %copy-done.17) | copy-start | bytes 147460
  212.0 19.0 %all-to-all-start.9 = ((bf16[4,32,512]{2,1,0:T(8,128)(2,1)}), bf16[4,32,512]{2,1,0:T(8,128)(2,1)}, u32[]{:S(2)}, u32[]{:S(2)}) async-start(bf16[4,32,512]{2,1,0:T(8,128)(2,1)} %broadcast_in_dim.65), calls=%async_computation.9 | async-start | bytes 262144 | tf_op jit(solution)/shard_map/all_to_all | solution.py:39
  232.7 13.4 %all-to-all-start.10 = ((bf16[4,128,512]{2,1,0:T(8,128)(2,1)}), bf16[4,128,512]{2,1,0:T(8,128)(2,1)}, u32[]{:S(2)}, u32[]{:S(2)}) async-start(bf16[4,128,512]{2,1,0:T(8,128)(2,1)} %broadcast_in_dim.67), calls=%async_computation.10 | async-start | bytes 1048576 | tf_op jit(solution)/shard_map/all_to_all | solution.py:39
  236.8 1.7 copy-start.6
  236.8 1.7 copy-start.12
  236.9 1.7 copy-start.13
  238.5 4.5 %copy-start.3 = (f32[384,512]{1,0:T(8,128)S(1)}, f32[384,512]{1,0:T(8,128)}, u32[]{:S(2)}) copy-start(f32[384,512]{1,0:T(8,128)} %copy-done.2) | copy-start | bytes 2359300
  238.5 4.5 %copy-start.23 = (f32[384]{0:T(512)S(1)}, f32[384]{0:T(512)}, u32[]{:S(2)}) copy-start(f32[384]{0:T(512)} %get-tuple-element.13) | copy-start | bytes 4612
  260.1 0.7 copy-start.20
  260.1 0.7 copy-start.22

commit v2 on v1

v2 whole, which is shorter than its diff:
```python
import functools

import jax
import jax.numpy as jnp
from jax import lax
from jax.experimental import pallas as pl
from jax.experimental.pallas import tpu as pltpu
from jax.sharding import PartitionSpec as P

D = 512
HEADS = 4
DH = 128
MAXLEN = 192
SECTIONS = 4 * HEADS
PLANE = 16
CAP = 48
NEG = 64
WROWS = 32
CHIPS = 16
HALF = 512
PIECE = 32
LANES = 128

epsilon = 1e-06
logit_scale = 64.0
loss_scale = 512.0

F32 = jnp.float32
BF16 = jnp.bfloat16
I32 = jnp.int32


def dot(a, b, contract, batch=((), ())):
    return lax.dot_general(a, b, (contract, batch), preferred_element_type=F32)


def iota(shape, axis):
    return lax.broadcasted_iota(I32, shape, axis)


def one_hot(mask):
    return jnp.where(mask, 1.0, 0.0).astype(BF16)


def silu_slope(values):
    sigmoid = jax.nn.sigmoid(values)
    return sigmoid * (1.0 + values * (1.0 - sigmoid))


def history_mask(lengths_row, rows_count):
    history_ends = jnp.cumsum(lengths_row)
    positions = jnp.arange(rows_count, dtype=jnp.int32)
    history_ids = jnp.sum((positions[:, None] >= history_ends[None, :-1]).astype(jnp.int32), axis=1)
    return (history_ids[:, None] == history_ids[None, :]) & (
        positions[None, :] <= positions[:, None]
    )


def exchange(pieces, axis, groups=None):
    return lax.all_to_all(
        pieces, axis, split_axis=0, concat_axis=0, tiled=True, axis_index_groups=groups
    )


def route_kernel(core_ref, owner_ref, row_ref, w_ref, out_ref, pos_ref):
    tok = owner_ref.shape[0]
    owners = owner_ref[...]
    hits = owners == iota((tok, LANES), 1)
    earlier = one_hot(iota((tok, tok), 1) < iota((tok, tok), 0))
    before = dot(earlier, one_hot(hits), ((1,), (0,)))
    slot = jnp.sum(jnp.where(hits, before, 0.0), axis=1, keepdims=True).astype(I32)
    pos_ref[...] = owners * CAP + slot
    spread = one_hot(owners * LANES + slot == iota((tok, PLANE * LANES), 1))
    asked = jnp.broadcast_to(row_ref[...], (16, tok))
    which = iota((16, tok), 0)
    digits = jnp.where(which == 0, asked >> 5, jnp.where(which == 1, asked & 31, 0))
    requests = dot(digits.astype(F32).astype(BF16), spread, ((1,), (0,))).astype(BF16)
    rows = w_ref.shape[0] // 2
    own = w_ref[pl.ds(pl.multiple_of(core_ref[0] * rows, rows), rows), :]
    for j in range(PLANE):
        out_ref[j, 0:rows, :] = own
        out_ref[j, rows : rows + 16, :] = requests[:, j * LANES : (j + 1) * LANES]


def serve_kernel(recv_ref, items_ref, negs_ref, out_ref, pick_ref):
    rows = recv_ref.shape[1] - 16
    count = items_ref.shape[0]
    diagonal = iota((CAP, LANES), 0) == iota((CAP, LANES), 1)
    for j in range(PLANE):
        digits = recv_ref[j, rows : rows + 16, :].astype(F32)
        asked = 32.0 * digits[0:1] + digits[1:2]
        column = jnp.sum(
            jnp.where(diagonal, jnp.broadcast_to(asked, (CAP, LANES)), 0.0), axis=1, keepdims=True
        ).astype(I32)
        pick_ref[j * CAP : (j + 1) * CAP, :] = one_hot(column == iota((CAP, count), 1))
    negs = negs_ref[...]
    step = 4
    for j in range(0, PLANE, step):
        served = dot(pick_ref[j * CAP : (j + step) * CAP, :], items_ref[...], ((1,), (0,)))
        served = served.astype(BF16)
        for i in range(step):
            out_ref[j + i, 0:CAP, :] = served[i * CAP : (i + 1) * CAP]
            out_ref[j + i, CAP : CAP + NEG, :] = negs


def loss_kernel(
    layer_ref,
    gated_ref,
    recv_ref,
    pos_ref,
    out_ref,
    grad_ref,
    grad_b_ref,
    fetched,
    decoys,
    probs,
    unit,
    back,
):
    tok = layer_ref.shape[0]
    for j in range(PLANE):
        fetched[j * CAP : (j + 1) * CAP, :] = recv_ref[j, 0:CAP, :]
        decoys[j * NEG : (j + 1) * NEG, :] = recv_ref[j, CAP : CAP + NEG, :]
    step = 128
    for c in range(0, tok, step):
        layer_out = layer_ref[c : c + step, :]
        placed = one_hot(pos_ref[c : c + step, :] == iota((step, PLANE * CAP), 1))
        clicked = dot(placed, fetched[...], ((1,), (0,)))
        out_scale = lax.rsqrt(jnp.sum(layer_out * layer_out, axis=1, keepdims=True) + epsilon)
        unit_b = (layer_out * out_scale).astype(BF16)
        unit[c : c + step, :] = unit_b
        unit_wide = unit_b.astype(F32)
        target_exp = jnp.exp(jnp.sum(unit_wide * clicked, axis=1, keepdims=True) * logit_scale)
        negative_exp = jnp.exp(dot(unit_b, decoys[...], ((1,), (1,))) * logit_scale)
        totals = target_exp + jnp.sum(negative_exp, axis=1, keepdims=True)
        negative_probs = (negative_exp * (loss_scale / totals)).astype(BF16)
        probs[c : c + step, :] = negative_probs
        target_coef = loss_scale * (target_exp / totals - 1.0)
        back[c : c + step, :] = (target_coef * unit_wide).astype(BF16)
        grad_unit = target_coef * clicked + dot(negative_probs, decoys[...], ((1,), (0,)))
        along = jnp.sum(layer_out * grad_unit, axis=1, keepdims=True)
        grad_out = out_scale * grad_unit - layer_out * (out_scale**3 * along)
        grad_ref[c : c + step, :] = grad_out
        grad_b_ref[c : c + step, :] = grad_out.astype(BF16)
    across = jnp.broadcast_to(pos_ref[...].astype(F32), (tok, LANES)).T[0:1, :].astype(I32)
    group = 4
    for j in range(0, PLANE, group):
        slots = group * CAP
        placed_t = one_hot(iota((slots, tok), 0) + j * CAP == across)
        sent = dot(placed_t, back[...], ((1,), (0,))).astype(BF16)
        negs = dot(probs[:, j * NEG : (j + group) * NEG], unit[...], ((0,), (0,))).astype(BF16)
        weights = dot(gated_ref[j // group], grad_b_ref[...], ((0,), (0,))).astype(BF16)
        for i in range(group):
            out_ref[j + i, 0:CAP, :] = sent[i * CAP : (i + 1) * CAP]
            out_ref[j + i, CAP : CAP + NEG, :] = negs[i * NEG : (i + 1) * NEG]
            out_ref[j + i, CAP + NEG :, :] = weights[i * WROWS : (i + 1) * WROWS]


def collect_kernel(core_ref, recv_ref, pick_ref, neg_row_ref, keep_ref, send_ref, returned):
    core = core_ref[0]
    negs = jnp.zeros((NEG, D), F32)
    weights = jnp.zeros((WROWS, D), F32)
    for j in range(PLANE):
        returned[j * CAP : (j + 1) * CAP, :] = recv_ref[j, 0:CAP, :]
        negs = negs + recv_ref[j, CAP : CAP + NEG, :].astype(F32)
        weights = weights + recv_ref[j, CAP + NEG :, :].astype(F32)
    negs = negs.astype(BF16)
    step = 256
    for ref, half in ((keep_ref, core), (send_ref, 1 - core)):
        for b in range(0, HALF, step):
            first = pl.multiple_of(half * HALF + b, step)
            here = one_hot(iota((step, NEG), 0) + first == neg_row_ref[...])
            total = dot(pick_ref[:, pl.ds(first, step)], returned[...], ((0,), (0,)))
            total = total + dot(here, negs, ((1,), (0,)))
            ref[b : b + step, :] = total.astype(BF16)
        part = jnp.where(half == 0, weights[0 : WROWS // 2], weights[WROWS // 2 :])
        ref[HALF:, :] = part.astype(BF16)


def pack_kernel(keep_ref, other_ref, out_ref):
    for i in range(CHIPS):
        rows = slice(i * PIECE, (i + 1) * PIECE)
        total = keep_ref[rows, :].astype(F32) + other_ref[rows, :].astype(F32)
        total = total.astype(BF16)
        for q in range(D // LANES):
            out_ref[i, q * PIECE : (q + 1) * PIECE, :] = total[:, q * LANES : (q + 1) * LANES]
    weights = keep_ref[HALF:, :].astype(F32) + other_ref[HALF:, :].astype(F32)
    for i in range(CHIPS):
        row = weights[i : i + 1, :]
        parts = [row[:, q * LANES : (q + 1) * LANES] for q in range(D // LANES)]
        parts.append(jnp.zeros((8 - D // LANES, LANES), F32))
        out_ref[i, D // LANES * PIECE :, :] = jnp.concatenate(parts, axis=0).astype(BF16)


def total_kernel(recv_ref, out_ref):
    total = recv_ref[0].astype(F32)
    for i in range(1, CHIPS):
        total = total + recv_ref[i].astype(F32)
    total = total.astype(BF16)
    for i in range(CHIPS):
        out_ref[i] = total


def weight_kernel(core_ref, mine_ref, other_ref, out_ref):
    first = core_ref[0] == 0
    rows = []
    for half in range(2):
        for i in range(CHIPS):
            mine = mine_ref[i, D // LANES * PIECE :, :].astype(F32)
            other = other_ref[i, D // LANES * PIECE :, :].astype(F32)
            block = jnp.where(first, mine, other) if half == 0 else jnp.where(first, other, mine)
            rows.append(
                jnp.concatenate([block[q : q + 1, :] for q in range(D // LANES)], axis=1)
            )
    gathered = jnp.concatenate(rows, axis=0).astype(BF16)
    for j in range(PLANE):
        out_ref[j] = gathered


def finish_kernel(core_ref, mine_ref, other_ref, items_ref, out_ref):
    def half_rows(source_ref, half):
        for i in range(CHIPS):
            first = pl.multiple_of(half * HALF + i * PIECE, PIECE)
            rows = items_ref[pl.ds(first, PIECE), :].astype(F32)
            grads = jnp.concatenate(
                [source_ref[i, q * PIECE : (q + 1) * PIECE, :] for q in range(D // LANES)], axis=1
            ).astype(F32)
            scale = lax.rsqrt(jnp.sum(rows * rows, axis=1, keepdims=True) + epsilon)
            along = jnp.sum(rows * grads, axis=1, keepdims=True)
            out_ref[pl.ds(first, PIECE), :] = (
                scale * grads - rows * (scale**3 * along)
            ) * (1.0 / loss_scale)

    half_rows(mine_ref, core_ref[0])
    half_rows(other_ref, 1 - core_ref[0])


def local(kernel, outs, operands, scalars=0, scratch=(), flops=0, name=None):
    spaces = [pltpu.SMEM] * scalars + [pltpu.VMEM] * (len(operands) - scalars)
    moved = sum(v.size * v.dtype.itemsize for v in operands) + sum(
        v.size * v.dtype.itemsize for v in outs
    )
    return pl.pallas_call(
        kernel,
        out_shape=tuple(outs),
        in_specs=[pl.BlockSpec(memory_space=s) for s in spaces],
        out_specs=tuple(pl.BlockSpec(memory_space=pltpu.VMEM) for _ in outs),
        scratch_shapes=list(scratch),
        compiler_params=pltpu.CompilerParams(vmem_limit_bytes=56 * 1024 * 1024),
        cost_estimate=pl.CostEstimate(flops=flops, bytes_accessed=moved, transcendentals=0),
        name=name,
    )(*operands)


def shaped(shape, dtype=BF16):
    return jax.ShapeDtypeStruct(shape, dtype)


def shards(tokens, w_proj, w_out, item_rows, lengths, target_owner, target_row, negative_rows):
    tok_rows = tokens.shape[0]
    width = tokens.shape[1]
    item_count = item_rows.shape[0]
    dp = lax.axis_size("dp")
    slots = PLANE * CAP
    negs = PLANE * NEG
    partners = [(i, i ^ 1) for i in range(dp)]
    columns = [[2 * z + c for z in range(CHIPS)] for c in range(2)]
    core = lax.rem(lax.axis_index("dp"), 2).astype(I32)
    core_s = core.reshape(1)

    half_w = width // 2
    first_out, position = local(
        route_kernel,
        [shaped((PLANE, half_w + 16, DH)), shaped((tok_rows, 1), I32)],
        [core_s, target_owner, target_row.reshape(1, tok_rows), w_proj],
        scalars=1,
        name="route",
    )
    first_in = exchange(first_out, "shard")
    w_mine = first_in[:, :half_w]
    w_other = lax.ppermute(w_mine, "dp", partners)

    rows_wide = item_rows.astype(F32)
    item_scale = lax.rsqrt(jnp.sum(rows_wide * rows_wide, axis=1, keepdims=True) + epsilon)
    unit_items = (rows_wide * item_scale).astype(BF16)
    own_pick = (negative_rows[:, None] == iota((NEG, item_count), 1)).astype(BF16)
    own_negs = dot(own_pick, unit_items, ((1,), (0,))).astype(BF16)
    served, asked_pick = local(
        serve_kernel,
        [shaped((PLANE, CAP + NEG, width)), shaped((slots, item_count))],
        [first_in, unit_items, own_negs],
        name="serve",
    )
    looked_up = exchange(served, "shard")

    w_all = jnp.where(
        core == 0,
        jnp.concatenate([w_mine, w_other], axis=1),
        jnp.concatenate([w_other, w_mine], axis=1),
    )
    visible = history_mask(lengths[0], tok_rows)[None]
    wide_tokens = tokens.astype(F32)
    input_scale = lax.rsqrt(jnp.mean(wide_tokens * wide_tokens, axis=1, keepdims=True) + epsilon)
    normed = (wide_tokens * input_scale).astype(BF16)
    normed_s = jnp.broadcast_to(normed[None], (SECTIONS, tok_rows, width))
    pre_act = dot(normed_s, w_all, ((2,), (1,)), ((0,), (0,)))
    activated = jax.nn.silu(pre_act).astype(BF16)
    gate, values, queries, keys = (activated[i * HEADS : (i + 1) * HEADS] for i in range(4))
    scores = dot(queries, keys, ((2,), (2,)), ((0,), (0,))) * DH ** (-0.5)
    score_sig = jax.nn.sigmoid(scores)
    weights = jnp.where(visible, scores * score_sig * (1.0 / MAXLEN), 0.0).astype(BF16)
    joined = dot(weights, values, ((2,), (1,)), ((0,), (0,))).astype(BF16)
    joined_wide = joined.astype(F32)
    middle_scale = lax.rsqrt(
        jnp.sum(joined_wide * joined_wide, axis=(0, 2), keepdims=True) / width + epsilon
    )
    gate_wide = gate.astype(F32)
    gated = (joined_wide * middle_scale * gate_wide).astype(BF16)
    w_out_h = w_out.reshape(HEADS, DH, width)
    layer_out = wide_tokens + jnp.sum(dot(gated, w_out_h, ((2,), (1,)), ((0,), (0,))), axis=0)

    third_out, grad_out, grad_out_b = local(
        loss_kernel,
        [
            shaped((PLANE, CAP + NEG + WROWS, width)),
            shaped((tok_rows, width), F32),
            shaped((tok_rows, width)),
        ],
        [layer_out, gated, looked_up, position],
        scratch=[
            pltpu.VMEM((slots, width), BF16),
            pltpu.VMEM((negs, width), BF16),
            pltpu.VMEM((tok_rows, negs), BF16),
            pltpu.VMEM((tok_rows, width), BF16),
            pltpu.VMEM((tok_rows, width), BF16),
        ],
        name="loss",
    )
    third_in = exchange(third_out, "shard")
    kept, sent = local(
        collect_kernel,
        [shaped((HALF + WROWS // 2, width))] * 2,
        [core_s, third_in, asked_pick, negative_rows.reshape(1, NEG)],
        scalars=1,
        scratch=[pltpu.VMEM((slots, width), BF16)],
        name="collect",
    )
    arrived = lax.ppermute(sent, "dp", partners)
    pieces = (CHIPS, width // LANES * PIECE + 8, LANES)
    (packed,) = local(pack_kernel, [shaped(pieces)], [kept, arrived], name="pack")
    (summed,) = local(
        total_kernel, [shaped(pieces)], [exchange(packed, "dp", columns)], name="total"
    )
    mine = exchange(summed, "dp", columns)
    other = lax.ppermute(mine, "dp", partners)
    (weight_rows,) = local(
        weight_kernel,
        [shaped((PLANE, WROWS, width))],
        [core_s, mine, other],
        scalars=1,
        name="weight",
    )
    weight_grads = exchange(weight_rows, "shard").reshape(width, width).astype(F32) / loss_scale
    (item_grads,) = local(
        finish_kernel,
        [shaped((item_count, width), F32)],
        [core_s, mine, other, item_rows],
        scalars=1,
        name="finish",
    )

    grad_gated = dot(
        jnp.broadcast_to(grad_out_b[None], (HEADS, tok_rows, width)),
        w_out_h,
        ((2,), (2,)),
        ((0,), (0,)),
    )
    grad_gate = grad_gated * joined_wide * middle_scale
    grad_norm = grad_gated * gate_wide
    grad_joined = middle_scale * grad_norm - joined_wide * middle_scale**3 * (
        jnp.sum(joined_wide * grad_norm, axis=(0, 2), keepdims=True) / width
    )
    grad_joined_b = grad_joined.astype(BF16)
    grad_weights = dot(grad_joined_b, values, ((2,), (2,)), ((0,), (0,)))
    grad_values = dot(weights, grad_joined_b, ((1,), (1,)), ((0,), (0,)))
    slope = score_sig * (1.0 + scores * (1.0 - score_sig))
    grad_scores = jnp.where(
        visible, grad_weights * (1.0 / MAXLEN) * slope * DH ** (-0.5), 0.0
    ).astype(BF16)
    grad_queries = dot(grad_scores, keys, ((2,), (1,)), ((0,), (0,)))
    grad_keys = dot(grad_scores, queries, ((1,), (1,)), ((0,), (0,)))
    grad_act = jnp.concatenate([grad_gate, grad_values, grad_queries, grad_keys], axis=0)
    grad_pre = (grad_act * silu_slope(pre_act)).astype(BF16)
    grad_normed = jnp.sum(dot(grad_pre, w_all, ((2,), (2,)), ((0,), (0,))), axis=0)
    grad_input = input_scale * grad_normed - wide_tokens * input_scale**3 * jnp.mean(
        wide_tokens * grad_normed, axis=1, keepdims=True
    )
    grad_tokens = (grad_out + grad_input).astype(BF16)
    return (grad_tokens, weight_grads, item_grads)


def solution(mesh):
    in_specs = (
        P(("dp", "shard"), None),
        P(None, "shard"),
        P(),
        P("shard", None),
        P(("dp", "shard"), None),
        P(("dp", "shard"), None),
        P(("dp", "shard")),
        P("shard"),
    )
    out_specs = (P(("dp", "shard"), None), P(), P("shard", None))
    return jax.shard_map(shards, mesh=mesh, in_specs=in_specs, out_specs=out_specs, check_vma=False)
```

time: 264 us -> 245 us (0.928)
  blocking collectives: 48.4 us -> 83.2 us
  Pallas kernels: 0 us -> 28.7 us
  waiting for transfers between devices: 83.1 us -> 57.4 us
  starting transfers between devices: 55.6 us -> 36.7 us
  other arithmetic: 22 us -> 5.47 us
  matrix products: 39.4 us -> 24.4 us
  local copies, waits for them, and re-layouts: 13 us -> 7.17 us
    all_to_all x9 -> x4, starting transfers between devices: 55.6 us -> 18.5 us  [exchange(): lax.all_to_all(pieces, axis, split_axis=0, concat_axis=0, tiled=True, axi...]
    all_to_all x4 -> x2, blocking collectives: 48.4 us -> 83.2 us  [exchange(): lax.all_to_all(pieces, axis, split_axis=0, concat_axis=0, tiled=True, axi...]
    pallas_call x0 -> x8, Pallas kernels: none -> 28.7 us  [local(): pl.pallas_call(kernel, out_shape=tuple(outs), in_specs=[pl.BlockSpec(memo...]
    all_to_all x9 -> x4, waiting for transfers between devices: 83.1 us -> 55.7 us  [exchange(): lax.all_to_all(pieces, axis, split_axis=0, concat_axis=0, tiled=True, axi...]
    ppermute x0 -> x3, starting transfers between devices: none -> 18.1 us  [the longest x1 8.65 us: shards(): other = lax.ppermute(mine, 'dp', partners)]
    dot_general x21 -> x11, matrix products: 39.4 us -> 24.4 us  [dot(): return lax.dot_general(a, b, (contract, batch), preferred_element_type=F32)]
    broadcast_in_dim x8 -> x0, local copies, waits for them, and re-layouts: 6.65 us -> none  [the longest x6 6.64 us: gather_from(): jnp.broadcast_to(piece[None], (count,) + piece.shape)]
    concatenate x4 -> x0, other arithmetic: 5.44 us -> none  [the longest x1 2.45 us: shards(): jnp.concatenate([outgoing.reshape(owners_count, capacity, width), of_pair...]
  transfers between devices with their start and end apart: 9 -> 7, of which waited for: 9 -> 5; matrix products, arithmetic and copies ran while one was open for 15% -> 12% of each run, Pallas kernels for 0% -> 3%
where the time goes in v2:
time: 245 us; the launch traced here: 244 us
  blocking collectives  83.2 us (34%)
  waiting for transfers between devices  57.4 us (23%)
  starting transfers between devices  36.7 us (15%)
  Pallas kernels  28.7 us (12%)
  matrix products  24.4 us (10%)
  local copies, waits for them, and re-layouts  7.17 us (3%)
  other arithmetic  5.47 us (2%)
    all_to_all x2, blocking collectives, exchange(): lax.all_to_all(pieces, axis, split_axis=0, concat_axis=0, tiled=True, axi...  83.2 us
    all_to_all x4, waiting for transfers between devices, exchange(): lax.all_to_all(pieces, axis, split_axis=0, concat_axis=0, tiled=True, axi...  55.7 us
    pallas_call x8, Pallas kernels, local(): pl.pallas_call(kernel, out_shape=tuple(outs), in_specs=[pl.BlockSpec(memo...  28.7 us
    dot_general x11, matrix products, dot(): return lax.dot_general(a, b, (contract, batch), preferred_element_type=F32)  24.4 us
    all_to_all x4, starting transfers between devices, exchange(): lax.all_to_all(pieces, axis, split_axis=0, concat_axis=0, tiled=True, axi...  18.5 us
    ppermute x1, starting transfers between devices, shards(): other = lax.ppermute(mine, 'dp', partners)  8.65 us
    ppermute x1, starting transfers between devices, shards(): w_other = lax.ppermute(w_mine, 'dp', partners)  5.87 us
  transfers between devices with their start and end apart: 7, of which 5 were waited for; matrix products, arithmetic and copies ran while one was open for 12% of the time, Pallas kernels for 3%

profile of v2, /device:TPU:1, one launch (start us, length us, event | category | flops | bytes accessed | tf_op | source)
XLA Modules:
  0.0 244.0 jit_solution(9699219817229739951)
XLA Ops:
  0.7 1.4 reshape.117.row_ref
  2.1 1.5 copy.20.owner_ref
  3.6 2.9 %route.1 = (bf16[16,272,128]{2,1,0:T(8,128)(2,1)}, s32[384,1]{1,0:T(8,128)}) custom-call(s32[1]{0:T(128)} %bitcast.2.core_ref, s32[384,1]{1,0:T(8,128)} %copy.20.owner_ref, s32[1,384]{1,0:T(1,128)} %reshape.117.row_ref, bf16[512,128]{1,0:T(8,128)(2,1)} %w_ref.1), custom_call_target="tpu_custom_call" | custom-call | bytes 1249796 | tf_op jit(solution)/shard_map/route/pallas_call | solution.py:243
  6.5 7.6 %all-to-all-start = ((bf16[16,272,128]{2,1,0:T(8,128)(2,1)}), bf16[16,272,128]{2,1,0:T(8,128)(2,1)S(1)}, u32[]{:S(2)}, u32[]{:S(2)}) async-start(bf16[16,272,128]{2,1,0:T(8,128)(2,1)} %get-tuple-element.12), calls=%async_computation | async-start | bytes 2228224 | tf_op jit(solution)/shard_map/all_to_all | solution.py:60
  14.1 0.2 reduce-window.4
  14.4 0.3 fusion.3
  14.7 14.6 %all-to-all-done.recv_ref = bf16[16,272,128]{2,1,0:T(8,128)(2,1)S(1)} async-done(((bf16[16,272,128]{2,1,0:T(8,128)(2,1)}), bf16[16,272,128]{2,1,0:T(8,128)(2,1)S(1)}, u32[]{:S(2)}, u32[]{:S(2)}) %all-to-all-start) | async-done | bytes 1114144 | tf_op jit(solution)/shard_map/all_to_all | solution.py:60
  29.4 1.2 slice.25
  30.5 5.9 %collective-permute-start = (bf16[16,256,128]{2,1,0:T(8,128)(2,1)}, bf16[16,256,128]{2,1,0:T(8,128)(2,1)}, u32[]{:S(2)}, u32[]{:S(2)}) collective-permute-start(bf16[16,256,128]{2,1,0:T(8,128)(2,1)} %slice.25), channel_id=1, source_target_pairs={{0,16},{16,0},{32,48},{48,32},{64,80},{80,64},{96,112},{112,96},{1... | collective-permute-start | bytes 3145736 | tf_op jit(solution)/shard_map/ppermute | solution.py:281
  36.5 0.8 fusion.26
  37.4 0.3 fusion.4.items_ref
  37.8 1.0 convolution_convert_fusion.1.negs_ref
  38.7 4.2 %serve.1 = (bf16[16,112,512]{2,1,0:T(8,128)(2,1)}, bf16[768,1024]{1,0:T(8,128)(2,1)}) custom-call(bf16[16,272,128]{2,1,0:T(8,128)(2,1)} %copy-done.1, bf16[1024,512]{1,0:T(8,128)(2,1)} %copy-done.3, bf16[64,512]{1,0:T(8,128)(2,1)} %convolution_convert_fusion.1.negs_ref), custom_call_target="tpu_custom_call" | custom-call | bytes 5636096 | tf_op jit(solution)/shard_map/serve/pallas_call | solution.py:243
  42.9 3.7 %all-to-all-start.1 = ((bf16[16,112,512]{2,1,0:T(8,128)(2,1)}), bf16[16,112,512]{2,1,0:T(8,128)(2,1)S(1)}, u32[]{:S(2)}, u32[]{:S(2)}) async-start(bf16[16,112,512]{2,1,0:T(8,128)(2,1)} %get-tuple-element.13), calls=%async_computation.1 | async-start | bytes 3670016 | tf_op jit(solution)/shard_map/all_to_all | solution.py:60
  46.7 5.7 %multiply_convert_fusion = (bf16[16,384,128]{2,1,0:T(8,128)(2,1)S(1)}, f32[16,384,128]{2,1,0:T(8,128)}) fusion(bf16[16,256,128]{2,1,0:T(8,128)(2,1)} %collective-permute-done, bf16[16,256,128]{2,1,0:T(8,128)(2,1)} %slice.25, pred[]{:T(512)S(6)} %eq.31, bf16[384,512]{1,0:T(8,128)(2,1)S(1)} %fusion.12), kind=kOutput, calls=%fused_computation.2 | convolution fusion | flops 818675712 | bytes 7208961 | tf_op jit(solution)/shard_map/dot_general | solution.py:34
  52.4 2.5 %select_convert_fusion.1 = (bf16[4,384,384]{2,1,0:T(8,128)(2,1)S(1)}, f32[4,384,384]{2,1,0:T(8,128)}) fusion(pred[384,384]{1,0:T(8,128)(4,1)S(1)} %copy-done.15, bf16[16,384,128]{2,1,0:T(8,128)(2,1)S(1)} %get-tuple-element.27), kind=kOutput, calls=%fused_computation.9 | convolution fusion | flops 155713536 | bytes 5652480 | tf_op jit(solution)/shard_map/dot_general | solution.py:34
  54.9 0.5 fusion.18
  55.4 0.2 fusion.10.gated_ref
  55.7 0.2 copy-done.11
  55.9 1.3 convert_add_fusion.layer_ref
  57.2 19.6 %all-to-all-done.1.recv_ref = bf16[16,112,512]{2,1,0:T(8,128)(2,1)S(1)} async-done(((bf16[16,112,512]{2,1,0:T(8,128)(2,1)}), bf16[16,112,512]{2,1,0:T(8,128)(2,1)S(1)}, u32[]{:S(2)}, u32[]{:S(2)}) %all-to-all-start.1) | async-done | bytes 1835040 | tf_op jit(solution)/shard_map/all_to_all | solution.py:60
  76.8 1.2 copy-done.4
  78.0 7.3 %loss.1 = (bf16[16,144,512]{2,1,0:T(8,128)(2,1)}, f32[384,512]{1,0:T(8,128)}, bf16[384,512]{1,0:T(8,128)(2,1)}) custom-call(f32[384,512]{1,0:T(8,128)} %convert_add_fusion.layer_ref, bf16[4,384,128]{2,1,0:T(8,128)(2,1)} %copy-done.7, bf16[16,112,512]{2,1,0:T(8,128)(2,1)} %copy-done.4, s32[384,1]{1,0:T(8,128)} %get-tuple-element.14.pos_ref), custom_call_target="tpu_custom_call" | custom-call | bytes 6555136 | tf_op jit(solution)/shard_map/loss/pallas_call | solution.py:243
  85.3 34.9 %all_to_all.30.recv_ref = bf16[16,144,512]{2,1,0:T(8,128)(2,1)} all-to-all(bf16[16,144,512]{2,1,0:T(8,128)(2,1)} %get-tuple-element.17), channel_id=1, replica_groups=mesh['dp'=32,'shard'=16] {'shard'}, dimensions={0} | all-to-all | bytes 4718592 | tf_op jit(solution)/shard_map/all_to_all | solution.py:60
  120.2 4.3 %collect.1 = (bf16[528,512]{1,0:T(8,128)(2,1)}, bf16[528,512]{1,0:T(8,128)(2,1)}) custom-call(s32[1]{0:T(128)} %bitcast.2.core_ref, bf16[16,144,512]{2,1,0:T(8,128)(2,1)} %all_to_all.30.recv_ref, bf16[768,1024]{1,0:T(8,128)(2,1)} %get-tuple-element.18.pick_ref, s32[1,64]{1,0:T(1,128)} %bitcast.27), custom_call_target="tpu_custom_call" | custom-call | bytes 5013764 | tf_op jit(solution)/shard_map/collect/pallas_call | solution.py:243
  124.5 3.6 %collective-permute-start.1 = (bf16[528,512]{1,0:T(8,128)(2,1)}, bf16[528,512]{1,0:T(8,128)(2,1)S(1)}, u32[]{:S(2)}, u32[]{:S(2)}) collective-permute-start(bf16[528,512]{1,0:T(8,128)(2,1)} %get-tuple-element.20), channel_id=1, source_target_pairs={{0,16},{16,0},{32,48},{48,32},{64,80},{80,64},{96,112},{112,96},{1... | collective-permute-start | bytes 1622024 | tf_op jit(solution)/shard_map/ppermute | solution.py:348
  128.2 1.7 collective-permute-done.1.other_ref
  129.9 0.8 copy-done.14
  130.7 2.3 pack.1
  133.0 48.2 %all_to_all.31.recv_ref = bf16[16,136,128]{2,1,0:T(8,128)(2,1)} all-to-all(bf16[16,136,128]{2,1,0:T(8,128)(2,1)} %pack.1), channel_id=1, replica_groups={{0,32,64,96,128,160,192,224,256,288,320,352,384,416,448,480},{16,48,80,..., dimensions={0} | all-to-all | bytes 1114112 | tf_op jit(solution)/shard_map/all_to_all | solution.py:60
  181.2 2.0 total.1
  183.2 3.7 %all-to-all-start.4 = ((bf16[16,136,128]{2,1,0:T(8,128)(2,1)}), bf16[16,136,128]{2,1,0:T(8,128)(2,1)S(1)}, u32[]{:S(2)}, u32[]{:S(2)}) async-start(bf16[16,136,128]{2,1,0:T(8,128)(2,1)} %total.1), calls=%async_computation.4 | async-start | bytes 1114112 | tf_op jit(solution)/shard_map/all_to_all | solution.py:60
  186.9 1.7 fusion.23
  188.7 1.2 fusion.19
  189.9 1.4 fusion.40
  191.3 1.4 select_convert_fusion
  192.8 1.5 fusion.27
  194.2 1.4 fusion.31
  195.6 14.9 %all-to-all-done.4.mine_ref = bf16[16,136,128]{2,1,0:T(8,128)(2,1)S(1)} async-done(((bf16[16,136,128]{2,1,0:T(8,128)(2,1)}), bf16[16,136,128]{2,1,0:T(8,128)(2,1)S(1)}, u32[]{:S(2)}, u32[]{:S(2)}) %all-to-all-start.4) | async-done | bytes 557088 | tf_op jit(solution)/shard_map/all_to_all | solution.py:60
  210.5 8.7 %collective-permute-start.2 = (bf16[16,136,128]{2,1,0:T(8,128)(2,1)S(1)}, bf16[16,136,128]{2,1,0:T(8,128)(2,1)S(1)}, u32[]{:S(2)}, u32[]{:S(2)}) collective-permute-start(bf16[16,136,128]{2,1,0:T(8,128)(2,1)S(1)} %all-to-all-done.4.mine_ref), channel_id=1, source_target_pairs={{0,16},{16,0},{32,48},{48,32},{64,80},{80,64},{96,112},{112,96},{1... | collective-permute-start | bytes 1671176 | tf_op jit(solution)/shard_map/ppermute | solution.py:355
  219.1 5.9 %fusion.17 = (f32[384]{0:T(512)S(1)}, f32[384,512]{1,0:T(8,128)S(1)}) fusion(bf16[384,512]{1,0:T(8,128)(2,1)S(1)} %copy-done.5, bf16[16,256,128]{2,1,0:T(8,128)(2,1)} %collective-permute-done, bf16[16,256,128]{2,1,0:T(8,128)(2,1)} %slice.25, pred[]{:T(512)S(6)} %eq.31, f32[4,384,128]{2,1,0:T(8,128)} %fusion.27, f32[4,384,128]{2,1,0:T(8,128)} %fusion.31, ...), kind=kOutput, calls=%fused_computation.39 | convolution fusion | flops 824770176 | bytes 9569793 | tf_op jit(solution)/shard_map/dot_general | solution.py:34
  225.1 0.8 copy-done.8
  225.9 2.1 weight.1
  228.0 3.6 %all-to-all-start.5 = ((bf16[16,32,512]{2,1,0:T(8,128)(2,1)}), bf16[16,32,512]{2,1,0:T(8,128)(2,1)S(1)}, u32[]{:S(2)}, u32[]{:S(2)}) async-start(bf16[16,32,512]{2,1,0:T(8,128)(2,1)} %weight.1), calls=%async_computation.5 | async-start | bytes 1048576 | tf_op jit(solution)/shard_map/all_to_all | solution.py:60
  231.6 1.0 fusion.16
  232.6 3.7 %finish.1 = f32[1024,512]{1,0:T(8,128)} custom-call(s32[1]{0:T(128)} %bitcast.2.core_ref, bf16[16,136,128]{2,1,0:T(8,128)(2,1)} %copy-done.6, bf16[16,136,128]{2,1,0:T(8,128)(2,1)} %copy-done.8, bf16[1024,512]{1,0:T(8,128)(2,1)} %items_ref.1), custom_call_target="tpu_custom_call" | custom-call | bytes 4259844 | tf_op jit(solution)/shard_map/finish/pallas_call | solution.py:243
  236.2 6.6 %all-to-all-done.5 = bf16[16,32,512]{2,1,0:T(8,128)(2,1)S(1)} async-done(((bf16[16,32,512]{2,1,0:T(8,128)(2,1)}), bf16[16,32,512]{2,1,0:T(8,128)(2,1)S(1)}, u32[]{:S(2)}, u32[]{:S(2)}) %all-to-all-start.5) | async-done | bytes 524320 | tf_op jit(solution)/shard_map/all_to_all | solution.py:60
  242.8 1.1 convert_multiply_fusion.11
  (47 shorter events, 0.5 us)
Async XLA Ops:
  0.6 55.0 %copy-start = (bf16[512,512]{1,0:T(8,128)(2,1)S(1)}, bf16[512,512]{1,0:T(8,128)(2,1)}, u32[]{:S(2)}) copy-start(bf16[512,512]{1,0:T(8,128)(2,1)} %param.10) | copy-start | bytes 1572868
  0.6 13.4 %copy-start.18 = (s32[1,4]{1,0:T(1,128)S(1)}, s32[1,4]{1,0:T(1,128)}, u32[]{:S(2)}) copy-start(s32[1,4]{1,0:T(1,128)} %param.12) | copy-start | bytes 52
  0.7 13.6 %copy-start.5 = (bf16[384,512]{1,0:T(8,128)(2,1)S(1)}, bf16[384,512]{1,0:T(8,128)(2,1)}, u32[]{:S(2)}) copy-start(bf16[384,512]{1,0:T(8,128)(2,1)} %param.8) | copy-start | bytes 1179652
  0.7 13.7 %copy-start.2 = (bf16[1024,512]{1,0:T(8,128)(2,1)S(1)}, bf16[1024,512]{1,0:T(8,128)(2,1)}, u32[]{:S(2)}) copy-start(bf16[1024,512]{1,0:T(8,128)(2,1)} %items_ref.1) | copy-start | bytes 3145732
  6.5 22.9 %all-to-all-start = ((bf16[16,272,128]{2,1,0:T(8,128)(2,1)}), bf16[16,272,128]{2,1,0:T(8,128)(2,1)S(1)}, u32[]{:S(2)}, u32[]{:S(2)}) async-start(bf16[16,272,128]{2,1,0:T(8,128)(2,1)} %get-tuple-element.12), calls=%async_computation | async-start | bytes 2228224 | tf_op jit(solution)/shard_map/all_to_all | solution.py:60
  14.7 23.0 %copy-start.17 = (s32[64]{0:T(128)S(1)}, s32[64]{0:T(128)}, u32[]{:S(2)}) copy-start(s32[64]{0:T(128)} %param.15) | copy-start | bytes 772
  29.4 8.4 %copy-start.1 = (bf16[16,272,128]{2,1,0:T(8,128)(2,1)}, bf16[16,272,128]{2,1,0:T(8,128)(2,1)S(1)}, u32[]{:S(2)}) copy-start(bf16[16,272,128]{2,1,0:T(8,128)(2,1)S(1)} %all-to-all-done.recv_ref) | copy-start | bytes 3342340
  30.5 16.1 %collective-permute-start = (bf16[16,256,128]{2,1,0:T(8,128)(2,1)}, bf16[16,256,128]{2,1,0:T(8,128)(2,1)}, u32[]{:S(2)}, u32[]{:S(2)}) collective-permute-start(bf16[16,256,128]{2,1,0:T(8,128)(2,1)} %slice.25), channel_id=1, source_target_pairs={{0,16},{16,0},{32,48},{48,32},{64,80},{80,64},{96,112},{112,96},{1... | collective-permute-start | bytes 3145736 | tf_op jit(solution)/shard_map/ppermute | solution.py:281
  37.7 1.0 copy-start.3
  42.9 33.8 %all-to-all-start.1 = ((bf16[16,112,512]{2,1,0:T(8,128)(2,1)}), bf16[16,112,512]{2,1,0:T(8,128)(2,1)S(1)}, u32[]{:S(2)}, u32[]{:S(2)}) async-start(bf16[16,112,512]{2,1,0:T(8,128)(2,1)} %get-tuple-element.13), calls=%async_computation.1 | async-start | bytes 3670016 | tf_op jit(solution)/shard_map/all_to_all | solution.py:60
  46.6 5.7 %copy-start.15 = (pred[384,384]{1,0:T(8,128)(4,1)S(1)}, pred[384,384]{1,0:T(8,128)(4,1)}, u32[]{:S(2)}) copy-start(pred[384,384]{1,0:T(8,128)(4,1)} %fusion.26) | copy-start | bytes 442372
  52.4 3.1 %copy-start.9 = (bf16[16,384,128]{2,1,0:T(8,128)(2,1)}, bf16[16,384,128]{2,1,0:T(8,128)(2,1)S(1)}, u32[]{:S(2)}) copy-start(bf16[16,384,128]{2,1,0:T(8,128)(2,1)S(1)} %get-tuple-element.27) | copy-start | bytes 4718596
  54.9 1.0 copy-start.11
  55.7 21.1 %copy-start.7 = (bf16[4,384,128]{2,1,0:T(8,128)(2,1)}, bf16[4,384,128]{2,1,0:T(8,128)(2,1)S(1)}, u32[]{:S(2)}) copy-start(bf16[4,384,128]{2,1,0:T(8,128)(2,1)S(1)} %fusion.10.gated_ref) | copy-start | bytes 1179652
  76.8 1.2 copy-start.4
  124.5 5.4 %collective-permute-start.1 = (bf16[528,512]{1,0:T(8,128)(2,1)}, bf16[528,512]{1,0:T(8,128)(2,1)S(1)}, u32[]{:S(2)}, u32[]{:S(2)}) collective-permute-start(bf16[528,512]{1,0:T(8,128)(2,1)} %get-tuple-element.20), channel_id=1, source_target_pairs={{0,16},{16,0},{32,48},{48,32},{64,80},{80,64},{96,112},{112,96},{1... | collective-permute-start | bytes 1622024 | tf_op jit(solution)/shard_map/ppermute | solution.py:348
  129.9 0.8 copy-start.14
  130.7 56.2 %copy-start.10 = (bf16[16,384,128]{2,1,0:T(8,128)(2,1)S(1)}, bf16[16,384,128]{2,1,0:T(8,128)(2,1)}, u32[]{:S(2)}) copy-start(bf16[16,384,128]{2,1,0:T(8,128)(2,1)} %copy-done.9) | copy-start | bytes 4718596
  183.2 27.3 %all-to-all-start.4 = ((bf16[16,136,128]{2,1,0:T(8,128)(2,1)}), bf16[16,136,128]{2,1,0:T(8,128)(2,1)S(1)}, u32[]{:S(2)}, u32[]{:S(2)}) async-start(bf16[16,136,128]{2,1,0:T(8,128)(2,1)} %total.1), calls=%async_computation.4 | async-start | bytes 1114112 | tf_op jit(solution)/shard_map/all_to_all | solution.py:60
  186.9 3.0 %copy-start.12 = (bf16[4,384,384]{2,1,0:T(8,128)(2,1)S(1)}, bf16[4,384,384]{2,1,0:T(8,128)(2,1)}, u32[]{:S(2)}) copy-start(bf16[4,384,384]{2,1,0:T(8,128)(2,1)} %copy-done.11) | copy-start | bytes 3538948
  188.6 2.7 %copy-start.16 = (pred[384,384]{1,0:T(8,128)(4,1)S(1)}, pred[384,384]{1,0:T(8,128)(4,1)}, u32[]{:S(2)}) copy-start(pred[384,384]{1,0:T(8,128)(4,1)} %fusion.26) | copy-start | bytes 442372
  188.7 2.7 %copy-start.19 = (f32[4,384,384]{2,1,0:T(8,128)S(1)}, f32[4,384,384]{2,1,0:T(8,128)}, u32[]{:S(2)}) copy-start(f32[4,384,384]{2,1,0:T(8,128)} %get-tuple-element.30) | copy-start | bytes 7077892
  210.5 14.6 %copy-start.6 = (bf16[16,136,128]{2,1,0:T(8,128)(2,1)}, bf16[16,136,128]{2,1,0:T(8,128)(2,1)S(1)}, u32[]{:S(2)}) copy-start(bf16[16,136,128]{2,1,0:T(8,128)(2,1)S(1)} %all-to-all-done.4.mine_ref) | copy-start | bytes 1671172
  210.5 14.6 %collective-permute-start.2 = (bf16[16,136,128]{2,1,0:T(8,128)(2,1)S(1)}, bf16[16,136,128]{2,1,0:T(8,128)(2,1)S(1)}, u32[]{:S(2)}, u32[]{:S(2)}) collective-permute-start(bf16[16,136,128]{2,1,0:T(8,128)(2,1)S(1)} %all-to-all-done.4.mine_ref), channel_id=1, source_target_pairs={{0,16},{16,0},{32,48},{48,32},{64,80},{80,64},{96,112},{112,96},{1... | collective-permute-start | bytes 1671176 | tf_op jit(solution)/shard_map/ppermute | solution.py:355
  225.0 6.5 %copy-start.13 = (f32[384,512]{1,0:T(8,128)S(1)}, f32[384,512]{1,0:T(8,128)}, u32[]{:S(2)}) copy-start(f32[384,512]{1,0:T(8,128)} %get-tuple-element.15) | copy-start | bytes 2359300
  225.1 0.8 copy-start.8
  228.0 14.9 %all-to-all-start.5 = ((bf16[16,32,512]{2,1,0:T(8,128)(2,1)}), bf16[16,32,512]{2,1,0:T(8,128)(2,1)S(1)}, u32[]{:S(2)}, u32[]{:S(2)}) async-start(bf16[16,32,512]{2,1,0:T(8,128)(2,1)} %weight.1), calls=%async_computation.5 | async-start | bytes 1048576 | tf_op jit(solution)/shard_map/all_to_all | solution.py:60

commit v3 on v2

--- a/solution.py
+++ b/solution.py
@@ -1,5 +1,3 @@
-import functools
-
 import jax
 import jax.numpy as jnp
 from jax import lax
@@ -17,9 +15,13 @@
 NEG = 64
 WROWS = 32
 CHIPS = 16
+NEAR = 4
+FAR = 4
 HALF = 512
 PIECE = 32
+SHARED = 16
 LANES = 128
+BLOCKS = D // LANES
 
 epsilon = 1e-06
 logit_scale = 64.0
@@ -62,27 +64,38 @@
     )
 
 
-def route_kernel(core_ref, owner_ref, row_ref, w_ref, out_ref, pos_ref):
-    tok = owner_ref.shape[0]
-    owners = owner_ref[...]
+def route_kernel(core_ref, index_ref, w_ref, items_ref, out_ref, pos_ref):
+    tok = pos_ref.shape[0]
+    first = core_ref[0] == 0
+    owners = jnp.broadcast_to(index_ref[0:1, 0:tok].astype(F32), (LANES, tok)).T.astype(I32)
     hits = owners == iota((tok, LANES), 1)
     earlier = one_hot(iota((tok, tok), 1) < iota((tok, tok), 0))
     before = dot(earlier, one_hot(hits), ((1,), (0,)))
     slot = jnp.sum(jnp.where(hits, before, 0.0), axis=1, keepdims=True).astype(I32)
+    owners = owners[:, 0:1]
     pos_ref[...] = owners * CAP + slot
     spread = one_hot(owners * LANES + slot == iota((tok, PLANE * LANES), 1))
-    asked = jnp.broadcast_to(row_ref[...], (16, tok))
+    asked = jnp.broadcast_to(index_ref[0:1, tok : 2 * tok], (16, tok))
     which = iota((16, tok), 0)
     digits = jnp.where(which == 0, asked >> 5, jnp.where(which == 1, asked & 31, 0))
     requests = dot(digits.astype(F32).astype(BF16), spread, ((1,), (0,))).astype(BF16)
+    here = one_hot(iota((items_ref.shape[0], NEG), 0) == index_ref[0:1, 2 * tok :])
+    negs = dot(here, items_ref[...], ((0,), (0,)))
+    negs = jnp.where(first, negs[0 : NEG // 2], negs[NEG // 2 :])
+    scale = lax.rsqrt(jnp.sum(negs * negs, axis=1, keepdims=True) + epsilon)
+    negs = (negs * scale).astype(BF16)
     rows = w_ref.shape[0] // 2
     own = w_ref[pl.ds(pl.multiple_of(core_ref[0] * rows, rows), rows), :]
     for j in range(PLANE):
         out_ref[j, 0:rows, :] = own
-        out_ref[j, rows : rows + 16, :] = requests[:, j * LANES : (j + 1) * LANES]
-
-
-def serve_kernel(recv_ref, items_ref, negs_ref, out_ref, pick_ref):
+        for q in range(BLOCKS):
+            at = rows + q * (NEG // 2)
+            out_ref[j, at : at + NEG // 2, :] = negs[:, q * LANES : (q + 1) * LANES]
+        at = rows + BLOCKS * (NEG // 2)
+        out_ref[j, at : at + 16, :] = requests[:, j * LANES : (j + 1) * LANES]
+
+
+def serve_kernel(recv_ref, items_ref, out_ref, pick_ref):
     rows = recv_ref.shape[1] - 16
     count = items_ref.shape[0]
     diagonal = iota((CAP, LANES), 0) == iota((CAP, LANES), 1)
@@ -93,20 +106,21 @@
             jnp.where(diagonal, jnp.broadcast_to(asked, (CAP, LANES)), 0.0), axis=1, keepdims=True
         ).astype(I32)
         pick_ref[j * CAP : (j + 1) * CAP, :] = one_hot(column == iota((CAP, count), 1))
-    negs = negs_ref[...]
     step = 4
     for j in range(0, PLANE, step):
         served = dot(pick_ref[j * CAP : (j + step) * CAP, :], items_ref[...], ((1,), (0,)))
         served = served.astype(BF16)
         for i in range(step):
-            out_ref[j + i, 0:CAP, :] = served[i * CAP : (i + 1) * CAP]
-            out_ref[j + i, CAP : CAP + NEG, :] = negs
+            out_ref[j + i] = served[i * CAP : (i + 1) * CAP]
 
 
 def loss_kernel(
+    core_ref,
     layer_ref,
     gated_ref,
     recv_ref,
+    mine_ref,
+    other_ref,
     pos_ref,
     out_ref,
     grad_ref,
@@ -118,9 +132,15 @@
     back,
 ):
     tok = layer_ref.shape[0]
+    part = NEG // 2
+    rows = mine_ref.shape[1] - 16 - BLOCKS * part
     for j in range(PLANE):
-        fetched[j * CAP : (j + 1) * CAP, :] = recv_ref[j, 0:CAP, :]
-        decoys[j * NEG : (j + 1) * NEG, :] = recv_ref[j, CAP : CAP + NEG, :]
+        fetched[j * CAP : (j + 1) * CAP, :] = recv_ref[j]
+        for ref, half in ((mine_ref, core_ref[0]), (other_ref, 1 - core_ref[0])):
+            at = pl.multiple_of(j * NEG + half * part, part)
+            for q in range(BLOCKS):
+                block = ref[j, rows + q * part : rows + (q + 1) * part, :]
+                decoys[pl.ds(at, part), q * LANES : (q + 1) * LANES] = block
     step = 128
     for c in range(0, tok, step):
         layer_out = layer_ref[c : c + step, :]
@@ -177,62 +197,61 @@
         ref[HALF:, :] = part.astype(BF16)
 
 
-def pack_kernel(keep_ref, other_ref, out_ref):
-    for i in range(CHIPS):
-        rows = slice(i * PIECE, (i + 1) * PIECE)
-        total = keep_ref[rows, :].astype(F32) + other_ref[rows, :].astype(F32)
-        total = total.astype(BF16)
-        for q in range(D // LANES):
-            out_ref[i, q * PIECE : (q + 1) * PIECE, :] = total[:, q * LANES : (q + 1) * LANES]
-    weights = keep_ref[HALF:, :].astype(F32) + other_ref[HALF:, :].astype(F32)
-    for i in range(CHIPS):
-        row = weights[i : i + 1, :]
-        parts = [row[:, q * LANES : (q + 1) * LANES] for q in range(D // LANES)]
-        parts.append(jnp.zeros((8 - D // LANES, LANES), F32))
-        out_ref[i, D // LANES * PIECE :, :] = jnp.concatenate(parts, axis=0).astype(BF16)
-
-
-def total_kernel(recv_ref, out_ref):
+def near_kernel(keep_ref, other_ref, out_ref):
+    rows = HALF // NEAR
+    weights = (keep_ref[HALF:, :].astype(F32) + other_ref[HALF:, :].astype(F32)).astype(BF16)
+    for i in range(NEAR):
+        at = slice(i * rows, (i + 1) * rows)
+        total = keep_ref[at, :].astype(F32) + other_ref[at, :].astype(F32)
+        out_ref[i, 0:rows, :] = total.astype(BF16)
+        out_ref[i, rows:, :] = weights
+
+
+def far_kernel(recv_ref, out_ref):
+    rows = recv_ref.shape[1] - SHARED
     total = recv_ref[0].astype(F32)
-    for i in range(1, CHIPS):
+    for i in range(1, NEAR):
+        total = total + recv_ref[i].astype(F32)
+    total = total.astype(BF16)
+    for i in range(FAR):
+        out_ref[i, 0:PIECE, :] = total[i * PIECE : (i + 1) * PIECE]
+        out_ref[i, PIECE:, :] = total[rows:]
+
+
+def total_kernel(recv_ref, out_ref, weights_ref):
+    total = recv_ref[0].astype(F32)
+    for i in range(1, FAR):
         total = total + recv_ref[i].astype(F32)
     total = total.astype(BF16)
     for i in range(CHIPS):
-        out_ref[i] = total
-
-
-def weight_kernel(core_ref, mine_ref, other_ref, out_ref):
-    first = core_ref[0] == 0
-    rows = []
-    for half in range(2):
+        out_ref[i] = total[0:PIECE]
+    weights_ref[...] = total[PIECE:]
+
+
+def weight_kernel(place_ref, mine_ref, other_ref, out_ref):
+    core, plane_y, plane_x = place_ref[0], place_ref[1], place_ref[2]
+    for ref, half in ((mine_ref, core), (other_ref, 1 - core)):
+        for ky in range(4):
+            for kx in range(4):
+                owner = ((plane_y - ky) & 3) * 4 + ((plane_x - kx) & 3)
+                at = pl.multiple_of(owner * WROWS + half * SHARED, SHARED)
+                first = (ky * 4 + kx) * SHARED
+                rows = ref[first : first + SHARED, :].astype(F32)
+                out_ref[pl.ds(at, SHARED), :] = rows * (1.0 / loss_scale)
+
+
+def finish_kernel(core_ref, mine_ref, other_ref, items_ref, out_ref):
+    for ref, half in ((mine_ref, core_ref[0]), (other_ref, 1 - core_ref[0])):
         for i in range(CHIPS):
-            mine = mine_ref[i, D // LANES * PIECE :, :].astype(F32)
-            other = other_ref[i, D // LANES * PIECE :, :].astype(F32)
-            block = jnp.where(first, mine, other) if half == 0 else jnp.where(first, other, mine)
-            rows.append(
-                jnp.concatenate([block[q : q + 1, :] for q in range(D // LANES)], axis=1)
-            )
-    gathered = jnp.concatenate(rows, axis=0).astype(BF16)
-    for j in range(PLANE):
-        out_ref[j] = gathered
-
-
-def finish_kernel(core_ref, mine_ref, other_ref, items_ref, out_ref):
-    def half_rows(source_ref, half):
-        for i in range(CHIPS):
-            first = pl.multiple_of(half * HALF + i * PIECE, PIECE)
+            start = (i % NEAR) * (HALF // NEAR) + (i // NEAR) * PIECE
+            first = pl.multiple_of(half * HALF + start, PIECE)
             rows = items_ref[pl.ds(first, PIECE), :].astype(F32)
-            grads = jnp.concatenate(
-                [source_ref[i, q * PIECE : (q + 1) * PIECE, :] for q in range(D // LANES)], axis=1
-            ).astype(F32)
+            grads = ref[i].astype(F32)
             scale = lax.rsqrt(jnp.sum(rows * rows, axis=1, keepdims=True) + epsilon)
             along = jnp.sum(rows * grads, axis=1, keepdims=True)
             out_ref[pl.ds(first, PIECE), :] = (
                 scale * grads - rows * (scale**3 * along)
             ) * (1.0 / loss_scale)
-
-    half_rows(mine_ref, core_ref[0])
-    half_rows(other_ref, 1 - core_ref[0])
 
 
 def local(kernel, outs, operands, scalars=0, scratch=(), flops=0, name=None):
@@ -265,33 +284,44 @@
     negs = PLANE * NEG
     partners = [(i, i ^ 1) for i in range(dp)]
     columns = [[2 * z + c for z in range(CHIPS)] for c in range(2)]
+    near = [[2 * (NEAR * h + l) + c for l in range(NEAR)] for h in range(FAR) for c in range(2)]
+    far = [[2 * (NEAR * h + l) + c for h in range(FAR)] for l in range(NEAR) for c in range(2)]
     core = lax.rem(lax.axis_index("dp"), 2).astype(I32)
     core_s = core.reshape(1)
+    plane = lax.axis_index("shard").astype(I32)
 
     half_w = width // 2
+    index = jnp.concatenate([target_owner[:, 0], target_row, negative_rows]).reshape(1, -1)
     first_out, position = local(
         route_kernel,
-        [shaped((PLANE, half_w + 16, DH)), shaped((tok_rows, 1), I32)],
-        [core_s, target_owner, target_row.reshape(1, tok_rows), w_proj],
+        [
+            shaped((PLANE, half_w + BLOCKS * NEG // 2 + 16, DH)),
+            shaped((tok_rows, 1), I32),
+        ],
+        [core_s, index, w_proj, item_rows],
         scalars=1,
         name="route",
     )
     first_in = exchange(first_out, "shard")
+    first_other = lax.ppermute(first_in, "dp", partners)
     w_mine = first_in[:, :half_w]
-    w_other = lax.ppermute(w_mine, "dp", partners)
+    w_other = first_other[:, :half_w]
 
     rows_wide = item_rows.astype(F32)
     item_scale = lax.rsqrt(jnp.sum(rows_wide * rows_wide, axis=1, keepdims=True) + epsilon)
     unit_items = (rows_wide * item_scale).astype(BF16)
-    own_pick = (negative_rows[:, None] == iota((NEG, item_count), 1)).astype(BF16)
-    own_negs = dot(own_pick, unit_items, ((1,), (0,))).astype(BF16)
     served, asked_pick = local(
         serve_kernel,
-        [shaped((PLANE, CAP + NEG, width)), shaped((slots, item_count))],
-        [first_in, unit_items, own_negs],
+        [shaped((PLANE, CAP, width)), shaped((slots, item_count))],
+        [first_in, unit_items],
         name="serve",
     )
     looked_up = exchange(served, "shard")
+    w_all = jnp.where(
+        core == 0,
+        jnp.concatenate([w_mine, w_other], axis=1),
+        jnp.concatenate([w_other, w_mine], axis=1),
+    )
 
     w_all = jnp.where(
         core == 0,
@@ -326,7 +356,8 @@
             shaped((tok_rows, width), F32),
             shaped((tok_rows, width)),
         ],
-        [layer_out, gated, looked_up, position],
+        [core_s, layer_out, gated, looked_up, first_in, first_other, position],
+        scalars=1,
         scratch=[
             pltpu.VMEM((slots, width), BF16),
             pltpu.VMEM((negs, width), BF16),
@@ -337,37 +368,6 @@
         name="loss",
     )
     third_in = exchange(third_out, "shard")
-    kept, sent = local(
-        collect_kernel,
-        [shaped((HALF + WROWS // 2, width))] * 2,
-        [core_s, third_in, asked_pick, negative_rows.reshape(1, NEG)],
-        scalars=1,
-        scratch=[pltpu.VMEM((slots, width), BF16)],
-        name="collect",
-    )
-    arrived = lax.ppermute(sent, "dp", partners)
-    pieces = (CHIPS, width // LANES * PIECE + 8, LANES)
-    (packed,) = local(pack_kernel, [shaped(pieces)], [kept, arrived], name="pack")
-    (summed,) = local(
-        total_kernel, [shaped(pieces)], [exchange(packed, "dp", columns)], name="total"
-    )
-    mine = exchange(summed, "dp", columns)
-    other = lax.ppermute(mine, "dp", partners)
-    (weight_rows,) = local(
-        weight_kernel,
-        [shaped((PLANE, WROWS, width))],
-        [core_s, mine, other],
-        scalars=1,
-        name="weight",
-    )
-    weight_grads = exchange(weight_rows, "shard").reshape(width, width).astype(F32) / loss_scale
-    (item_grads,) = local(
-        finish_kernel,
-        [shaped((item_count, width), F32)],
-        [core_s, mine, other, item_rows],
-        scalars=1,
-        name="finish",
-    )
 
     grad_gated = dot(
         jnp.broadcast_to(grad_out_b[None], (HEADS, tok_rows, width)),
@@ -396,6 +396,62 @@
         wide_tokens * grad_normed, axis=1, keepdims=True
     )
     grad_tokens = (grad_out + grad_input).astype(BF16)
+    third_in, grad_tokens = lax.optimization_barrier((third_in, grad_tokens))
+
+    kept, sent = local(
+        collect_kernel,
+        [shaped((HALF + WROWS // 2, width))] * 2,
+        [core_s, third_in, asked_pick, negative_rows.reshape(1, NEG)],
+        scalars=1,
+        scratch=[pltpu.VMEM((slots, width), BF16)],
+        name="collect",
+    )
+    arrived = lax.ppermute(sent, "dp", partners)
+    (near_out,) = local(
+        near_kernel,
+        [shaped((NEAR, HALF // NEAR + SHARED, width))],
+        [kept, arrived],
+        name="near",
+    )
+    (far_out,) = local(
+        far_kernel,
+        [shaped((FAR, PIECE + SHARED, width))],
+        [exchange(near_out, "dp", near)],
+        name="far",
+    )
+    summed, w_rows = local(
+        total_kernel,
+        [shaped((CHIPS, PIECE, width)), shaped((SHARED, width))],
+        [exchange(far_out, "dp", far)],
+        name="total",
+    )
+    mine = exchange(summed, "dp", columns)
+
+    def turned(rows, step_y, step_x):
+        moves = [
+            (y * 4 + x, (y + step_y) % 4 * 4 + (x + step_x) % 4) for y in range(4) for x in range(4)
+        ]
+        return lax.ppermute(rows, "shard", moves)
+
+    w_rows = jnp.concatenate([w_rows] + [turned(w_rows, 0, k) for k in (1, 2, 3)], axis=0)
+    w_rows = jnp.concatenate([w_rows] + [turned(w_rows, k, 0) for k in (1, 2, 3)], axis=0)
+    w_other_rows = lax.ppermute(w_rows, "dp", partners)
+    mine, w_other_rows = lax.optimization_barrier((mine, w_other_rows))
+    (weight_grads,) = local(
+        weight_kernel,
+        [shaped((width, width), F32)],
+        [jnp.stack([core, plane >> 2, plane & 3]), w_rows, w_other_rows],
+        scalars=1,
+        name="weight",
+    )
+    other = lax.ppermute(mine, "dp", partners)
+    (item_grads,) = local(
+        finish_kernel,
+        [shaped((item_count, width), F32)],
+        [core_s, mine, other, item_rows],
+        scalars=1,
+        name="finish",
+    )
     return (grad_tokens, weight_grads, item_grads)
 
 

time: 245 us -> 233 us (0.951)
  blocking collectives: 83.2 us -> 49.1 us
  starting transfers between devices: 36.7 us -> 57.1 us
  matrix products: 24.4 us -> 14.1 us
  waiting for transfers between devices: 57.4 us -> 60.7 us
  Pallas kernels: 28.7 us -> 31.8 us
  other arithmetic: 5.47 us -> 8.56 us
    all_to_all x2, blocking collectives: 83.2 us -> 49.1 us  [exchange(): lax.all_to_all(pieces, axis, split_axis=0, concat_axis=0, tiled=True, axi...]
    ppermute x1 -> x8, starting transfers between devices: 5.87 us -> 28.8 us  [the longest x6 15.6 us: turned(): return lax.ppermute(rows, 'shard', moves)]
    dot_general x11 -> x10, matrix products: 24.4 us -> 14.1 us  [dot(): return lax.dot_general(a, b, (contract, batch), preferred_element_type=F32)]
    ppermute x1 -> x8, waiting for transfers between devices: 0.01 us -> 9.28 us  [the longest x6 8.13 us: turned(): return lax.ppermute(rows, 'shard', moves)]
    ppermute x1, starting transfers between devices: 8.65 us -> 2.28 us  [shards(): other = lax.ppermute(mine, 'dp', partners)]
    all_to_all x4, waiting for transfers between devices: 55.7 us -> 49.6 us  [exchange(): lax.all_to_all(pieces, axis, split_axis=0, concat_axis=0, tiled=True, axi...]
    all_to_all x4, starting transfers between devices: 18.5 us -> 22.5 us  [exchange(): lax.all_to_all(pieces, axis, split_axis=0, concat_axis=0, tiled=True, axi...]
    pallas_call x8 -> x9, Pallas kernels: 28.7 us -> 31.8 us  [local(): pl.pallas_call(kernel, out_shape=tuple(outs), in_specs=[pl.BlockSpec(memo...]
  transfers between devices with their start and end apart: 7 -> 14, of which waited for: 5 -> 7; matrix products, arithmetic and copies ran while one was open for 12% -> 11% of each run, Pallas kernels for 3% -> 3%
where the time goes in v3:
time: 233 us; the launch traced here: 232 us
  waiting for transfers between devices  60.7 us (26%)
  starting transfers between devices  57.1 us (25%)
  blocking collectives  49.1 us (21%)
  Pallas kernels  31.8 us (14%)
  matrix products  14.1 us (6%)
  local copies, waits for them, and re-layouts  9.21 us (4%)
  other arithmetic  8.56 us (4%)
    all_to_all x4, waiting for transfers between devices, exchange(): lax.all_to_all(pieces, axis, split_axis=0, concat_axis=0, tiled=True, axi...  49.6 us
    all_to_all x2, blocking collectives, exchange(): lax.all_to_all(pieces, axis, split_axis=0, concat_axis=0, tiled=True, axi...  49.1 us
    pallas_call x9, Pallas kernels, local(): pl.pallas_call(kernel, out_shape=tuple(outs), in_specs=[pl.BlockSpec(memo...  31.8 us
    all_to_all x4, starting transfers between devices, exchange(): lax.all_to_all(pieces, axis, split_axis=0, concat_axis=0, tiled=True, axi...  22.5 us
    ppermute x6, starting transfers between devices, turned(): return lax.ppermute(rows, 'shard', moves)  15.6 us
    dot_general x10, matrix products, dot(): return lax.dot_general(a, b, (contract, batch), preferred_element_type=F32)  14.1 us
    ppermute x6, waiting for transfers between devices, turned(): return lax.ppermute(rows, 'shard', moves)  8.13 us
    ppermute x1, starting transfers between devices, shards(): first_other = lax.ppermute(first_in, 'dp', partners)  6.83 us
  transfers between devices with their start and end apart: 14, of which 7 were waited for; matrix products, arithmetic and copies ran while one was open for 11% of the time, Pallas kernels for 3%

profile of v3, /device:TPU:1, one launch (start us, length us, event | category | flops | bytes accessed | tf_op | source)
XLA Modules:
  0.0 231.6 jit_solution(12330621342458062572)
XLA Ops:
  0.7 0.8 reduce
  2.7 3.8 %route.1 = (bf16[16,400,128]{2,1,0:T(8,128)(2,1)}, s32[384,1]{1,0:T(8,128)}) custom-call(s32[1]{0:T(128)} %bitcast.core_ref, s32[1,832]{1,0:T(1,128)} %reshape.112.index_ref, bf16[512,128]{1,0:T(8,128)(2,1)} %w_ref.1, bf16[1024,512]{1,0:T(8,128)(2,1)} %items_ref.3), custom_call_target="tpu_custom_call" | custom-call | bytes 2822916 | tf_op jit(solution)/shard_map/route/pallas_call | solution.py:262
  6.5 7.6 %all-to-all-start = ((bf16[16,400,128]{2,1,0:T(8,128)(2,1)}), bf16[16,400,128]{2,1,0:T(8,128)(2,1)S(1)}, u32[]{:S(2)}, u32[]{:S(2)}) async-start(bf16[16,400,128]{2,1,0:T(8,128)(2,1)} %get-tuple-element.18), calls=%async_computation | async-start | bytes 3276800 | tf_op jit(solution)/shard_map/all_to_all | solution.py:62
  14.3 20.3 %all-to-all-done.recv_ref.mine_ref = bf16[16,400,128]{2,1,0:T(8,128)(2,1)S(1)} async-done(((bf16[16,400,128]{2,1,0:T(8,128)(2,1)}), bf16[16,400,128]{2,1,0:T(8,128)(2,1)S(1)}, u32[]{:S(2)}, u32[]{:S(2)}) %all-to-all-start) | async-done | bytes 1638432 | tf_op jit(solution)/shard_map/all_to_all | solution.py:62
  34.6 6.8 %collective-permute-start = (bf16[16,400,128]{2,1,0:T(8,128)(2,1)S(1)}, bf16[16,400,128]{2,1,0:T(8,128)(2,1)}, u32[]{:S(2)}, u32[]{:S(2)}) collective-permute-start(bf16[16,400,128]{2,1,0:T(8,128)(2,1)S(1)} %all-to-all-done.recv_ref.mine_ref), channel_id=1, source_target_pairs={{0,16},{16,0},{32,48},{48,32},{64,80},{80,64},{96,112},{112,96},{1... | collective-permute-start | bytes 4915208 | tf_op jit(solution)/shard_map/ppermute | solution.py:306
  41.5 1.2 fusion.11
  43.1 1.9 fusion.12
  45.0 1.3 fusion.4.items_ref
  46.2 4.0 %serve.1 = (bf16[16,48,512]{2,1,0:T(8,128)(2,1)}, bf16[768,1024]{1,0:T(8,128)(2,1)}) custom-call(bf16[16,400,128]{2,1,0:T(8,128)(2,1)} %copy-done.1, bf16[1024,512]{1,0:T(8,128)(2,1)} %fusion.4.items_ref), custom_call_target="tpu_custom_call" | custom-call | bytes 5046272 | tf_op jit(solution)/shard_map/serve/pallas_call | solution.py:262
  50.3 4.3 %all-to-all-start.1 = ((bf16[16,48,512]{2,1,0:T(8,128)(2,1)}), bf16[16,48,512]{2,1,0:T(8,128)(2,1)}, u32[]{:S(2)}, u32[]{:S(2)}) async-start(bf16[16,48,512]{2,1,0:T(8,128)(2,1)} %get-tuple-element.19), calls=%async_computation.1 | async-start | bytes 1572864 | tf_op jit(solution)/shard_map/all_to_all | solution.py:62
  54.6 1.4 slice.29
  56.0 1.7 slice.30
  57.7 3.2 %multiply_convert_fusion = (bf16[16,384,128]{2,1,0:T(8,128)(2,1)S(1)}, f32[16,384,128]{2,1,0:T(8,128)}) fusion(bf16[16,256,128]{2,1,0:T(8,128)(2,1)S(1)} %slice.30, bf16[16,256,128]{2,1,0:T(8,128)(2,1)S(1)} %slice.29, pred[]{:T(512)S(6)} %eq.23, bf16[384,512]{1,0:T(8,128)(2,1)S(1)} %copy-done.20), kind=kOutput, calls=%fused_computation.2 | convolution fusion | flops 818675712 | bytes 7208961 | tf_op jit(solution)/shard_map/dot_general | solution.py:36
  60.9 2.5 %select_convert_fusion.1 = (bf16[4,384,384]{2,1,0:T(8,128)(2,1)S(1)}, f32[4,384,384]{2,1,0:T(8,128)}) fusion(pred[384,384]{1,0:T(8,128)(4,1)S(1)} %fusion.26, bf16[16,384,128]{2,1,0:T(8,128)(2,1)S(1)} %get-tuple-element.47), kind=kOutput, calls=%fused_computation.9 | convolution fusion | flops 155713536 | bytes 5652480 | tf_op jit(solution)/shard_map/dot_general | solution.py:36
  64.7 1.3 convert_add_fusion.layer_ref
  65.9 3.4 %all-to-all-done.1.recv_ref = bf16[16,48,512]{2,1,0:T(8,128)(2,1)} async-done(((bf16[16,48,512]{2,1,0:T(8,128)(2,1)}), bf16[16,48,512]{2,1,0:T(8,128)(2,1)}, u32[]{:S(2)}, u32[]{:S(2)}) %all-to-all-start.1) | async-done | bytes 786464 | tf_op jit(solution)/shard_map/all_to_all | solution.py:62
  69.4 8.1 %loss.1 = (bf16[16,144,512]{2,1,0:T(8,128)(2,1)}, f32[384,512]{1,0:T(8,128)}, bf16[384,512]{1,0:T(8,128)(2,1)}) custom-call(s32[1]{0:T(128)} %bitcast.core_ref, f32[384,512]{1,0:T(8,128)} %convert_add_fusion.layer_ref, bf16[4,384,128]{2,1,0:T(8,128)(2,1)} %copy-done.5, bf16[16,48,512]{2,1,0:T(8,128)(2,1)} %all-to-all-done.1.recv_ref, ...), custom_call_target="tpu_custom_call" | custom-call | bytes 8783364 | tf_op jit(solution)/shard_map/loss/pallas_call | solution.py:262
  77.5 3.9 %all-to-all-start.2 = ((bf16[16,144,512]{2,1,0:T(8,128)(2,1)}), bf16[16,144,512]{2,1,0:T(8,128)(2,1)S(1)}, u32[]{:S(2)}, u32[]{:S(2)}) async-start(bf16[16,144,512]{2,1,0:T(8,128)(2,1)} %get-tuple-element.21), calls=%async_computation.2 | async-start | bytes 4718592 | tf_op jit(solution)/shard_map/all_to_all | solution.py:62
  81.4 2.0 fusion.23
  84.0 1.4 select_convert_fusion
  88.1 1.6 fusion.17
  89.7 1.0 fusion.16
  90.7 25.9 %all-to-all-done.2.recv_ref = bf16[16,144,512]{2,1,0:T(8,128)(2,1)S(1)} async-done(((bf16[16,144,512]{2,1,0:T(8,128)(2,1)}), bf16[16,144,512]{2,1,0:T(8,128)(2,1)S(1)}, u32[]{:S(2)}, u32[]{:S(2)}) %all-to-all-start.2) | async-done | bytes 2359328 | tf_op jit(solution)/shard_map/all_to_all | solution.py:62
  116.6 1.4 copy-done.3
  118.0 4.3 %collect.1 = (bf16[528,512]{1,0:T(8,128)(2,1)}, bf16[528,512]{1,0:T(8,128)(2,1)}) custom-call(s32[1]{0:T(128)} %bitcast.core_ref, bf16[16,144,512]{2,1,0:T(8,128)(2,1)} %copy-done.3, bf16[768,1024]{1,0:T(8,128)(2,1)} %get-tuple-element.26.pick_ref, s32[1,64]{1,0:T(1,128)} %bitcast.26), custom_call_target="tpu_custom_call" | custom-call | bytes 5013764 | tf_op jit(solution)/shard_map/collect/pallas_call | solution.py:262
  122.4 3.6 %collective-permute-start.1 = (bf16[528,512]{1,0:T(8,128)(2,1)}, bf16[528,512]{1,0:T(8,128)(2,1)S(1)}, u32[]{:S(2)}, u32[]{:S(2)}) collective-permute-start(bf16[528,512]{1,0:T(8,128)(2,1)} %get-tuple-element.28), channel_id=1, source_target_pairs={{0,16},{16,0},{32,48},{48,32},{64,80},{80,64},{96,112},{112,96},{1... | collective-permute-start | bytes 1622024 | tf_op jit(solution)/shard_map/ppermute | solution.py:409
  126.0 1.7 collective-permute-done.1.other_ref
  127.7 0.8 copy-done.18
  128.5 2.1 near.1
  130.7 21.9 %all_to_all.30.recv_ref = bf16[4,144,512]{2,1,0:T(8,128)(2,1)} all-to-all(bf16[4,144,512]{2,1,0:T(8,128)(2,1)} %near.1), channel_id=1, replica_groups={{0,32,64,96},{16,48,80,112},{128,160,192,224},{144,176,208,240},{256,28..., dimensions={0} | all-to-all | bytes 1179648 | tf_op jit(solution)/shard_map/all_to_all | solution.py:62
  152.6 1.8 far.1
  154.4 27.2 %all_to_all.31.recv_ref = bf16[4,48,512]{2,1,0:T(8,128)(2,1)} all-to-all(bf16[4,48,512]{2,1,0:T(8,128)(2,1)} %far.1), channel_id=1, replica_groups={{0,128,256,384},{16,144,272,400},{32,160,288,416},{48,176,304,432},{64,..., dimensions={0} | all-to-all | bytes 393216 | tf_op jit(solution)/shard_map/all_to_all | solution.py:62
  181.6 1.8 total.1
  183.4 6.7 %all-to-all-start.5 = ((bf16[16,32,512]{2,1,0:T(8,128)(2,1)}), bf16[16,32,512]{2,1,0:T(8,128)(2,1)S(1)}, u32[]{:S(2)}, u32[]{:S(2)}) async-start(bf16[16,32,512]{2,1,0:T(8,128)(2,1)} %get-tuple-element.30), calls=%async_computation.5 | async-start | bytes 1048576 | tf_op jit(solution)/shard_map/all_to_all | solution.py:62
  190.1 1.9 collective-permute-start.4
  192.0 1.9 collective-permute-start.3
  193.9 3.4 %collective-permute-start.2 = (bf16[16,512]{1,0:T(8,128)(2,1)}, bf16[16,512]{1,0:T(8,128)(2,1)S(1)}, u32[]{:S(2)}, u32[]{:S(2)}) collective-permute-start(bf16[16,512]{1,0:T(8,128)(2,1)} %get-tuple-element.29), channel_id=1, source_target_pairs={{0,1},{1,2},{2,3},{3,0},{4,5},{5,6},{6,7},{7,4},{8,9},{9,10},{10,1... | collective-permute-start | bytes 49160 | tf_op jit(solution)/shard_map/ppermute | solution.py:434
  198.0 3.3 %collective-permute-done.2 = bf16[16,512]{1,0:T(8,128)(2,1)S(1)} collective-permute-done((bf16[16,512]{1,0:T(8,128)(2,1)}, bf16[16,512]{1,0:T(8,128)(2,1)S(1)}, u32[]{:S(2)}, u32[]{:S(2)}) %collective-permute-start.2) | collective-permute-done | bytes 16416 | tf_op jit(solution)/shard_map/ppermute | solution.py:434
  201.3 1.9 collective-permute-start.5
  203.3 4.6 %collective-permute-start.7 = (bf16[64,512]{1,0:T(8,128)(2,1)S(1)}, bf16[64,512]{1,0:T(8,128)(2,1)S(1)}, u32[]{:S(2)}, u32[]{:S(2)}) collective-permute-start(bf16[64,512]{1,0:T(8,128)(2,1)S(1)} %get-tuple-element.35), channel_id=1, source_target_pairs={{0,12},{1,13},{2,14},{3,15},{4,0},{5,1},{6,2},{7,3},{8,4},{9,5},{1... | collective-permute-start | bytes 196616 | tf_op jit(solution)/shard_map/ppermute | solution.py:434
  207.9 1.9 collective-permute-start.6
  209.8 4.9 %collective-permute-done.6 = bf16[64,512]{1,0:T(8,128)(2,1)S(1)} collective-permute-done((bf16[64,512]{1,0:T(8,128)(2,1)S(1)}, bf16[64,512]{1,0:T(8,128)(2,1)S(1)}, u32[]{:S(2)}, u32[]{:S(2)}) %collective-permute-start.6) | collective-permute-done | bytes 65568 | tf_op jit(solution)/shard_map/ppermute | solution.py:434
  214.7 6.3 %collective-permute-start.8 = (bf16[256,512]{1,0:T(8,128)(2,1)S(1)}, bf16[256,512]{1,0:T(8,128)(2,1)S(1)}, u32[]{:S(2)}, u32[]{:S(2)}) collective-permute-start(bf16[256,512]{1,0:T(8,128)(2,1)S(1)} %constant_dynamic-update-slice_fusion.4.mine_ref), channel_id=1, source_target_pairs={{0,16},{16,0},{32,48},{48,32},{64,80},{80,64},{96,112},{112,96},{1... | collective-permute-start | bytes 786440 | tf_op jit(solution)/shard_map/ppermute | solution.py:438
  221.0 1.1 collective-permute-done.8.other_ref
  222.2 2.3 collective-permute-start.9
  225.0 2.1 weight.1
  227.2 0.8 copy-done.19
  228.0 3.7 %finish.1 = f32[1024,512]{1,0:T(8,128)} custom-call(s32[1]{0:T(128)} %bitcast.core_ref, bf16[16,32,512]{2,1,0:T(8,128)(2,1)} %copy-done.6, bf16[16,32,512]{2,1,0:T(8,128)(2,1)} %copy-done.19, bf16[1024,512]{1,0:T(8,128)(2,1)} %items_ref.3), custom_call_target="tpu_custom_call" | custom-call | bytes 4194308 | tf_op jit(solution)/shard_map/finish/pallas_call | solution.py:262
  (82 shorter events, 7.8 us)
Async XLA Ops:
  0.6 64.0 %copy-start = (bf16[512,512]{1,0:T(8,128)(2,1)S(1)}, bf16[512,512]{1,0:T(8,128)(2,1)}, u32[]{:S(2)}) copy-start(bf16[512,512]{1,0:T(8,128)(2,1)} %param.10) | copy-start | bytes 1572868
  0.6 13.4 %copy-start.23 = (s32[1,4]{1,0:T(1,128)S(1)}, s32[1,4]{1,0:T(1,128)}, u32[]{:S(2)}) copy-start(s32[1,4]{1,0:T(1,128)} %param.12) | copy-start | bytes 52
  2.7 39.9 %copy-start.2 = (bf16[1024,512]{1,0:T(8,128)(2,1)S(1)}, bf16[1024,512]{1,0:T(8,128)(2,1)}, u32[]{:S(2)}) copy-start(bf16[1024,512]{1,0:T(8,128)(2,1)} %items_ref.3) | copy-start | bytes 3145732
  6.5 28.1 %all-to-all-start = ((bf16[16,400,128]{2,1,0:T(8,128)(2,1)}), bf16[16,400,128]{2,1,0:T(8,128)(2,1)S(1)}, u32[]{:S(2)}, u32[]{:S(2)}) async-start(bf16[16,400,128]{2,1,0:T(8,128)(2,1)} %get-tuple-element.18), calls=%async_computation | async-start | bytes 3276800 | tf_op jit(solution)/shard_map/all_to_all | solution.py:62
  34.6 11.7 %copy-start.1 = (bf16[16,400,128]{2,1,0:T(8,128)(2,1)}, bf16[16,400,128]{2,1,0:T(8,128)(2,1)S(1)}, u32[]{:S(2)}) copy-start(bf16[16,400,128]{2,1,0:T(8,128)(2,1)S(1)} %all-to-all-done.recv_ref.mine_ref) | copy-start | bytes 4915204
  34.6 21.4 %collective-permute-start = (bf16[16,400,128]{2,1,0:T(8,128)(2,1)S(1)}, bf16[16,400,128]{2,1,0:T(8,128)(2,1)}, u32[]{:S(2)}, u32[]{:S(2)}) collective-permute-start(bf16[16,400,128]{2,1,0:T(8,128)(2,1)S(1)} %all-to-all-done.recv_ref.mine_ref), channel_id=1, source_target_pairs={{0,16},{16,0},{32,48},{48,32},{64,80},{80,64},{96,112},{112,96},{1... | collective-permute-start | bytes 4915208 | tf_op jit(solution)/shard_map/ppermute | solution.py:306
  50.3 19.1 %all-to-all-start.1 = ((bf16[16,48,512]{2,1,0:T(8,128)(2,1)}), bf16[16,48,512]{2,1,0:T(8,128)(2,1)}, u32[]{:S(2)}, u32[]{:S(2)}) async-start(bf16[16,48,512]{2,1,0:T(8,128)(2,1)} %get-tuple-element.19), calls=%async_computation.1 | async-start | bytes 1572864 | tf_op jit(solution)/shard_map/all_to_all | solution.py:62
  54.6 3.1 %copy-start.20 = (bf16[384,512]{1,0:T(8,128)(2,1)S(1)}, bf16[384,512]{1,0:T(8,128)(2,1)}, u32[]{:S(2)}) copy-start(bf16[384,512]{1,0:T(8,128)(2,1)} %fusion.12) | copy-start | bytes 1179652
  55.9 4.9 %copy-start.13 = (bf16[16,256,128]{2,1,0:T(8,128)(2,1)}, bf16[16,256,128]{2,1,0:T(8,128)(2,1)S(1)}, u32[]{:S(2)}) copy-start(bf16[16,256,128]{2,1,0:T(8,128)(2,1)S(1)} %slice.29) | copy-start | bytes 3145732
  57.7 3.2 %copy-start.15 = (bf16[16,256,128]{2,1,0:T(8,128)(2,1)}, bf16[16,256,128]{2,1,0:T(8,128)(2,1)S(1)}, u32[]{:S(2)}) copy-start(bf16[16,256,128]{2,1,0:T(8,128)(2,1)S(1)} %slice.30) | copy-start | bytes 3145732
  60.9 3.0 %copy-start.7 = (bf16[16,384,128]{2,1,0:T(8,128)(2,1)}, bf16[16,384,128]{2,1,0:T(8,128)(2,1)S(1)}, u32[]{:S(2)}) copy-start(bf16[16,384,128]{2,1,0:T(8,128)(2,1)S(1)} %get-tuple-element.47) | copy-start | bytes 4718596
  63.4 1.3 copy-start.11
  63.4 1.3 copy-start.4
  63.9 0.8 copy-start.9
  64.7 4.7 %copy-start.5 = (bf16[4,384,128]{2,1,0:T(8,128)(2,1)}, bf16[4,384,128]{2,1,0:T(8,128)(2,1)S(1)}, u32[]{:S(2)}) copy-start(bf16[4,384,128]{2,1,0:T(8,128)(2,1)S(1)} %fusion.10.gated_ref) | copy-start | bytes 1179652
  77.5 39.1 %all-to-all-start.2 = ((bf16[16,144,512]{2,1,0:T(8,128)(2,1)}), bf16[16,144,512]{2,1,0:T(8,128)(2,1)S(1)}, u32[]{:S(2)}, u32[]{:S(2)}) async-start(bf16[16,144,512]{2,1,0:T(8,128)(2,1)} %get-tuple-element.21), calls=%async_computation.2 | async-start | bytes 4718592 | tf_op jit(solution)/shard_map/all_to_all | solution.py:62
  81.4 2.1 copy-start.8
  81.4 2.1 copy-start.10
  81.4 2.6 %copy-start.24 = (f32[4,384,384]{2,1,0:T(8,128)S(1)}, f32[4,384,384]{2,1,0:T(8,128)}, u32[]{:S(2)}) copy-start(f32[4,384,384]{2,1,0:T(8,128)} %get-tuple-element.50) | copy-start | bytes 7077892
  84.0 1.4 copy-start.12
  85.5 1.9 copy-start.25
  86.0 1.7 copy-start.14
  86.0 2.1 copy-start.16
  88.1 1.6 copy-start.17
  116.6 1.4 copy-start.3
  122.4 5.3 %collective-permute-start.1 = (bf16[528,512]{1,0:T(8,128)(2,1)}, bf16[528,512]{1,0:T(8,128)(2,1)S(1)}, u32[]{:S(2)}, u32[]{:S(2)}) collective-permute-start(bf16[528,512]{1,0:T(8,128)(2,1)} %get-tuple-element.28), channel_id=1, source_target_pairs={{0,16},{16,0},{32,48},{48,32},{64,80},{80,64},{96,112},{112,96},{1... | collective-permute-start | bytes 1622024 | tf_op jit(solution)/shard_map/ppermute | solution.py:409
  127.7 0.8 copy-start.18
  183.4 38.8 %all-to-all-start.5 = ((bf16[16,32,512]{2,1,0:T(8,128)(2,1)}), bf16[16,32,512]{2,1,0:T(8,128)(2,1)S(1)}, u32[]{:S(2)}, u32[]{:S(2)}) async-start(bf16[16,32,512]{2,1,0:T(8,128)(2,1)} %get-tuple-element.30), calls=%async_computation.5 | async-start | bytes 1048576 | tf_op jit(solution)/shard_map/all_to_all | solution.py:62
  190.1 11.2 %collective-permute-start.4 = (bf16[16,512]{1,0:T(8,128)(2,1)}, bf16[16,512]{1,0:T(8,128)(2,1)S(1)}, u32[]{:S(2)}, u32[]{:S(2)}) collective-permute-start(bf16[16,512]{1,0:T(8,128)(2,1)} %get-tuple-element.29), channel_id=1, source_target_pairs={{0,3},{1,0},{2,1},{3,2},{4,7},{5,4},{6,5},{7,6},{8,11},{9,8},{10,9... | collective-permute-start | bytes 49160 | tf_op jit(solution)/shard_map/ppermute | solution.py:434
  192.0 9.3 %collective-permute-start.3 = (bf16[16,512]{1,0:T(8,128)(2,1)}, bf16[16,512]{1,0:T(8,128)(2,1)S(1)}, u32[]{:S(2)}, u32[]{:S(2)}) collective-permute-start(bf16[16,512]{1,0:T(8,128)(2,1)} %get-tuple-element.29), channel_id=1, source_target_pairs={{0,2},{1,3},{2,0},{3,1},{4,6},{5,7},{6,4},{7,5},{8,10},{9,11},{10,... | collective-permute-start | bytes 49160 | tf_op jit(solution)/shard_map/ppermute | solution.py:434
  193.9 7.4 %collective-permute-start.2 = (bf16[16,512]{1,0:T(8,128)(2,1)}, bf16[16,512]{1,0:T(8,128)(2,1)S(1)}, u32[]{:S(2)}, u32[]{:S(2)}) collective-permute-start(bf16[16,512]{1,0:T(8,128)(2,1)} %get-tuple-element.29), channel_id=1, source_target_pairs={{0,1},{1,2},{2,3},{3,0},{4,5},{5,6},{6,7},{7,4},{8,9},{9,10},{10,1... | collective-permute-start | bytes 49160 | tf_op jit(solution)/shard_map/ppermute | solution.py:434
  201.3 8.4 %collective-permute-start.5 = (bf16[64,512]{1,0:T(8,128)(2,1)S(1)}, bf16[64,512]{1,0:T(8,128)(2,1)S(1)}, u32[]{:S(2)}, u32[]{:S(2)}) collective-permute-start(bf16[64,512]{1,0:T(8,128)(2,1)S(1)} %get-tuple-element.35), channel_id=1, source_target_pairs={{0,4},{1,5},{2,6},{3,7},{4,8},{5,9},{6,10},{7,11},{8,12},{9,13},{1... | collective-permute-start | bytes 196616 | tf_op jit(solution)/shard_map/ppermute | solution.py:434
  203.3 11.4 %collective-permute-start.7 = (bf16[64,512]{1,0:T(8,128)(2,1)S(1)}, bf16[64,512]{1,0:T(8,128)(2,1)S(1)}, u32[]{:S(2)}, u32[]{:S(2)}) collective-permute-start(bf16[64,512]{1,0:T(8,128)(2,1)S(1)} %get-tuple-element.35), channel_id=1, source_target_pairs={{0,12},{1,13},{2,14},{3,15},{4,0},{5,1},{6,2},{7,3},{8,4},{9,5},{1... | collective-permute-start | bytes 196616 | tf_op jit(solution)/shard_map/ppermute | solution.py:434
  207.9 6.8 %collective-permute-start.6 = (bf16[64,512]{1,0:T(8,128)(2,1)S(1)}, bf16[64,512]{1,0:T(8,128)(2,1)S(1)}, u32[]{:S(2)}, u32[]{:S(2)}) collective-permute-start(bf16[64,512]{1,0:T(8,128)(2,1)S(1)} %get-tuple-element.35), channel_id=1, source_target_pairs={{0,8},{1,9},{2,10},{3,11},{4,12},{5,13},{6,14},{7,15},{8,0},{9,1},... | collective-permute-start | bytes 196616 | tf_op jit(solution)/shard_map/ppermute | solution.py:434
  214.7 10.3 %copy-start.21 = (bf16[256,512]{1,0:T(8,128)(2,1)}, bf16[256,512]{1,0:T(8,128)(2,1)S(1)}, u32[]{:S(2)}) copy-start(bf16[256,512]{1,0:T(8,128)(2,1)S(1)} %constant_dynamic-update-slice_fusion.4.mine_ref) | copy-start | bytes 786436
  214.7 7.5 %collective-permute-start.8 = (bf16[256,512]{1,0:T(8,128)(2,1)S(1)}, bf16[256,512]{1,0:T(8,128)(2,1)S(1)}, u32[]{:S(2)}, u32[]{:S(2)}) collective-permute-start(bf16[256,512]{1,0:T(8,128)(2,1)S(1)} %constant_dynamic-update-slice_fusion.4.mine_ref), channel_id=1, source_target_pairs={{0,16},{16,0},{32,48},{48,32},{64,80},{80,64},{96,112},{112,96},{1... | collective-permute-start | bytes 786440 | tf_op jit(solution)/shard_map/ppermute | solution.py:438
  222.2 2.9 %copy-start.22 = (bf16[256,512]{1,0:T(8,128)(2,1)}, bf16[256,512]{1,0:T(8,128)(2,1)S(1)}, u32[]{:S(2)}) copy-start(bf16[256,512]{1,0:T(8,128)(2,1)S(1)} %collective-permute-done.8.other_ref) | copy-start | bytes 786436
  222.2 5.0 %copy-start.6 = (bf16[16,32,512]{2,1,0:T(8,128)(2,1)}, bf16[16,32,512]{2,1,0:T(8,128)(2,1)S(1)}, u32[]{:S(2)}) copy-start(bf16[16,32,512]{2,1,0:T(8,128)(2,1)S(1)} %all-to-all-done.5.mine_ref) | copy-start | bytes 1572868
  222.2 5.0 %collective-permute-start.9 = (bf16[16,32,512]{2,1,0:T(8,128)(2,1)S(1)}, bf16[16,32,512]{2,1,0:T(8,128)(2,1)S(1)}, u32[]{:S(2)}, u32[]{:S(2)}) collective-permute-start(bf16[16,32,512]{2,1,0:T(8,128)(2,1)S(1)} %all-to-all-done.5.mine_ref), channel_id=1, source_target_pairs={{0,16},{16,0},{32,48},{48,32},{64,80},{80,64},{96,112},{112,96},{1... | collective-permute-start | bytes 1572872 | tf_op jit(solution)/shard_map/ppermute | solution.py:447
  227.2 0.8 copy-start.19

commit v4 on v3

--- a/solution.py
+++ b/solution.py
@@ -112,6 +112,81 @@
         served = served.astype(BF16)
         for i in range(step):
             out_ref[j + i] = served[i * CAP : (i + 1) * CAP]
+
+
+def normalize(tokens_ref, normed_ref):
+    step = 128
+    for c in range(0, tokens_ref.shape[0], step):
+        wide = tokens_ref[c : c + step, :].astype(F32)
+        scale = lax.rsqrt(jnp.mean(wide * wide, axis=1, keepdims=True) + epsilon)
+        normed_ref[c : c + step, :] = (wide * scale).astype(BF16)
+
+
+def norm_kernel(tokens_ref, after_ref, normed_ref):
+    normalize(tokens_ref, normed_ref)
+
+
+def forward_kernel(
+    core_ref,
+    lengths_ref,
+    tokens_ref,
+    mine_ref,
+    other_ref,
+    w_out_ref,
+    layer_ref,
+    gated_ref,
+    w_all_ref,
+    normed,
+    act,
+):
+    tok, width = tokens_ref.shape
+    core = core_ref[0]
+    half = width // 2
+    step = 128
+    normalize(tokens_ref, normed)
+    left = normed[:, pl.ds(pl.multiple_of(core * half, half), half)]
+    right = normed[:, pl.ds(pl.multiple_of((1 - core) * half, half), half)]
+    for ref, part in ((mine_ref, core), (other_ref, 1 - core)):
+        at = pl.multiple_of(part * half, half)
+        for j in range(SECTIONS):
+            w_all_ref[j, pl.ds(at, half), :] = ref[j, 0:half, :]
+    for j in range(0, SECTIONS, 2):
+        w_left = jnp.concatenate([mine_ref[j, 0:half, :], mine_ref[j + 1, 0:half, :]], axis=1)
+        w_right = jnp.concatenate([other_ref[j, 0:half, :], other_ref[j + 1, 0:half, :]], axis=1)
+        pre = dot(left, w_left, ((1,), (0,))) + dot(right, w_right, ((1,), (0,)))
+        pair = (pre * jax.nn.sigmoid(pre)).astype(BF16)
+        act[j] = pair[:, 0:DH]
+        act[j + 1] = pair[:, DH:]
+    end_0 = lengths_ref[0, 0]
+    end_1 = end_0 + lengths_ref[0, 1]
+    end_2 = end_1 + lengths_ref[0, 2]
+    for c in range(0, tok, step):
+        seen = c + step
+        row = iota((step, 1), 0) + c
+        start = jnp.where(row >= end_0, end_0, 0)
+        start = jnp.where(row >= end_1, end_1, start)
+        start = jnp.where(row >= end_2, end_2, start)
+        col = iota((step, seen), 1)
+        visible = (col <= row) & (col >= start)
+        heads = []
+        total = jnp.zeros((step, 1), F32)
+        for h in range(HEADS):
+            values = act[HEADS + h, 0:seen, :]
+            queries = act[2 * HEADS + h, c:seen, :]
+            keys = act[3 * HEADS + h, 0:seen, :]
+            scores = dot(queries, keys, ((1,), (1,))) * DH ** (-0.5)
+            silu = scores * jax.nn.sigmoid(scores) * (1.0 / MAXLEN)
+            weights = jnp.where(visible, silu, 0.0).astype(BF16)
+            joined = dot(weights, values, ((1,), (0,))).astype(BF16).astype(F32)
+            total = total + jnp.sum(joined * joined, axis=1, keepdims=True)
+            heads.append(joined)
+        scale = lax.rsqrt(total * (1.0 / width) + epsilon)
+        out = tokens_ref[c:seen, :].astype(F32)
+        for h in range(HEADS):
+            gated = (heads[h] * scale * act[h, c:seen, :].astype(F32)).astype(BF16)
+            gated_ref[h, c:seen, :] = gated
+            out = out + dot(gated, w_out_ref[h * DH : (h + 1) * DH, :], ((1,), (0,)))
+        layer_ref[c:seen, :] = out
 
 
 def loss_kernel(
@@ -176,8 +251,21 @@
             out_ref[j + i, CAP + NEG :, :] = weights[i * WROWS : (i + 1) * WROWS]
 
 
-def collect_kernel(core_ref, recv_ref, pick_ref, neg_row_ref, keep_ref, send_ref, returned):
-    core = core_ref[0]
+def half_sums(half, pick_ref, neg_row_ref, returned, negs, weights, ref):
+    step = 256
+    for b in range(0, HALF, step):
+        first = pl.multiple_of(half * HALF + b, step)
+        here = one_hot(iota((step, NEG), 0) + first == neg_row_ref[...])
+        total = dot(pick_ref[:, pl.ds(first, step)], returned[...], ((0,), (0,)))
+        total = total + dot(here, negs, ((1,), (0,)))
+        ref[b : b + step, :] = total.astype(BF16)
+    part = jnp.where(half == 0, weights[0:SHARED], weights[SHARED:])
+    ref[HALF:, :] = part.astype(BF16)
+
+
+def send_kernel(
+    core_ref, recv_ref, pick_ref, neg_row_ref, send_ref, returned, negs_ref, weights_ref
+):
     negs = jnp.zeros((NEG, D), F32)
     weights = jnp.zeros((WROWS, D), F32)
     for j in range(PLANE):
@@ -185,16 +273,16 @@
         negs = negs + recv_ref[j, CAP : CAP + NEG, :].astype(F32)
         weights = weights + recv_ref[j, CAP + NEG :, :].astype(F32)
     negs = negs.astype(BF16)
-    step = 256
-    for ref, half in ((keep_ref, core), (send_ref, 1 - core)):
-        for b in range(0, HALF, step):
-            first = pl.multiple_of(half * HALF + b, step)
-            here = one_hot(iota((step, NEG), 0) + first == neg_row_ref[...])
-            total = dot(pick_ref[:, pl.ds(first, step)], returned[...], ((0,), (0,)))
-            total = total + dot(here, negs, ((1,), (0,)))
-            ref[b : b + step, :] = total.astype(BF16)
-        part = jnp.where(half == 0, weights[0 : WROWS // 2], weights[WROWS // 2 :])
-        ref[HALF:, :] = part.astype(BF16)
+    negs_ref[...] = negs
+    weights_ref[...] = weights
+    half_sums(1 - core_ref[0], pick_ref, neg_row_ref, returned, negs, weights, send_ref)
+
+
+def keep_kernel(
+    core_ref, pick_ref, neg_row_ref, returned, negs_ref, weights_ref, keep_ref
+):
+    negs, weights = negs_ref[...], weights_ref[...]
+    half_sums(core_ref[0], pick_ref, neg_row_ref, returned, negs, weights, keep_ref)
 
 
 def near_kernel(keep_ref, other_ref, out_ref):
@@ -240,21 +328,42 @@
                 out_ref[pl.ds(at, SHARED), :] = rows * (1.0 / loss_scale)
 
 
-def finish_kernel(core_ref, mine_ref, other_ref, items_ref, out_ref):
-    for ref, half in ((mine_ref, core_ref[0]), (other_ref, 1 - core_ref[0])):
-        for i in range(CHIPS):
-            start = (i % NEAR) * (HALF // NEAR) + (i // NEAR) * PIECE
-            first = pl.multiple_of(half * HALF + start, PIECE)
-            rows = items_ref[pl.ds(first, PIECE), :].astype(F32)
-            grads = ref[i].astype(F32)
-            scale = lax.rsqrt(jnp.sum(rows * rows, axis=1, keepdims=True) + epsilon)
-            along = jnp.sum(rows * grads, axis=1, keepdims=True)
-            out_ref[pl.ds(first, PIECE), :] = (
-                scale * grads - rows * (scale**3 * along)
-            ) * (1.0 / loss_scale)
-
-
-def local(kernel, outs, operands, scalars=0, scratch=(), flops=0, name=None):
+def finish_kernel(half_ref, grads_ref, items_ref, *rest):
+    out_ref = rest[-1]
+    for i in range(CHIPS):
+        first = (i % NEAR) * (HALF // NEAR) + (i // NEAR) * PIECE
+        rows = items_ref[first : first + PIECE, :].astype(F32)
+        grads = grads_ref[i].astype(F32)
+        scale = lax.rsqrt(jnp.sum(rows * rows, axis=1, keepdims=True) + epsilon)
+        along = jnp.sum(rows * grads, axis=1, keepdims=True)
+        out_ref[first : first + PIECE, :] = (scale * grads - rows * (scale**3 * along)) * (
+            1.0 / loss_scale
+        )
+
+
+def finish(half, grads, items, earlier=None):
+    count, width = items.shape
+    half_block = pl.BlockSpec((HALF, width), lambda i, half_ref: (half_ref[0], 0))
+    operands = [half.reshape(1), grads, items]
+    in_specs = [pl.BlockSpec((CHIPS, PIECE, width), lambda i, half_ref: (0, 0, 0)), half_block]
+    aliases = {}
+    if earlier is not None:
+        operands.append(earlier)
+        in_specs.append(pl.BlockSpec(memory_space=pl.ANY))
+        aliases = {3: 0}
+    return pl.pallas_call(
+        finish_kernel,
+        out_shape=jax.ShapeDtypeStruct((count, width), F32),
+        grid_spec=pltpu.PrefetchScalarGridSpec(
+            num_scalar_prefetch=1, grid=(1,), in_specs=in_specs, out_specs=half_block
+        ),
+        input_output_aliases=aliases,
+        cost_estimate=pl.CostEstimate(flops=0, bytes_accessed=1 << 21, transcendentals=0),
+        name="finish",
+    )(*operands)
+
+
+def local(kernel, outs, operands, scalars=0, scratch=(), flops=0):
     spaces = [pltpu.SMEM] * scalars + [pltpu.VMEM] * (len(operands) - scalars)
     moved = sum(v.size * v.dtype.itemsize for v in operands) + sum(
         v.size * v.dtype.itemsize for v in outs
@@ -267,7 +376,6 @@
         scratch_shapes=list(scratch),
         compiler_params=pltpu.CompilerParams(vmem_limit_bytes=56 * 1024 * 1024),
         cost_estimate=pl.CostEstimate(flops=flops, bytes_accessed=moved, transcendentals=0),
-        name=name,
     )(*operands)
 
 
@@ -300,38 +408,62 @@
         ],
         [core_s, index, w_proj, item_rows],
         scalars=1,
-        name="route",
     )
     first_in = exchange(first_out, "shard")
-    first_other = lax.ppermute(first_in, "dp", partners)
-    w_mine = first_in[:, :half_w]
-    w_other = first_other[:, :half_w]
 
     rows_wide = item_rows.astype(F32)
     item_scale = lax.rsqrt(jnp.sum(rows_wide * rows_wide, axis=1, keepdims=True) + epsilon)
     unit_items = (rows_wide * item_scale).astype(BF16)
+    first_in, unit_items = lax.optimization_barrier((first_in, unit_items))
     served, asked_pick = local(
         serve_kernel,
         [shaped((PLANE, CAP, width)), shaped((slots, item_count))],
         [first_in, unit_items],
-        name="serve",
-    )
+    )
+    served, first_mine = lax.optimization_barrier((served, first_in))
     looked_up = exchange(served, "shard")
-    w_all = jnp.where(
-        core == 0,
-        jnp.concatenate([w_mine, w_other], axis=1),
-        jnp.concatenate([w_other, w_mine], axis=1),
-    )
-
-    w_all = jnp.where(
-        core == 0,
-        jnp.concatenate([w_mine, w_other], axis=1),
-        jnp.concatenate([w_other, w_mine], axis=1),
+    first_other = lax.ppermute(first_mine, "dp", partners)
+    layer_out, gated, w_all = local(
+        forward_kernel,
+        [
+            shaped((tok_rows, width), F32),
+            shaped((HEADS, tok_rows, DH)),
+            shaped((SECTIONS, width, DH)),
+        ],
+        [core_s, lengths, tokens, first_mine, first_other, w_out],
+        scalars=2,
+        scratch=[
+            pltpu.VMEM((tok_rows, width), BF16),
+            pltpu.VMEM((SECTIONS, tok_rows, DH), BF16),
+        ],
+    )
+
+    third_out, grad_out, grad_out_b = local(
+        loss_kernel,
+        [
+            shaped((PLANE, CAP + NEG + WROWS, width)),
+            shaped((tok_rows, width), F32),
+            shaped((tok_rows, width)),
+        ],
+        [core_s, layer_out, gated, looked_up, first_mine, first_other, position],
+        scalars=1,
+        scratch=[
+            pltpu.VMEM((slots, width), BF16),
+            pltpu.VMEM((negs, width), BF16),
+            pltpu.VMEM((tok_rows, negs), BF16),
+            pltpu.VMEM((tok_rows, width), BF16),
+            pltpu.VMEM((tok_rows, width), BF16),
+        ],
+    )
+    third_in = exchange(third_out, "shard")
+
+    (normed,) = local(norm_kernel, [shaped((tok_rows, width))], [tokens, grad_out_b])
+    grad_out_b, w_all, normed, tokens = lax.optimization_barrier(
+        (grad_out_b, w_all, normed, tokens)
     )
     visible = history_mask(lengths[0], tok_rows)[None]
     wide_tokens = tokens.astype(F32)
     input_scale = lax.rsqrt(jnp.mean(wide_tokens * wide_tokens, axis=1, keepdims=True) + epsilon)
-    normed = (wide_tokens * input_scale).astype(BF16)
     normed_s = jnp.broadcast_to(normed[None], (SECTIONS, tok_rows, width))
     pre_act = dot(normed_s, w_all, ((2,), (1,)), ((0,), (0,)))
     activated = jax.nn.silu(pre_act).astype(BF16)
@@ -345,30 +477,7 @@
         jnp.sum(joined_wide * joined_wide, axis=(0, 2), keepdims=True) / width + epsilon
     )
     gate_wide = gate.astype(F32)
-    gated = (joined_wide * middle_scale * gate_wide).astype(BF16)
     w_out_h = w_out.reshape(HEADS, DH, width)
-    layer_out = wide_tokens + jnp.sum(dot(gated, w_out_h, ((2,), (1,)), ((0,), (0,))), axis=0)
-
-    third_out, grad_out, grad_out_b = local(
-        loss_kernel,
-        [
-            shaped((PLANE, CAP + NEG + WROWS, width)),
-            shaped((tok_rows, width), F32),
-            shaped((tok_rows, width)),
-        ],
-        [core_s, layer_out, gated, looked_up, first_in, first_other, position],
-        scalars=1,
-        scratch=[
-            pltpu.VMEM((slots, width), BF16),
-            pltpu.VMEM((negs, width), BF16),
-            pltpu.VMEM((tok_rows, negs), BF16),
-            pltpu.VMEM((tok_rows, width), BF16),
-            pltpu.VMEM((tok_rows, width), BF16),
-        ],
-        name="loss",
-    )
-    third_in = exchange(third_out, "shard")
-
     grad_gated = dot(
         jnp.broadcast_to(grad_out_b[None], (HEADS, tok_rows, width)),
         w_out_h,
@@ -398,32 +507,35 @@
     grad_tokens = (grad_out + grad_input).astype(BF16)
     third_in, grad_tokens = lax.optimization_barrier((third_in, grad_tokens))
 
-    kept, sent = local(
-        collect_kernel,
-        [shaped((HALF + WROWS // 2, width))] * 2,
-        [core_s, third_in, asked_pick, negative_rows.reshape(1, NEG)],
+    neg_row = negative_rows.reshape(1, NEG)
+    sent, returned, neg_sum, w_sum = local(
+        send_kernel,
+        [
+            shaped((HALF + SHARED, width)),
+            shaped((slots, width)),
+            shaped((NEG, width)),
+            shaped((WROWS, width), F32),
+        ],
+        [core_s, third_in, asked_pick, neg_row],
         scalars=1,
-        scratch=[pltpu.VMEM((slots, width), BF16)],
-        name="collect",
     )
     arrived = lax.ppermute(sent, "dp", partners)
+    (kept,) = local(
+        keep_kernel,
+        [shaped((HALF + SHARED, width))],
+        [core_s, asked_pick, neg_row, returned, neg_sum, w_sum],
+        scalars=1,
+    )
     (near_out,) = local(
-        near_kernel,
-        [shaped((NEAR, HALF // NEAR + SHARED, width))],
-        [kept, arrived],
-        name="near",
+        near_kernel, [shaped((NEAR, HALF // NEAR + SHARED, width))], [kept, arrived]
     )
     (far_out,) = local(
-        far_kernel,
-        [shaped((FAR, PIECE + SHARED, width))],
-        [exchange(near_out, "dp", near)],
-        name="far",
+        far_kernel, [shaped((FAR, PIECE + SHARED, width))], [exchange(near_out, "dp", near)]
     )
     summed, w_rows = local(
         total_kernel,
         [shaped((CHIPS, PIECE, width)), shaped((SHARED, width))],
         [exchange(far_out, "dp", far)],
-        name="total",
     )
     mine = exchange(summed, "dp", columns)
 
@@ -436,21 +548,14 @@
     w_rows = jnp.concatenate([w_rows] + [turned(w_rows, 0, k) for k in (1, 2, 3)], axis=0)
     w_rows = jnp.concatenate([w_rows] + [turned(w_rows, k, 0) for k in (1, 2, 3)], axis=0)
     w_other_rows = lax.ppermute(w_rows, "dp", partners)
-    mine, w_other_rows = lax.optimization_barrier((mine, w_other_rows))
+    other = lax.ppermute(mine, "dp", partners)
+    item_grads = finish(1 - core, other, item_rows, finish(core, mine, item_rows))
+    w_rows, w_other_rows, item_grads = lax.optimization_barrier((w_rows, w_other_rows, item_grads))
     (weight_grads,) = local(
         weight_kernel,
         [shaped((width, width), F32)],
         [jnp.stack([core, plane >> 2, plane & 3]), w_rows, w_other_rows],
         scalars=1,
-        name="weight",
-    )
-    other = lax.ppermute(mine, "dp", partners)
-    (item_grads,) = local(
-        finish_kernel,
-        [shaped((item_count, width), F32)],
-        [core_s, mine, other, item_rows],
-        scalars=1,
-        name="finish",
     )
     return (grad_tokens, weight_grads, item_grads)
 
@@ -467,4 +572,6 @@
         P("shard"),
     )
     out_specs = (P(("dp", "shard"), None), P(), P("shard", None))
-    return jax.shard_map(shards, mesh=mesh, in_specs=in_specs, out_specs=out_specs, check_vma=False)
+    return jax.shard_map(
+        shards, mesh=mesh, in_specs=in_specs, out_specs=out_specs, check_vma=False
+    )

time: 233 us -> 245 us (1.052)
  Pallas kernels: 31.8 us -> 45.5 us
  waiting for transfers between devices: 60.7 us -> 55.4 us
  starting transfers between devices: 57.1 us -> 60.9 us
    pallas_call x9 -> x11, Pallas kernels: 31.8 us -> 40.4 us  [local(): pl.pallas_call(kernel, out_shape=tuple(outs), in_specs=[pl.BlockSpec(memo...]
    ppermute x1, starting transfers between devices: 2.28 us -> 9.13 us  [shards(): other = lax.ppermute(mine, 'dp', partners)]
    ppermute x6, waiting for transfers between devices: 8.13 us -> 2.15 us  [turned(): return lax.ppermute(rows, 'shard', moves)]
    pallas_call x0 -> x2, Pallas kernels: none -> 5.14 us  [finish(): pl.pallas_call(finish_kernel, out_shape=jax.ShapeDtypeStruct((count, widt...]
    ppermute x1, starting transfers between devices: 6.32 us -> 1.92 us  [shards(): w_other_rows = lax.ppermute(w_rows, 'dp', partners)]
    all_to_all x4, waiting for transfers between devices: 49.6 us -> 53.3 us  [exchange(): lax.all_to_all(pieces, axis, split_axis=0, concat_axis=0, tiled=True, axi...]
    slice x2 -> x0, local copies, waits for them, and re-layouts: 3.04 us -> none  [the longest x1 1.68 us: shards(): w_other = first_other[:, :half_w]]
    unnamed x57 -> x49, local copies, waits for them, and re-layouts: 5.57 us -> 8.42 us
  transfers between devices with their start and end apart: 14 -> 14, of which waited for: 7 -> 5; matrix products, arithmetic and copies ran while one was open for 11% -> 4% of each run, Pallas kernels for 3% -> 6%
where the time goes in v4:
time: 245 us; the launch traced here: 243 us
  starting transfers between devices  60.9 us (25%)
  waiting for transfers between devices  55.4 us (23%)
  blocking collectives  49.1 us (20%)
  Pallas kernels  45.5 us (19%)
  matrix products  16.1 us (7%)
  local copies, waits for them, and re-layouts  9.02 us (4%)
  other arithmetic  6.21 us (3%)
    all_to_all x4, waiting for transfers between devices, exchange(): lax.all_to_all(pieces, axis, split_axis=0, concat_axis=0, tiled=True, axi...  53.3 us
    all_to_all x2, blocking collectives, exchange(): lax.all_to_all(pieces, axis, split_axis=0, concat_axis=0, tiled=True, axi...  49.1 us
    pallas_call x11, Pallas kernels, local(): pl.pallas_call(kernel, out_shape=tuple(outs), in_specs=[pl.BlockSpec(memo...  40.4 us
    all_to_all x4, starting transfers between devices, exchange(): lax.all_to_all(pieces, axis, split_axis=0, concat_axis=0, tiled=True, axi...  21.7 us
    ppermute x6, starting transfers between devices, turned(): return lax.ppermute(rows, 'shard', moves)  17.7 us
    dot_general x9, matrix products, dot(): return lax.dot_general(a, b, (contract, batch), preferred_element_type=F32)  16.1 us
    ppermute x1, starting transfers between devices, shards(): other = lax.ppermute(mine, 'dp', partners)  9.13 us
    unnamed x49, local copies, waits for them, and re-layouts  8.42 us
  transfers between devices with their start and end apart: 14, of which 5 were waited for; matrix products, arithmetic and copies ran while one was open for 4% of the time, Pallas kernels for 6%

profile of v4, /device:TPU:1, one launch (start us, length us, event | category | flops | bytes accessed | tf_op | source)
XLA Modules:
  0.0 243.5 jit_solution(17278998853983289888)
XLA Ops:
  2.7 3.7 %shard_map.103 = (bf16[16,400,128]{2,1,0:T(8,128)(2,1)}, s32[384,1]{1,0:T(8,128)}) custom-call(s32[1]{0:T(128)} %bitcast.core_ref.half_ref, s32[1,832]{1,0:T(1,128)} %reshape.115.index_ref, bf16[512,128]{1,0:T(8,128)(2,1)} %w_ref.1, bf16[1024,512]{1,0:T(8,128)(2,1)} %items_ref.5), custom_call_target="tpu_custom_call" | custom-call | bytes 2822916 | tf_op jit(solution)/shard_map/pallas_call | solution.py:371
  6.4 7.6 %all-to-all-start = ((bf16[16,400,128]{2,1,0:T(8,128)(2,1)}), bf16[16,400,128]{2,1,0:T(8,128)(2,1)S(1)}, u32[]{:S(2)}, u32[]{:S(2)}) async-start(bf16[16,400,128]{2,1,0:T(8,128)(2,1)} %get-tuple-element.32), calls=%async_computation | async-start | bytes 3276800 | tf_op jit(solution)/shard_map/all_to_all | solution.py:62
  14.3 1.3 fusion.4.items_ref
  15.6 18.9 %all-to-all-done.recv_ref.mine_ref = bf16[16,400,128]{2,1,0:T(8,128)(2,1)S(1)} async-done(((bf16[16,400,128]{2,1,0:T(8,128)(2,1)}), bf16[16,400,128]{2,1,0:T(8,128)(2,1)S(1)}, u32[]{:S(2)}, u32[]{:S(2)}) %all-to-all-start) | async-done | bytes 1638432 | tf_op jit(solution)/shard_map/all_to_all | solution.py:62
  34.5 1.2 copy-done
  35.7 4.0 %shard_map.104 = (bf16[16,48,512]{2,1,0:T(8,128)(2,1)}, bf16[768,1024]{1,0:T(8,128)(2,1)}) custom-call(bf16[16,400,128]{2,1,0:T(8,128)(2,1)} %copy-done, bf16[1024,512]{1,0:T(8,128)(2,1)} %fusion.4.items_ref), custom_call_target="tpu_custom_call" | custom-call | bytes 5046272 | tf_op jit(solution)/shard_map/pallas_call | solution.py:371
  39.7 6.8 %collective-permute-start = (bf16[16,400,128]{2,1,0:T(8,128)(2,1)}, bf16[16,400,128]{2,1,0:T(8,128)(2,1)S(1)}, u32[]{:S(2)}, u32[]{:S(2)}) collective-permute-start(bf16[16,400,128]{2,1,0:T(8,128)(2,1)} %copy-done), channel_id=1, source_target_pairs={{0,16},{16,0},{32,48},{48,32},{64,80},{80,64},{96,112},{112,96},{1... | collective-permute-start | bytes 4915208 | tf_op jit(solution)/shard_map/ppermute | solution.py:425
  46.6 3.8 %all-to-all-start.1 = ((bf16[16,48,512]{2,1,0:T(8,128)(2,1)}), bf16[16,48,512]{2,1,0:T(8,128)(2,1)S(1)}, u32[]{:S(2)}, u32[]{:S(2)}) async-start(bf16[16,48,512]{2,1,0:T(8,128)(2,1)} %get-tuple-element.39), calls=%async_computation.1 | async-start | bytes 1572864 | tf_op jit(solution)/shard_map/all_to_all | solution.py:62
  50.9 1.2 copy-done.3
  52.1 7.5 %shard_map.105 = (f32[384,512]{1,0:T(8,128)}, bf16[4,384,128]{2,1,0:T(8,128)(2,1)}, bf16[16,512,128]{2,1,0:T(8,128)(2,1)}) custom-call(s32[1]{0:T(128)} %bitcast.core_ref.half_ref, s32[1,4]{1,0:T(1,128)} %lengths_ref.1, bf16[384,512]{1,0:T(8,128)(2,1)} %tokens_ref.3, bf16[16,400,128]{2,1,0:T(8,128)(2,1)} %copy-done, bf16[16,400,128]{2,1,0:T(8,128)(2,1)} %copy-done.3, ...), custom_call_target="tpu_custom_call" | custom-call | bytes 7471124 | tf_op jit(solution)/shard_map/pallas_call | solution.py:371
  59.6 5.4 %all-to-all-done.1.recv_ref = bf16[16,48,512]{2,1,0:T(8,128)(2,1)S(1)} async-done(((bf16[16,48,512]{2,1,0:T(8,128)(2,1)}), bf16[16,48,512]{2,1,0:T(8,128)(2,1)S(1)}, u32[]{:S(2)}, u32[]{:S(2)}) %all-to-all-start.1) | async-done | bytes 786464 | tf_op jit(solution)/shard_map/all_to_all | solution.py:62
  64.9 0.9 copy-done.5
  65.8 8.3 %shard_map.106 = (bf16[16,144,512]{2,1,0:T(8,128)(2,1)}, f32[384,512]{1,0:T(8,128)}, bf16[384,512]{1,0:T(8,128)(2,1)}) custom-call(s32[1]{0:T(128)} %bitcast.core_ref.half_ref, f32[384,512]{1,0:T(8,128)} %get-tuple-element.37.layer_ref, bf16[4,384,128]{2,1,0:T(8,128)(2,1)} %get-tuple-element.38.gated_ref, bf16[16,48,512]{2,1,0:T(8,128)(2,1)} %copy-done.5, ...), custom_call_target="tpu_custom_call" | custom-call | bytes 8783364 | tf_op jit(solution)/shard_map/pallas_call | solution.py:371
  74.1 2.0 shard_map.107
  76.1 4.5 %multiply_convert_fusion = (bf16[16,384,128]{1,2,0:T(8,128)(2,1)S(1)}, f32[16,384,128]{1,2,0:T(8,128)}) fusion(bf16[16,512,128]{2,1,0:T(8,128)(2,1)S(1)} %copy-done.20, bf16[384,512]{1,0:T(8,128)(2,1)} %shard_map.107), kind=kOutput, calls=%fused_computation.2 | convolution fusion | flops 809238528 | bytes 7208960 | tf_op jit(solution)/shard_map/dot_general | solution.py:36
  80.6 1.1 select_convert_fusion.1
  83.5 1.2 fusion.16
  84.6 1.3 fusion.35
  86.0 1.5 select_convert_fusion
  87.4 4.0 %all-to-all-start.2 = ((bf16[16,144,512]{2,1,0:T(8,128)(2,1)}), bf16[16,144,512]{2,1,0:T(8,128)(2,1)S(1)}, u32[]{:S(2)}, u32[]{:S(2)}) async-start(bf16[16,144,512]{2,1,0:T(8,128)(2,1)} %get-tuple-element.41), calls=%async_computation.2 | async-start | bytes 4718592 | tf_op jit(solution)/shard_map/all_to_all | solution.py:62
  91.5 1.6 fusion.29
  93.1 1.4 fusion.25
  94.6 3.5 %fusion.10 = (f32[384]{0:T(512)S(1)}, f32[384]{0:T(512)S(1)}, f32[384,512]{1,0:T(8,128)S(1)}) fusion(bf16[384,512]{1,0:T(8,128)(2,1)S(1)} %copy-done.4, bf16[16,512,128]{2,1,0:T(8,128)(2,1)S(1)} %copy-done.21, f32[4,384,128]{1,2,0:T(8,128)S(1)} %fusion.25, f32[4,384,128]{1,2,0:T(8,128)S(1)} %fusion.29, f32[4,384,128]{1,2,0:T(8,128)S(1)} %copy-done.12, ...), kind=kOutput, calls=%fused_computation.23 | convolution fusion | flops 815725824 | bytes 9571328 | tf_op jit(solution)/shard_map/dot_general | solution.py:36
  98.1 1.0 fusion.14
  99.1 27.6 %all-to-all-done.2.recv_ref = bf16[16,144,512]{2,1,0:T(8,128)(2,1)S(1)} async-done(((bf16[16,144,512]{2,1,0:T(8,128)(2,1)}), bf16[16,144,512]{2,1,0:T(8,128)(2,1)S(1)}, u32[]{:S(2)}, u32[]{:S(2)}) %all-to-all-start.2) | async-done | bytes 2359328 | tf_op jit(solution)/shard_map/all_to_all | solution.py:62
  126.8 1.4 copy-done.2
  128.2 3.9 %shard_map.108 = (bf16[528,512]{1,0:T(8,128)(2,1)}, bf16[768,512]{1,0:T(8,128)(2,1)}, bf16[64,512]{1,0:T(8,128)(2,1)}, f32[32,512]{1,0:T(8,128)}) custom-call(s32[1]{0:T(128)} %bitcast.core_ref.half_ref, bf16[16,144,512]{2,1,0:T(8,128)(2,1)} %copy-done.2, bf16[768,1024]{1,0:T(8,128)(2,1)} %get-tuple-element.50.pick_ref, s32[1,64]{1,0:T(1,128)} %bitcast.22), custom_call_target="tpu_custom_call" | custom-call | bytes 5390596 | tf_op jit(solution)/shard_map/pallas_call | solution.py:371
  132.0 3.6 %collective-permute-start.1 = (bf16[528,512]{1,0:T(8,128)(2,1)}, bf16[528,512]{1,0:T(8,128)(2,1)S(1)}, u32[]{:S(2)}, u32[]{:S(2)}) collective-permute-start(bf16[528,512]{1,0:T(8,128)(2,1)} %get-tuple-element.55), channel_id=1, source_target_pairs={{0,16},{16,0},{32,48},{48,32},{64,80},{80,64},{96,112},{112,96},{1... | collective-permute-start | bytes 1622024 | tf_op jit(solution)/shard_map/ppermute | solution.py:522
  135.7 3.2 %shard_map.109.keep_ref = bf16[528,512]{1,0:T(8,128)(2,1)} custom-call(s32[1]{0:T(128)} %bitcast.core_ref.half_ref, bf16[768,1024]{1,0:T(8,128)(2,1)} %get-tuple-element.50.pick_ref, s32[1,64]{1,0:T(1,128)} %bitcast.23, bf16[768,512]{1,0:T(8,128)(2,1)} %get-tuple-element.52.returned, bf16[64,512]{1,0:T(8,128)(2,1)} %get-tuple-element.53.negs_ref, ...), custom_call_target="tpu_custom_call" | custom-call | bytes 3031300 | tf_op jit(solution)/shard_map/pallas_call | solution.py:371
  139.6 2.1 shard_map.110
  141.8 22.0 %all_to_all.30.recv_ref = bf16[4,144,512]{2,1,0:T(8,128)(2,1)} all-to-all(bf16[4,144,512]{2,1,0:T(8,128)(2,1)} %shard_map.110), channel_id=1, replica_groups={{0,32,64,96},{16,48,80,112},{128,160,192,224},{144,176,208,240},{256,28..., dimensions={0} | all-to-all | bytes 1179648 | tf_op jit(solution)/shard_map/all_to_all | solution.py:62
  163.8 1.8 shard_map.111
  165.6 27.1 %all_to_all.31.recv_ref = bf16[4,48,512]{2,1,0:T(8,128)(2,1)} all-to-all(bf16[4,48,512]{2,1,0:T(8,128)(2,1)} %shard_map.111), channel_id=1, replica_groups={{0,128,256,384},{16,144,272,400},{32,160,288,416},{48,176,304,432},{64,..., dimensions={0} | all-to-all | bytes 393216 | tf_op jit(solution)/shard_map/all_to_all | solution.py:62
  192.7 1.8 shard_map.112
  194.5 6.4 %all-to-all-start.5 = ((bf16[16,32,512]{2,1,0:T(8,128)(2,1)}), bf16[16,32,512]{2,1,0:T(8,128)(2,1)S(1)}, u32[]{:S(2)}, u32[]{:S(2)}) async-start(bf16[16,32,512]{2,1,0:T(8,128)(2,1)} %get-tuple-element.57), calls=%async_computation.5 | async-start | bytes 1048576 | tf_op jit(solution)/shard_map/all_to_all | solution.py:62
  200.9 1.9 collective-permute-start.2
  203.6 2.6 %collective-permute-start.3 = (bf16[16,512]{1,0:T(8,128)(2,1)}, bf16[16,512]{1,0:T(8,128)(2,1)S(1)}, u32[]{:S(2)}, u32[]{:S(2)}) collective-permute-start(bf16[16,512]{1,0:T(8,128)(2,1)} %get-tuple-element.56), channel_id=1, source_target_pairs={{0,2},{1,3},{2,0},{3,1},{4,6},{5,7},{6,4},{7,5},{8,10},{9,11},{10,... | collective-permute-start | bytes 49160 | tf_op jit(solution)/shard_map/ppermute | solution.py:546
  206.2 3.9 %collective-permute-start.4 = (bf16[16,512]{1,0:T(8,128)(2,1)}, bf16[16,512]{1,0:T(8,128)(2,1)S(1)}, u32[]{:S(2)}, u32[]{:S(2)}) collective-permute-start(bf16[16,512]{1,0:T(8,128)(2,1)} %get-tuple-element.56), channel_id=1, source_target_pairs={{0,3},{1,0},{2,1},{3,2},{4,7},{5,4},{6,5},{7,6},{8,11},{9,8},{10,9... | collective-permute-start | bytes 49160 | tf_op jit(solution)/shard_map/ppermute | solution.py:546
  210.1 2.1 collective-permute-done.4
  212.2 1.9 collective-permute-start.5
  214.2 4.3 %collective-permute-start.6 = (bf16[64,512]{1,0:T(8,128)(2,1)S(1)}, bf16[64,512]{1,0:T(8,128)(2,1)S(1)}, u32[]{:S(2)}, u32[]{:S(2)}) collective-permute-start(bf16[64,512]{1,0:T(8,128)(2,1)S(1)} %get-tuple-element.67), channel_id=1, source_target_pairs={{0,8},{1,9},{2,10},{3,11},{4,12},{5,13},{6,14},{7,15},{8,0},{9,1},... | collective-permute-start | bytes 196616 | tf_op jit(solution)/shard_map/ppermute | solution.py:546
  218.4 3.1 %collective-permute-start.7 = (bf16[64,512]{1,0:T(8,128)(2,1)S(1)}, bf16[64,512]{1,0:T(8,128)(2,1)S(1)}, u32[]{:S(2)}, u32[]{:S(2)}) collective-permute-start(bf16[64,512]{1,0:T(8,128)(2,1)S(1)} %get-tuple-element.67), channel_id=1, source_target_pairs={{0,12},{1,13},{2,14},{3,15},{4,0},{5,1},{6,2},{7,3},{8,4},{9,5},{1... | collective-permute-start | bytes 196616 | tf_op jit(solution)/shard_map/ppermute | solution.py:546
  221.6 1.3 all-to-all-done.5.grads_ref
  222.9 9.1 %collective-permute-start.9 = (bf16[16,32,512]{2,1,0:T(8,128)(2,1)S(1)}, bf16[16,32,512]{2,1,0:T(8,128)(2,1)S(1)}, u32[]{:S(2)}, u32[]{:S(2)}) collective-permute-start(bf16[16,32,512]{2,1,0:T(8,128)(2,1)S(1)} %all-to-all-done.5.grads_ref), channel_id=1, source_target_pairs={{0,16},{16,0},{32,48},{48,32},{64,80},{80,64},{96,112},{112,96},{1... | collective-permute-start | bytes 1572872 | tf_op jit(solution)/shard_map/ppermute | solution.py:551
  232.1 1.9 collective-permute-start.8
  234.7 2.6 %finish.2.rest_0_ = f32[1024,512]{1,0:T(8,128)} custom-call(s32[1]{0:T(128)} %bitcast.core_ref.half_ref, bf16[16,32,512]{2,1,0:T(8,128)(2,1)} %copy-done.7, bf16[1024,512]{1,0:T(8,128)(2,1)} %items_ref.5), custom_call_target="tpu_custom_call" | custom-call | bytes 2097152 | tf_op jit(solution)/shard_map/finish/pallas_call | solution.py:354
  238.1 2.6 %finish.3 = f32[1024,512]{1,0:T(8,128)} custom-call(s32[1]{0:T(128)} %bitcast.8.half_ref, bf16[16,32,512]{2,1,0:T(8,128)(2,1)} %copy-done.14, bf16[1024,512]{1,0:T(8,128)(2,1)} %items_ref.5, f32[1024,512]{1,0:T(8,128)} %finish.2.rest_0_), custom_call_target="tpu_custom_call", output_to_operand_aliasing={{}: (3, {})} | custom-call | bytes 2097152 | tf_op jit(solution)/shard_map/finish/pallas_call | solution.py:354
  241.3 2.1 shard_map.113
  (71 shorter events, 8.3 us)
Async XLA Ops:
  0.6 13.4 %copy-start.1 = (bf16[1024,512]{1,0:T(8,128)(2,1)S(1)}, bf16[1024,512]{1,0:T(8,128)(2,1)}, u32[]{:S(2)}) copy-start(bf16[1024,512]{1,0:T(8,128)(2,1)} %items_ref.5) | copy-start | bytes 3145732
  6.4 28.1 %all-to-all-start = ((bf16[16,400,128]{2,1,0:T(8,128)(2,1)}), bf16[16,400,128]{2,1,0:T(8,128)(2,1)S(1)}, u32[]{:S(2)}, u32[]{:S(2)}) async-start(bf16[16,400,128]{2,1,0:T(8,128)(2,1)} %get-tuple-element.32), calls=%async_computation | async-start | bytes 3276800 | tf_op jit(solution)/shard_map/all_to_all | solution.py:62
  15.6 34.8 %copy-start.19 = (s32[1,4]{1,0:T(1,128)S(1)}, s32[1,4]{1,0:T(1,128)}, u32[]{:S(2)}) copy-start(s32[1,4]{1,0:T(1,128)} %lengths_ref.1) | copy-start | bytes 52
  34.5 1.2 copy-start
  39.7 11.1 %collective-permute-start = (bf16[16,400,128]{2,1,0:T(8,128)(2,1)}, bf16[16,400,128]{2,1,0:T(8,128)(2,1)S(1)}, u32[]{:S(2)}, u32[]{:S(2)}) collective-permute-start(bf16[16,400,128]{2,1,0:T(8,128)(2,1)} %copy-done), channel_id=1, source_target_pairs={{0,16},{16,0},{32,48},{48,32},{64,80},{80,64},{96,112},{112,96},{1... | collective-permute-start | bytes 4915208 | tf_op jit(solution)/shard_map/ppermute | solution.py:425
  46.6 18.3 %all-to-all-start.1 = ((bf16[16,48,512]{2,1,0:T(8,128)(2,1)}), bf16[16,48,512]{2,1,0:T(8,128)(2,1)S(1)}, u32[]{:S(2)}, u32[]{:S(2)}) async-start(bf16[16,48,512]{2,1,0:T(8,128)(2,1)} %get-tuple-element.39), calls=%async_computation.1 | async-start | bytes 1572864 | tf_op jit(solution)/shard_map/all_to_all | solution.py:62
  50.8 29.8 %copy-start.17 = (pred[384,384]{1,0:T(8,128)(4,1)}, pred[384,384]{1,0:T(8,128)(4,1)S(1)}, u32[]{:S(2)}) copy-start(pred[384,384]{1,0:T(8,128)(4,1)S(1)} %fusion.24) | copy-start | bytes 442372
  50.9 1.2 copy-start.3
  64.9 0.9 copy-start.5
  65.8 10.3 %copy-start.20 = (bf16[16,512,128]{2,1,0:T(8,128)(2,1)S(1)}, bf16[16,512,128]{2,1,0:T(8,128)(2,1)}, u32[]{:S(2)}) copy-start(bf16[16,512,128]{2,1,0:T(8,128)(2,1)} %get-tuple-element.48) | copy-start | bytes 6291460
  80.6 5.4 %copy-start.9 = (bf16[16,384,128]{1,2,0:T(8,128)(2,1)}, bf16[16,384,128]{1,2,0:T(8,128)(2,1)S(1)}, u32[]{:S(2)}) copy-start(bf16[16,384,128]{1,2,0:T(8,128)(2,1)S(1)} %get-tuple-element.79) | copy-start | bytes 4718596
  80.6 1.4 copy-start.6
  80.6 1.7 copy-start.8
  83.5 2.5 %copy-start.18 = (pred[384,384]{1,0:T(8,128)(4,1)S(1)}, pred[384,384]{1,0:T(8,128)(4,1)}, u32[]{:S(2)}) copy-start(pred[384,384]{1,0:T(8,128)(4,1)} %copy-done.17) | copy-start | bytes 442372
  87.4 39.3 %all-to-all-start.2 = ((bf16[16,144,512]{2,1,0:T(8,128)(2,1)}), bf16[16,144,512]{2,1,0:T(8,128)(2,1)S(1)}, u32[]{:S(2)}, u32[]{:S(2)}) async-start(bf16[16,144,512]{2,1,0:T(8,128)(2,1)} %get-tuple-element.41), calls=%async_computation.2 | async-start | bytes 4718592 | tf_op jit(solution)/shard_map/all_to_all | solution.py:62
  91.4 3.1 %copy-start.4 = (bf16[384,512]{1,0:T(8,128)(2,1)S(1)}, bf16[384,512]{1,0:T(8,128)(2,1)}, u32[]{:S(2)}) copy-start(bf16[384,512]{1,0:T(8,128)(2,1)} %tokens_ref.3) | copy-start | bytes 1179652
  91.4 3.1 %copy-start.11 = (f32[4,384,128]{1,2,0:T(8,128)S(1)}, f32[4,384,128]{1,2,0:T(8,128)}, u32[]{:S(2)}) copy-start(f32[4,384,128]{1,2,0:T(8,128)} %get-tuple-element.65) | copy-start | bytes 2359300
  91.4 3.1 %copy-start.12 = (f32[4,384,128]{1,2,0:T(8,128)S(1)}, f32[4,384,128]{1,2,0:T(8,128)}, u32[]{:S(2)}) copy-start(f32[4,384,128]{1,2,0:T(8,128)} %fusion.35) | copy-start | bytes 2359300
  91.4 3.1 %copy-start.21 = (bf16[16,512,128]{2,1,0:T(8,128)(2,1)S(1)}, bf16[16,512,128]{2,1,0:T(8,128)(2,1)}, u32[]{:S(2)}) copy-start(bf16[16,512,128]{2,1,0:T(8,128)(2,1)} %get-tuple-element.48) | copy-start | bytes 6291460
  94.6 3.6 %copy-start.10 = (f32[384,512]{1,0:T(8,128)S(1)}, f32[384,512]{1,0:T(8,128)}, u32[]{:S(2)}) copy-start(f32[384,512]{1,0:T(8,128)} %get-tuple-element.42) | copy-start | bytes 2359300
  126.8 1.4 copy-start.2
  132.0 6.8 %collective-permute-start.1 = (bf16[528,512]{1,0:T(8,128)(2,1)}, bf16[528,512]{1,0:T(8,128)(2,1)S(1)}, u32[]{:S(2)}, u32[]{:S(2)}) collective-permute-start(bf16[528,512]{1,0:T(8,128)(2,1)} %get-tuple-element.55), channel_id=1, source_target_pairs={{0,16},{16,0},{32,48},{48,32},{64,80},{80,64},{96,112},{112,96},{1... | collective-permute-start | bytes 1622024 | tf_op jit(solution)/shard_map/ppermute | solution.py:522
  138.8 0.8 copy-start.13
  194.5 28.4 %all-to-all-start.5 = ((bf16[16,32,512]{2,1,0:T(8,128)(2,1)}), bf16[16,32,512]{2,1,0:T(8,128)(2,1)S(1)}, u32[]{:S(2)}, u32[]{:S(2)}) async-start(bf16[16,32,512]{2,1,0:T(8,128)(2,1)} %get-tuple-element.57), calls=%async_computation.5 | async-start | bytes 1048576 | tf_op jit(solution)/shard_map/all_to_all | solution.py:62
  200.9 9.2 %collective-permute-start.2 = (bf16[16,512]{1,0:T(8,128)(2,1)}, bf16[16,512]{1,0:T(8,128)(2,1)S(1)}, u32[]{:S(2)}, u32[]{:S(2)}) collective-permute-start(bf16[16,512]{1,0:T(8,128)(2,1)} %get-tuple-element.56), channel_id=1, source_target_pairs={{0,1},{1,2},{2,3},{3,0},{4,5},{5,6},{6,7},{7,4},{8,9},{9,10},{10,1... | collective-permute-start | bytes 49160 | tf_op jit(solution)/shard_map/ppermute | solution.py:546
  203.6 6.5 %collective-permute-start.3 = (bf16[16,512]{1,0:T(8,128)(2,1)}, bf16[16,512]{1,0:T(8,128)(2,1)S(1)}, u32[]{:S(2)}, u32[]{:S(2)}) collective-permute-start(bf16[16,512]{1,0:T(8,128)(2,1)} %get-tuple-element.56), channel_id=1, source_target_pairs={{0,2},{1,3},{2,0},{3,1},{4,6},{5,7},{6,4},{7,5},{8,10},{9,11},{10,... | collective-permute-start | bytes 49160 | tf_op jit(solution)/shard_map/ppermute | solution.py:546
  206.2 6.1 %collective-permute-start.4 = (bf16[16,512]{1,0:T(8,128)(2,1)}, bf16[16,512]{1,0:T(8,128)(2,1)S(1)}, u32[]{:S(2)}, u32[]{:S(2)}) collective-permute-start(bf16[16,512]{1,0:T(8,128)(2,1)} %get-tuple-element.56), channel_id=1, source_target_pairs={{0,3},{1,0},{2,1},{3,2},{4,7},{5,4},{6,5},{7,6},{8,11},{9,8},{10,9... | collective-permute-start | bytes 49160 | tf_op jit(solution)/shard_map/ppermute | solution.py:546
  212.2 19.8 %collective-permute-start.5 = (bf16[64,512]{1,0:T(8,128)(2,1)S(1)}, bf16[64,512]{1,0:T(8,128)(2,1)S(1)}, u32[]{:S(2)}, u32[]{:S(2)}) collective-permute-start(bf16[64,512]{1,0:T(8,128)(2,1)S(1)} %get-tuple-element.67), channel_id=1, source_target_pairs={{0,4},{1,5},{2,6},{3,7},{4,8},{5,9},{6,10},{7,11},{8,12},{9,13},{1... | collective-permute-start | bytes 196616 | tf_op jit(solution)/shard_map/ppermute | solution.py:546
  214.2 17.9 %collective-permute-start.6 = (bf16[64,512]{1,0:T(8,128)(2,1)S(1)}, bf16[64,512]{1,0:T(8,128)(2,1)S(1)}, u32[]{:S(2)}, u32[]{:S(2)}) collective-permute-start(bf16[64,512]{1,0:T(8,128)(2,1)S(1)} %get-tuple-element.67), channel_id=1, source_target_pairs={{0,8},{1,9},{2,10},{3,11},{4,12},{5,13},{6,14},{7,15},{8,0},{9,1},... | collective-permute-start | bytes 196616 | tf_op jit(solution)/shard_map/ppermute | solution.py:546
  218.4 13.7 %collective-permute-start.7 = (bf16[64,512]{1,0:T(8,128)(2,1)S(1)}, bf16[64,512]{1,0:T(8,128)(2,1)S(1)}, u32[]{:S(2)}, u32[]{:S(2)}) collective-permute-start(bf16[64,512]{1,0:T(8,128)(2,1)S(1)} %get-tuple-element.67), channel_id=1, source_target_pairs={{0,12},{1,13},{2,14},{3,15},{4,0},{5,1},{6,2},{7,3},{8,4},{9,5},{1... | collective-permute-start | bytes 196616 | tf_op jit(solution)/shard_map/ppermute | solution.py:546
  222.9 11.8 %copy-start.7 = (bf16[16,32,512]{2,1,0:T(8,128)(2,1)}, bf16[16,32,512]{2,1,0:T(8,128)(2,1)S(1)}, u32[]{:S(2)}) copy-start(bf16[16,32,512]{2,1,0:T(8,128)(2,1)S(1)} %all-to-all-done.5.grads_ref) | copy-start | bytes 1572868
  222.9 14.3 %collective-permute-start.9 = (bf16[16,32,512]{2,1,0:T(8,128)(2,1)S(1)}, bf16[16,32,512]{2,1,0:T(8,128)(2,1)S(1)}, u32[]{:S(2)}, u32[]{:S(2)}) collective-permute-start(bf16[16,32,512]{2,1,0:T(8,128)(2,1)S(1)} %all-to-all-done.5.grads_ref), channel_id=1, source_target_pairs={{0,16},{16,0},{32,48},{48,32},{64,80},{80,64},{96,112},{112,96},{1... | collective-permute-start | bytes 1572872 | tf_op jit(solution)/shard_map/ppermute | solution.py:551
  232.1 8.5 %copy-start.15 = (bf16[256,512]{1,0:T(8,128)(2,1)}, bf16[256,512]{1,0:T(8,128)(2,1)S(1)}, u32[]{:S(2)}) copy-start(bf16[256,512]{1,0:T(8,128)(2,1)S(1)} %constant_dynamic-update-slice_fusion.4.mine_ref) | copy-start | bytes 786436
  232.1 8.5 %collective-permute-start.8 = (bf16[256,512]{1,0:T(8,128)(2,1)S(1)}, bf16[256,512]{1,0:T(8,128)(2,1)S(1)}, u32[]{:S(2)}, u32[]{:S(2)}) collective-permute-start(bf16[256,512]{1,0:T(8,128)(2,1)S(1)} %constant_dynamic-update-slice_fusion.4.mine_ref), channel_id=1, source_target_pairs={{0,16},{16,0},{32,48},{48,32},{64,80},{80,64},{96,112},{112,96},{1... | collective-permute-start | bytes 786440 | tf_op jit(solution)/shard_map/ppermute | solution.py:550
  237.3 0.8 copy-start.14
  240.6 0.7 copy-start.16

commit v5 on v4

--- a/solution.py
+++ b/solution.py
@@ -15,13 +15,13 @@
 NEG = 64
 WROWS = 32
 CHIPS = 16
-NEAR = 4
-FAR = 4
 HALF = 512
 PIECE = 32
 SHARED = 16
 LANES = 128
 BLOCKS = D // LANES
+GRANT = 24 * 1024 * 1024
+WIDE_GRANT = 56 * 1024 * 1024
 
 epsilon = 1e-06
 logit_scale = 64.0
@@ -285,35 +285,22 @@
     half_sums(core_ref[0], pick_ref, neg_row_ref, returned, negs, weights, keep_ref)
 
 
-def near_kernel(keep_ref, other_ref, out_ref):
-    rows = HALF // NEAR
-    weights = (keep_ref[HALF:, :].astype(F32) + other_ref[HALF:, :].astype(F32)).astype(BF16)
-    for i in range(NEAR):
-        at = slice(i * rows, (i + 1) * rows)
-        total = keep_ref[at, :].astype(F32) + other_ref[at, :].astype(F32)
-        out_ref[i, 0:rows, :] = total.astype(BF16)
-        out_ref[i, rows:, :] = weights
-
-
-def far_kernel(recv_ref, out_ref):
-    rows = recv_ref.shape[1] - SHARED
+def pair_kernel(keep_ref, other_ref, out_ref, weights_ref):
+    for i in range(CHIPS):
+        at = slice(i * PIECE, (i + 1) * PIECE)
+        out_ref[i] = (keep_ref[at, :].astype(F32) + other_ref[at, :].astype(F32)).astype(BF16)
+    weights_ref[...] = (keep_ref[HALF:, :].astype(F32) + other_ref[HALF:, :].astype(F32)).astype(
+        BF16
+    )
+
+
+def total_kernel(recv_ref, out_ref):
     total = recv_ref[0].astype(F32)
-    for i in range(1, NEAR):
-        total = total + recv_ref[i].astype(F32)
-    total = total.astype(BF16)
-    for i in range(FAR):
-        out_ref[i, 0:PIECE, :] = total[i * PIECE : (i + 1) * PIECE]
-        out_ref[i, PIECE:, :] = total[rows:]
-
-
-def total_kernel(recv_ref, out_ref, weights_ref):
-    total = recv_ref[0].astype(F32)
-    for i in range(1, FAR):
+    for i in range(1, CHIPS):
         total = total + recv_ref[i].astype(F32)
     total = total.astype(BF16)
     for i in range(CHIPS):
-        out_ref[i] = total[0:PIECE]
-    weights_ref[...] = total[PIECE:]
+        out_ref[i] = total
 
 
 def weight_kernel(place_ref, mine_ref, other_ref, out_ref):
@@ -331,7 +318,7 @@
 def finish_kernel(half_ref, grads_ref, items_ref, *rest):
     out_ref = rest[-1]
     for i in range(CHIPS):
-        first = (i % NEAR) * (HALF // NEAR) + (i // NEAR) * PIECE
+        first = i * PIECE
         rows = items_ref[first : first + PIECE, :].astype(F32)
         grads = grads_ref[i].astype(F32)
         scale = lax.rsqrt(jnp.sum(rows * rows, axis=1, keepdims=True) + epsilon)
@@ -345,7 +332,7 @@
     count, width = items.shape
     half_block = pl.BlockSpec((HALF, width), lambda i, half_ref: (half_ref[0], 0))
     operands = [half.reshape(1), grads, items]
-    in_specs = [pl.BlockSpec((CHIPS, PIECE, width), lambda i, half_ref: (0, 0, 0)), half_block]
+    in_specs = [pl.BlockSpec(memory_space=pltpu.VMEM), half_block]
     aliases = {}
     if earlier is not None:
         operands.append(earlier)
@@ -358,12 +345,13 @@
             num_scalar_prefetch=1, grid=(1,), in_specs=in_specs, out_specs=half_block
         ),
         input_output_aliases=aliases,
+        compiler_params=pltpu.CompilerParams(vmem_limit_bytes=GRANT),
         cost_estimate=pl.CostEstimate(flops=0, bytes_accessed=1 << 21, transcendentals=0),
         name="finish",
     )(*operands)
 
 
-def local(kernel, outs, operands, scalars=0, scratch=(), flops=0):
+def local(kernel, outs, operands, scalars=0, scratch=(), grant=GRANT):
     spaces = [pltpu.SMEM] * scalars + [pltpu.VMEM] * (len(operands) - scalars)
     moved = sum(v.size * v.dtype.itemsize for v in operands) + sum(
         v.size * v.dtype.itemsize for v in outs
@@ -374,8 +362,8 @@
         in_specs=[pl.BlockSpec(memory_space=s) for s in spaces],
         out_specs=tuple(pl.BlockSpec(memory_space=pltpu.VMEM) for _ in outs),
         scratch_shapes=list(scratch),
-        compiler_params=pltpu.CompilerParams(vmem_limit_bytes=56 * 1024 * 1024),
-        cost_estimate=pl.CostEstimate(flops=flops, bytes_accessed=moved, transcendentals=0),
+        compiler_params=pltpu.CompilerParams(vmem_limit_bytes=grant),
+        cost_estimate=pl.CostEstimate(flops=0, bytes_accessed=moved, transcendentals=0),
     )(*operands)
 
 
@@ -392,8 +380,6 @@
     negs = PLANE * NEG
     partners = [(i, i ^ 1) for i in range(dp)]
     columns = [[2 * z + c for z in range(CHIPS)] for c in range(2)]
-    near = [[2 * (NEAR * h + l) + c for l in range(NEAR)] for h in range(FAR) for c in range(2)]
-    far = [[2 * (NEAR * h + l) + c for h in range(FAR)] for l in range(NEAR) for c in range(2)]
     core = lax.rem(lax.axis_index("dp"), 2).astype(I32)
     core_s = core.reshape(1)
     plane = lax.axis_index("shard").astype(I32)
@@ -408,6 +394,7 @@
         ],
         [core_s, index, w_proj, item_rows],
         scalars=1,
+        grant=WIDE_GRANT,
     )
     first_in = exchange(first_out, "shard")
 
@@ -419,6 +406,7 @@
         serve_kernel,
         [shaped((PLANE, CAP, width)), shaped((slots, item_count))],
         [first_in, unit_items],
+        grant=WIDE_GRANT,
     )
     served, first_mine = lax.optimization_barrier((served, first_in))
     looked_up = exchange(served, "shard")
@@ -454,6 +442,7 @@
             pltpu.VMEM((tok_rows, width), BF16),
             pltpu.VMEM((tok_rows, width), BF16),
         ],
+        grant=WIDE_GRANT,
     )
     third_in = exchange(third_out, "shard")
 
@@ -526,17 +515,15 @@
         [core_s, asked_pick, neg_row, returned, neg_sum, w_sum],
         scalars=1,
     )
-    (near_out,) = local(
-        near_kernel, [shaped((NEAR, HALF // NEAR + SHARED, width))], [kept, arrived]
-    )
-    (far_out,) = local(
-        far_kernel, [shaped((FAR, PIECE + SHARED, width))], [exchange(near_out, "dp", near)]
-    )
-    summed, w_rows = local(
-        total_kernel,
-        [shaped((CHIPS, PIECE, width)), shaped((SHARED, width))],
-        [exchange(far_out, "dp", far)],
-    )
+    pieces, w_rows = local(
+        pair_kernel, [shaped((CHIPS, PIECE, width)), shaped((SHARED, width))], [kept, arrived]
+    )
+    pieces = exchange(pieces, "dp", columns)
+    for k in range(4):
+        crossed = lax.ppermute(w_rows, "dp", [(i, i ^ (2 << k)) for i in range(dp)])
+        w_rows = (w_rows.astype(F32) + crossed.astype(F32)).astype(BF16)
+    pieces, w_rows = lax.optimization_barrier((pieces, w_rows))
+    (summed,) = local(total_kernel, [shaped((CHIPS, PIECE, width))], [pieces])
     mine = exchange(summed, "dp", columns)
 
     def turned(rows, step_y, step_x):
@@ -548,15 +535,15 @@
     w_rows = jnp.concatenate([w_rows] + [turned(w_rows, 0, k) for k in (1, 2, 3)], axis=0)
     w_rows = jnp.concatenate([w_rows] + [turned(w_rows, k, 0) for k in (1, 2, 3)], axis=0)
     w_other_rows = lax.ppermute(w_rows, "dp", partners)
-    other = lax.ppermute(mine, "dp", partners)
-    item_grads = finish(1 - core, other, item_rows, finish(core, mine, item_rows))
-    w_rows, w_other_rows, item_grads = lax.optimization_barrier((w_rows, w_other_rows, item_grads))
     (weight_grads,) = local(
         weight_kernel,
         [shaped((width, width), F32)],
         [jnp.stack([core, plane >> 2, plane & 3]), w_rows, w_other_rows],
         scalars=1,
     )
+    mine, weight_grads = lax.optimization_barrier((mine, weight_grads))
+    other = lax.ppermute(mine, "dp", partners)
+    item_grads = finish(1 - core, other, item_rows, finish(core, mine, item_rows))
     return (grad_tokens, weight_grads, item_grads)
 
 

time: 245 us -> 253 us (1.033)
  blocking collectives: 49.1 us -> 0 us
  starting transfers between devices: 60.9 us -> 110 us
  waiting for transfers between devices: 55.4 us -> 82.3 us
  Pallas kernels: 45.5 us -> 31 us
    all_to_all x2 -> x0, blocking collectives: 49.1 us -> none  [exchange(): lax.all_to_all(pieces, axis, split_axis=0, concat_axis=0, tiled=True, axi...]
    ppermute x0 -> x4, starting transfers between devices: none -> 27.1 us  [shards(): crossed = lax.ppermute(w_rows, 'dp', [(i, i ^ 2 << k) for i in range(dp)])]
    ppermute x0 -> x4, waiting for transfers between devices: none -> 24.5 us  [shards(): crossed = lax.ppermute(w_rows, 'dp', [(i, i ^ 2 << k) for i in range(dp)])]
    all_to_all x4 -> x5, starting transfers between devices: 21.7 us -> 44.1 us  [exchange(): lax.all_to_all(pieces, axis, split_axis=0, concat_axis=0, tiled=True, axi...]
    pallas_call x11 -> x10, Pallas kernels: 40.4 us -> 28.2 us  [local(): pl.pallas_call(kernel, out_shape=tuple(outs), in_specs=[pl.BlockSpec(memo...]
    ppermute x1, starting transfers between devices: 9.13 us -> 2.27 us  [shards(): other = lax.ppermute(mine, 'dp', partners)]
    ppermute x1, starting transfers between devices: 1.92 us -> 8.5 us  [shards(): w_other_rows = lax.ppermute(w_rows, 'dp', partners)]
    all_to_all x4 -> x5, waiting for transfers between devices: 53.3 us -> 51.5 us  [exchange(): lax.all_to_all(pieces, axis, split_axis=0, concat_axis=0, tiled=True, axi...]
  transfers between devices with their start and end apart: 14 -> 19, of which waited for: 5 -> 12; matrix products, arithmetic and copies ran while one was open for 4% -> 4% of each run, Pallas kernels for 6% -> 4%
where the time goes in v5:
time: 253 us; the launch traced here: 252 us
  starting transfers between devices  110 us (43%)
  waiting for transfers between devices  82.3 us (33%)
  Pallas kernels  31 us (12%)
  matrix products  15.1 us (6%)
  local copies, waits for them, and re-layouts  7.44 us (3%)
  other arithmetic  4.83 us (2%)
    all_to_all x5, waiting for transfers between devices, exchange(): lax.all_to_all(pieces, axis, split_axis=0, concat_axis=0, tiled=True, axi...  51.5 us
    all_to_all x5, starting transfers between devices, exchange(): lax.all_to_all(pieces, axis, split_axis=0, concat_axis=0, tiled=True, axi...  44.1 us
    pallas_call x10, Pallas kernels, local(): pl.pallas_call(kernel, out_shape=tuple(outs), in_specs=[pl.BlockSpec(memo...  28.2 us
    ppermute x4, starting transfers between devices, shards(): crossed = lax.ppermute(w_rows, 'dp', [(i, i ^ 2 << k) for i in range(dp)])  27.1 us
    ppermute x4, waiting for transfers between devices, shards(): crossed = lax.ppermute(w_rows, 'dp', [(i, i ^ 2 << k) for i in range(dp)])  24.5 us
    ppermute x6, starting transfers between devices, turned(): return lax.ppermute(rows, 'shard', moves)  17.6 us
    dot_general x9, matrix products, dot(): return lax.dot_general(a, b, (contract, batch), preferred_element_type=F32)  15.1 us
    ppermute x1, starting transfers between devices, shards(): w_other_rows = lax.ppermute(w_rows, 'dp', partners)  8.5 us
  transfers between devices with their start and end apart: 19, of which 12 were waited for; matrix products, arithmetic and copies ran while one was open for 4% of the time, Pallas kernels for 4%

profile of v5, /device:TPU:1, one launch (start us, length us, event | category | flops | bytes accessed | tf_op | source)
XLA Modules:
  0.0 251.9 jit_solution(1199807587493919660)
XLA Ops:
  2.7 3.7 %shard_map.103 = (bf16[16,400,128]{2,1,0:T(8,128)(2,1)}, s32[384,1]{1,0:T(8,128)}) custom-call(s32[1]{0:T(128)} %bitcast.core_ref.half_ref, s32[1,832]{1,0:T(1,128)} %reshape.115.index_ref, bf16[512,128]{1,0:T(8,128)(2,1)} %w_ref.1, bf16[1024,512]{1,0:T(8,128)(2,1)} %items_ref.5), custom_call_target="tpu_custom_call" | custom-call | bytes 2822916 | tf_op jit(solution)/shard_map/pallas_call | solution.py:359
  6.4 7.6 %all-to-all-start = ((bf16[16,400,128]{2,1,0:T(8,128)(2,1)}), bf16[16,400,128]{2,1,0:T(8,128)(2,1)S(1)}, u32[]{:S(2)}, u32[]{:S(2)}) async-start(bf16[16,400,128]{2,1,0:T(8,128)(2,1)} %get-tuple-element.33), calls=%async_computation | async-start | bytes 3276800 | tf_op jit(solution)/shard_map/all_to_all | solution.py:62
  14.3 1.3 fusion.4.items_ref
  15.6 18.9 %all-to-all-done.recv_ref.mine_ref = bf16[16,400,128]{2,1,0:T(8,128)(2,1)S(1)} async-done(((bf16[16,400,128]{2,1,0:T(8,128)(2,1)}), bf16[16,400,128]{2,1,0:T(8,128)(2,1)S(1)}, u32[]{:S(2)}, u32[]{:S(2)}) %all-to-all-start) | async-done | bytes 1638432 | tf_op jit(solution)/shard_map/all_to_all | solution.py:62
  34.5 1.2 copy-done
  35.7 4.1 %shard_map.104 = (bf16[16,48,512]{2,1,0:T(8,128)(2,1)}, bf16[768,1024]{1,0:T(8,128)(2,1)}) custom-call(bf16[16,400,128]{2,1,0:T(8,128)(2,1)} %copy-done, bf16[1024,512]{1,0:T(8,128)(2,1)} %fusion.4.items_ref), custom_call_target="tpu_custom_call" | custom-call | bytes 5046272 | tf_op jit(solution)/shard_map/pallas_call | solution.py:359
  39.8 7.0 %collective-permute-start = (bf16[16,400,128]{2,1,0:T(8,128)(2,1)}, bf16[16,400,128]{2,1,0:T(8,128)(2,1)}, u32[]{:S(2)}, u32[]{:S(2)}) collective-permute-start(bf16[16,400,128]{2,1,0:T(8,128)(2,1)} %copy-done), channel_id=1, source_target_pairs={{0,16},{16,0},{32,48},{48,32},{64,80},{80,64},{96,112},{112,96},{1... | collective-permute-start | bytes 4915208 | tf_op jit(solution)/shard_map/ppermute | solution.py:413
  46.7 4.5 %all-to-all-start.1 = ((bf16[16,48,512]{2,1,0:T(8,128)(2,1)}), bf16[16,48,512]{2,1,0:T(8,128)(2,1)}, u32[]{:S(2)}, u32[]{:S(2)}) async-start(bf16[16,48,512]{2,1,0:T(8,128)(2,1)} %get-tuple-element.40), calls=%async_computation.1 | async-start | bytes 1572864 | tf_op jit(solution)/shard_map/all_to_all | solution.py:62
  51.7 1.0 copy-done.5
  52.7 5.3 %shard_map.105 = (f32[384,512]{1,0:T(8,128)S(1)}, bf16[4,384,128]{2,1,0:T(8,128)(2,1)S(1)}, bf16[16,512,128]{2,1,0:T(8,128)(2,1)S(1)}) custom-call(s32[1]{0:T(128)} %bitcast.core_ref.half_ref, s32[1,4]{1,0:T(1,128)S(1)} %copy-done.12, bf16[384,512]{1,0:T(8,128)(2,1)S(1)} %copy-done.4, bf16[16,400,128]{2,1,0:T(8,128)(2,1)S(1)} %copy-done.1, ...), custom_call_target="tpu_custom_call" | custom-call | bytes 7471124 | tf_op jit(solution)/shard_map/pallas_call | solution.py:359
  59.7 1.3 copy-done.13
  61.0 4.8 %all-to-all-done.1.recv_ref = bf16[16,48,512]{2,1,0:T(8,128)(2,1)} async-done(((bf16[16,48,512]{2,1,0:T(8,128)(2,1)}), bf16[16,48,512]{2,1,0:T(8,128)(2,1)}, u32[]{:S(2)}, u32[]{:S(2)}) %all-to-all-start.1) | async-done | bytes 786464 | tf_op jit(solution)/shard_map/all_to_all | solution.py:62
  65.8 8.3 %shard_map.106 = (bf16[16,144,512]{2,1,0:T(8,128)(2,1)}, f32[384,512]{1,0:T(8,128)}, bf16[384,512]{1,0:T(8,128)(2,1)}) custom-call(s32[1]{0:T(128)} %bitcast.core_ref.half_ref, f32[384,512]{1,0:T(8,128)} %copy-done.9, bf16[4,384,128]{2,1,0:T(8,128)(2,1)} %copy-done.10, bf16[16,48,512]{2,1,0:T(8,128)(2,1)} %all-to-all-done.1.recv_ref, ...), custom_call_target="tpu_custom_call" | custom-call | bytes 8783364 | tf_op jit(solution)/shard_map/pallas_call | solution.py:359
  75.3 3.5 %multiply_convert_fusion = (bf16[16,384,128]{1,2,0:T(8,128)(2,1)S(1)}, f32[16,384,128]{1,2,0:T(8,128)}) fusion(bf16[16,512,128]{2,1,0:T(8,128)(2,1)S(1)} %copy-done.14, bf16[384,512]{1,0:T(8,128)(2,1)S(1)} %shard_map.107), kind=kOutput, calls=%fused_computation.2 | convolution fusion | flops 809238528 | bytes 7208960 | tf_op jit(solution)/shard_map/dot_general | solution.py:36
  78.8 1.1 select_convert_fusion.1
  81.9 1.3 fusion.35
  83.2 1.5 select_convert_fusion
  84.7 4.7 %all-to-all-start.2 = ((bf16[16,144,512]{2,1,0:T(8,128)(2,1)}), bf16[16,144,512]{2,1,0:T(8,128)(2,1)}, u32[]{:S(2)}, u32[]{:S(2)}) async-start(bf16[16,144,512]{2,1,0:T(8,128)(2,1)} %get-tuple-element.42), calls=%async_computation.2 | async-start | bytes 4718592 | tf_op jit(solution)/shard_map/all_to_all | solution.py:62
  89.4 1.6 fusion.29
  91.1 1.4 fusion.25
  92.5 3.5 %fusion.10 = (f32[384]{0:T(512)S(1)}, f32[384]{0:T(512)S(1)}, f32[384,512]{1,0:T(8,128)S(1)}) fusion(bf16[384,512]{1,0:T(8,128)(2,1)S(1)} %copy-done.4, bf16[16,512,128]{2,1,0:T(8,128)(2,1)S(1)} %copy-done.15, f32[4,384,128]{1,2,0:T(8,128)S(1)} %fusion.25, f32[4,384,128]{1,2,0:T(8,128)S(1)} %fusion.29, f32[4,384,128]{1,2,0:T(8,128)S(1)} %copy-done.18, ...), kind=kOutput, calls=%fused_computation.23 | convolution fusion | flops 815725824 | bytes 9571328 | tf_op jit(solution)/shard_map/dot_general | solution.py:36
  97.1 27.8 %all-to-all-done.2.recv_ref = bf16[16,144,512]{2,1,0:T(8,128)(2,1)} async-done(((bf16[16,144,512]{2,1,0:T(8,128)(2,1)}), bf16[16,144,512]{2,1,0:T(8,128)(2,1)}, u32[]{:S(2)}, u32[]{:S(2)}) %all-to-all-start.2) | async-done | bytes 2359328 | tf_op jit(solution)/shard_map/all_to_all | solution.py:62
  124.9 2.6 %shard_map.108 = (bf16[528,512]{1,0:T(8,128)(2,1)S(1)}, bf16[768,512]{1,0:T(8,128)(2,1)S(1)}, bf16[64,512]{1,0:T(8,128)(2,1)S(1)}, f32[32,512]{1,0:T(8,128)S(1)}) custom-call(s32[1]{0:T(128)} %bitcast.core_ref.half_ref, bf16[16,144,512]{2,1,0:T(8,128)(2,1)} %all-to-all-done.2.recv_ref, bf16[768,1024]{1,0:T(8,128)(2,1)S(1)} %copy-done.3, s32[1,64]{1,0:T(1,128)S(1)} %bitcast.22), custom_call_target="tpu_custom_call" | custom-call | bytes 5390596 | tf_op jit(solution)/shard_map/pallas_call | solution.py:359
  127.4 3.6 %collective-permute-start.1 = (bf16[528,512]{1,0:T(8,128)(2,1)S(1)}, bf16[528,512]{1,0:T(8,128)(2,1)S(1)}, u32[]{:S(2)}, u32[]{:S(2)}) collective-permute-start(bf16[528,512]{1,0:T(8,128)(2,1)S(1)} %get-tuple-element.56), channel_id=1, source_target_pairs={{0,16},{16,0},{32,48},{48,32},{64,80},{80,64},{96,112},{112,96},{1... | collective-permute-start | bytes 1622024 | tf_op jit(solution)/shard_map/ppermute | solution.py:511
  133.5 15.8 %all-to-all-start.3 = ((bf16[16,32,512]{2,1,0:T(8,128)(2,1)}), bf16[16,32,512]{2,1,0:T(8,128)(2,1)S(1)}, u32[]{:S(2)}, u32[]{:S(2)}) async-start(bf16[16,32,512]{2,1,0:T(8,128)(2,1)} %get-tuple-element.57), calls=%async_computation.3 | async-start | bytes 1048576 | tf_op jit(solution)/shard_map/all_to_all | solution.py:62
  149.3 3.3 %collective-permute-start.2 = (bf16[16,512]{1,0:T(8,128)(2,1)S(1)}, bf16[16,512]{1,0:T(8,128)(2,1)S(1)}, u32[]{:S(2)}, u32[]{:S(2)}) collective-permute-start(bf16[16,512]{1,0:T(8,128)(2,1)S(1)} %get-tuple-element.58), channel_id=1, source_target_pairs={{0,32},{16,48},{32,0},{48,16},{64,96},{80,112},{96,64},{112,80},{1... | collective-permute-start | bytes 49160 | tf_op jit(solution)/shard_map/ppermute | solution.py:523
  152.6 19.8 %collective-permute-done.2 = bf16[16,512]{1,0:T(8,128)(2,1)S(1)} collective-permute-done((bf16[16,512]{1,0:T(8,128)(2,1)S(1)}, bf16[16,512]{1,0:T(8,128)(2,1)S(1)}, u32[]{:S(2)}, u32[]{:S(2)}) %collective-permute-start.2) | collective-permute-done | bytes 16416 | tf_op jit(solution)/shard_map/ppermute | solution.py:523
  172.4 3.3 %collective-permute-start.3 = (bf16[16,512]{1,0:T(8,128)(2,1)S(1)}, bf16[16,512]{1,0:T(8,128)(2,1)S(1)}, u32[]{:S(2)}, u32[]{:S(2)}) collective-permute-start(bf16[16,512]{1,0:T(8,128)(2,1)S(1)} %add_convert_fusion.3), channel_id=1, source_target_pairs={{0,64},{16,80},{32,96},{48,112},{64,0},{80,16},{96,32},{112,48},{1... | collective-permute-start | bytes 49160 | tf_op jit(solution)/shard_map/ppermute | solution.py:523
  175.7 2.5 collective-permute-done.3
  178.2 7.2 %collective-permute-start.4 = (bf16[16,512]{1,0:T(8,128)(2,1)S(1)}, bf16[16,512]{1,0:T(8,128)(2,1)S(1)}, u32[]{:S(2)}, u32[]{:S(2)}) collective-permute-start(bf16[16,512]{1,0:T(8,128)(2,1)S(1)} %add_convert_fusion.2), channel_id=1, source_target_pairs={{0,128},{16,144},{32,160},{48,176},{64,192},{80,208},{96,224},{112... | collective-permute-start | bytes 49160 | tf_op jit(solution)/shard_map/ppermute | solution.py:523
  185.4 1.2 collective-permute-done.4
  186.6 13.3 %collective-permute-start.5 = (bf16[16,512]{1,0:T(8,128)(2,1)S(1)}, bf16[16,512]{1,0:T(8,128)(2,1)S(1)}, u32[]{:S(2)}, u32[]{:S(2)}) collective-permute-start(bf16[16,512]{1,0:T(8,128)(2,1)S(1)} %add_convert_fusion.1), channel_id=1, source_target_pairs={{0,256},{16,272},{32,288},{48,304},{64,320},{80,336},{96,352},{112... | collective-permute-start | bytes 49160 | tf_op jit(solution)/shard_map/ppermute | solution.py:523
  199.9 1.1 collective-permute-done.5
  201.9 11.5 %all-to-all-start.4 = ((bf16[16,32,512]{2,1,0:T(8,128)(2,1)}), bf16[16,32,512]{2,1,0:T(8,128)(2,1)S(1)}, u32[]{:S(2)}, u32[]{:S(2)}) async-start(bf16[16,32,512]{2,1,0:T(8,128)(2,1)} %shard_map.111), calls=%async_computation.4 | async-start | bytes 1048576 | tf_op jit(solution)/shard_map/all_to_all | solution.py:62
  213.5 1.9 collective-permute-start.6
  215.4 2.6 %collective-permute-start.7 = (bf16[16,512]{1,0:T(8,128)(2,1)S(1)}, bf16[16,512]{1,0:T(8,128)(2,1)S(1)}, u32[]{:S(2)}, u32[]{:S(2)}) collective-permute-start(bf16[16,512]{1,0:T(8,128)(2,1)S(1)} %add_convert_fusion), channel_id=1, source_target_pairs={{0,2},{1,3},{2,0},{3,1},{4,6},{5,7},{6,4},{7,5},{8,10},{9,11},{10,... | collective-permute-start | bytes 49160 | tf_op jit(solution)/shard_map/ppermute | solution.py:533
  218.1 3.9 %collective-permute-start.8 = (bf16[16,512]{1,0:T(8,128)(2,1)S(1)}, bf16[16,512]{1,0:T(8,128)(2,1)S(1)}, u32[]{:S(2)}, u32[]{:S(2)}) collective-permute-start(bf16[16,512]{1,0:T(8,128)(2,1)S(1)} %add_convert_fusion), channel_id=1, source_target_pairs={{0,3},{1,0},{2,1},{3,2},{4,7},{5,4},{6,5},{7,6},{8,11},{9,8},{10,9... | collective-permute-start | bytes 49160 | tf_op jit(solution)/shard_map/ppermute | solution.py:533
  222.0 1.9 collective-permute-done.8
  223.9 1.9 collective-permute-start.9
  225.8 4.3 %collective-permute-start.10 = (bf16[64,512]{1,0:T(8,128)(2,1)S(1)}, bf16[64,512]{1,0:T(8,128)(2,1)S(1)}, u32[]{:S(2)}, u32[]{:S(2)}) collective-permute-start(bf16[64,512]{1,0:T(8,128)(2,1)S(1)} %get-tuple-element.69), channel_id=1, source_target_pairs={{0,8},{1,9},{2,10},{3,11},{4,12},{5,13},{6,14},{7,15},{8,0},{9,1},... | collective-permute-start | bytes 196616 | tf_op jit(solution)/shard_map/ppermute | solution.py:533
  230.1 3.0 %collective-permute-start.11 = (bf16[64,512]{1,0:T(8,128)(2,1)S(1)}, bf16[64,512]{1,0:T(8,128)(2,1)S(1)}, u32[]{:S(2)}, u32[]{:S(2)}) collective-permute-start(bf16[64,512]{1,0:T(8,128)(2,1)S(1)} %get-tuple-element.69), channel_id=1, source_target_pairs={{0,12},{1,13},{2,14},{3,15},{4,0},{5,1},{6,2},{7,3},{8,4},{9,5},{1... | collective-permute-start | bytes 196616 | tf_op jit(solution)/shard_map/ppermute | solution.py:533
  233.1 2.3 collective-permute-done.11
  235.4 8.5 %collective-permute-start.12 = (bf16[256,512]{1,0:T(8,128)(2,1)S(1)}, bf16[256,512]{1,0:T(8,128)(2,1)S(1)}, u32[]{:S(2)}, u32[]{:S(2)}) collective-permute-start(bf16[256,512]{1,0:T(8,128)(2,1)S(1)} %constant_dynamic-update-slice_fusion.4.mine_ref), channel_id=1, source_target_pairs={{0,16},{16,0},{32,48},{48,32},{64,80},{80,64},{96,112},{112,96},{1... | collective-permute-start | bytes 786440 | tf_op jit(solution)/shard_map/ppermute | solution.py:537
  244.0 1.1 collective-permute-done.12.other_ref
  245.1 1.6 shard_map.112
  246.7 2.3 collective-permute-start.13
  249.0 1.4 finish.2.rest_0_
  250.5 1.4 finish.3
  (76 shorter events, 12.2 us)
Async XLA Ops:
  0.6 13.4 %copy-start.2 = (bf16[1024,512]{1,0:T(8,128)(2,1)S(1)}, bf16[1024,512]{1,0:T(8,128)(2,1)}, u32[]{:S(2)}) copy-start(bf16[1024,512]{1,0:T(8,128)(2,1)} %items_ref.5) | copy-start | bytes 3145732
  6.4 28.1 %all-to-all-start = ((bf16[16,400,128]{2,1,0:T(8,128)(2,1)}), bf16[16,400,128]{2,1,0:T(8,128)(2,1)S(1)}, u32[]{:S(2)}, u32[]{:S(2)}) async-start(bf16[16,400,128]{2,1,0:T(8,128)(2,1)} %get-tuple-element.33), calls=%async_computation | async-start | bytes 3276800 | tf_op jit(solution)/shard_map/all_to_all | solution.py:62
  15.6 35.7 %copy-start.12 = (s32[1,4]{1,0:T(1,128)S(1)}, s32[1,4]{1,0:T(1,128)}, u32[]{:S(2)}) copy-start(s32[1,4]{1,0:T(1,128)} %lengths_ref.1) | copy-start | bytes 52
  15.6 36.1 %copy-start.4 = (bf16[384,512]{1,0:T(8,128)(2,1)S(1)}, bf16[384,512]{1,0:T(8,128)(2,1)}, u32[]{:S(2)}) copy-start(bf16[384,512]{1,0:T(8,128)(2,1)} %tokens_ref.3) | copy-start | bytes 1179652
  34.5 1.2 copy-start
  39.8 11.9 %copy-start.1 = (bf16[16,400,128]{2,1,0:T(8,128)(2,1)S(1)}, bf16[16,400,128]{2,1,0:T(8,128)(2,1)}, u32[]{:S(2)}) copy-start(bf16[16,400,128]{2,1,0:T(8,128)(2,1)} %copy-done) | copy-start | bytes 4915204
  39.8 11.9 %collective-permute-start = (bf16[16,400,128]{2,1,0:T(8,128)(2,1)}, bf16[16,400,128]{2,1,0:T(8,128)(2,1)}, u32[]{:S(2)}, u32[]{:S(2)}) collective-permute-start(bf16[16,400,128]{2,1,0:T(8,128)(2,1)} %copy-done), channel_id=1, source_target_pairs={{0,16},{16,0},{32,48},{48,32},{64,80},{80,64},{96,112},{112,96},{1... | collective-permute-start | bytes 4915208 | tf_op jit(solution)/shard_map/ppermute | solution.py:413
  46.7 19.1 %all-to-all-start.1 = ((bf16[16,48,512]{2,1,0:T(8,128)(2,1)}), bf16[16,48,512]{2,1,0:T(8,128)(2,1)}, u32[]{:S(2)}, u32[]{:S(2)}) async-start(bf16[16,48,512]{2,1,0:T(8,128)(2,1)} %get-tuple-element.40), calls=%async_computation.1 | async-start | bytes 1572864 | tf_op jit(solution)/shard_map/all_to_all | solution.py:62
  51.7 1.0 copy-start.5
  58.1 0.9 copy-start.9
  59.0 0.7 copy-start.10
  59.7 1.3 copy-start.13
  65.8 9.4 %copy-start.14 = (bf16[16,512,128]{2,1,0:T(8,128)(2,1)S(1)}, bf16[16,512,128]{2,1,0:T(8,128)(2,1)}, u32[]{:S(2)}) copy-start(bf16[16,512,128]{2,1,0:T(8,128)(2,1)} %copy-done.13) | copy-start | bytes 6291460
  74.1 1.0 copy-start.7
  78.8 4.5 %copy-start.16 = (bf16[16,384,128]{1,2,0:T(8,128)(2,1)}, bf16[16,384,128]{1,2,0:T(8,128)(2,1)S(1)}, u32[]{:S(2)}) copy-start(bf16[16,384,128]{1,2,0:T(8,128)(2,1)S(1)} %get-tuple-element.81) | copy-start | bytes 4718596
  78.8 1.4 copy-start.6
  78.8 1.7 copy-start.8
  84.7 40.2 %all-to-all-start.2 = ((bf16[16,144,512]{2,1,0:T(8,128)(2,1)}), bf16[16,144,512]{2,1,0:T(8,128)(2,1)}, u32[]{:S(2)}, u32[]{:S(2)}) async-start(bf16[16,144,512]{2,1,0:T(8,128)(2,1)} %get-tuple-element.42), calls=%async_computation.2 | async-start | bytes 4718592 | tf_op jit(solution)/shard_map/all_to_all | solution.py:62
  89.4 3.1 %copy-start.15 = (bf16[16,512,128]{2,1,0:T(8,128)(2,1)S(1)}, bf16[16,512,128]{2,1,0:T(8,128)(2,1)}, u32[]{:S(2)}) copy-start(bf16[16,512,128]{2,1,0:T(8,128)(2,1)} %copy-done.13) | copy-start | bytes 6291460
  89.4 3.1 %copy-start.18 = (f32[4,384,128]{1,2,0:T(8,128)S(1)}, f32[4,384,128]{1,2,0:T(8,128)}, u32[]{:S(2)}) copy-start(f32[4,384,128]{1,2,0:T(8,128)} %fusion.35) | copy-start | bytes 2359300
  92.5 3.6 %copy-start.17 = (f32[384,512]{1,0:T(8,128)S(1)}, f32[384,512]{1,0:T(8,128)}, u32[]{:S(2)}) copy-start(f32[384,512]{1,0:T(8,128)} %get-tuple-element.43) | copy-start | bytes 2359300
  96.0 28.8 %copy-start.3 = (bf16[768,1024]{1,0:T(8,128)(2,1)S(1)}, bf16[768,1024]{1,0:T(8,128)(2,1)}, u32[]{:S(2)}) copy-start(bf16[768,1024]{1,0:T(8,128)(2,1)} %get-tuple-element.51.pick_ref) | copy-start | bytes 4718596
  96.0 28.8 %copy-start.11 = (s32[64]{0:T(128)S(1)}, s32[64]{0:T(128)}, u32[]{:S(2)}) copy-start(s32[64]{0:T(128)} %param.15) | copy-start | bytes 772
  127.4 5.2 %collective-permute-start.1 = (bf16[528,512]{1,0:T(8,128)(2,1)S(1)}, bf16[528,512]{1,0:T(8,128)(2,1)S(1)}, u32[]{:S(2)}, u32[]{:S(2)}) collective-permute-start(bf16[528,512]{1,0:T(8,128)(2,1)S(1)} %get-tuple-element.56), channel_id=1, source_target_pairs={{0,16},{16,0},{32,48},{48,32},{64,80},{80,64},{96,112},{112,96},{1... | collective-permute-start | bytes 1622024 | tf_op jit(solution)/shard_map/ppermute | solution.py:511
  133.5 67.5 %all-to-all-start.3 = ((bf16[16,32,512]{2,1,0:T(8,128)(2,1)}), bf16[16,32,512]{2,1,0:T(8,128)(2,1)S(1)}, u32[]{:S(2)}, u32[]{:S(2)}) async-start(bf16[16,32,512]{2,1,0:T(8,128)(2,1)} %get-tuple-element.57), calls=%async_computation.3 | async-start | bytes 1048576 | tf_op jit(solution)/shard_map/all_to_all | solution.py:62
  149.3 23.1 %collective-permute-start.2 = (bf16[16,512]{1,0:T(8,128)(2,1)S(1)}, bf16[16,512]{1,0:T(8,128)(2,1)S(1)}, u32[]{:S(2)}, u32[]{:S(2)}) collective-permute-start(bf16[16,512]{1,0:T(8,128)(2,1)S(1)} %get-tuple-element.58), channel_id=1, source_target_pairs={{0,32},{16,48},{32,0},{48,16},{64,96},{80,112},{96,64},{112,80},{1... | collective-permute-start | bytes 49160 | tf_op jit(solution)/shard_map/ppermute | solution.py:523
  172.4 5.8 %collective-permute-start.3 = (bf16[16,512]{1,0:T(8,128)(2,1)S(1)}, bf16[16,512]{1,0:T(8,128)(2,1)S(1)}, u32[]{:S(2)}, u32[]{:S(2)}) collective-permute-start(bf16[16,512]{1,0:T(8,128)(2,1)S(1)} %add_convert_fusion.3), channel_id=1, source_target_pairs={{0,64},{16,80},{32,96},{48,112},{64,0},{80,16},{96,32},{112,48},{1... | collective-permute-start | bytes 49160 | tf_op jit(solution)/shard_map/ppermute | solution.py:523
  178.2 8.4 %collective-permute-start.4 = (bf16[16,512]{1,0:T(8,128)(2,1)S(1)}, bf16[16,512]{1,0:T(8,128)(2,1)S(1)}, u32[]{:S(2)}, u32[]{:S(2)}) collective-permute-start(bf16[16,512]{1,0:T(8,128)(2,1)S(1)} %add_convert_fusion.2), channel_id=1, source_target_pairs={{0,128},{16,144},{32,160},{48,176},{64,192},{80,208},{96,224},{112... | collective-permute-start | bytes 49160 | tf_op jit(solution)/shard_map/ppermute | solution.py:523
  186.6 14.4 %collective-permute-start.5 = (bf16[16,512]{1,0:T(8,128)(2,1)S(1)}, bf16[16,512]{1,0:T(8,128)(2,1)S(1)}, u32[]{:S(2)}, u32[]{:S(2)}) collective-permute-start(bf16[16,512]{1,0:T(8,128)(2,1)S(1)} %add_convert_fusion.1), channel_id=1, source_target_pairs={{0,256},{16,272},{32,288},{48,304},{64,320},{80,336},{96,352},{112... | collective-permute-start | bytes 49160 | tf_op jit(solution)/shard_map/ppermute | solution.py:523
  201.9 44.8 %all-to-all-start.4 = ((bf16[16,32,512]{2,1,0:T(8,128)(2,1)}), bf16[16,32,512]{2,1,0:T(8,128)(2,1)S(1)}, u32[]{:S(2)}, u32[]{:S(2)}) async-start(bf16[16,32,512]{2,1,0:T(8,128)(2,1)} %shard_map.111), calls=%async_computation.4 | async-start | bytes 1048576 | tf_op jit(solution)/shard_map/all_to_all | solution.py:62
  213.5 8.5 %collective-permute-start.6 = (bf16[16,512]{1,0:T(8,128)(2,1)S(1)}, bf16[16,512]{1,0:T(8,128)(2,1)S(1)}, u32[]{:S(2)}, u32[]{:S(2)}) collective-permute-start(bf16[16,512]{1,0:T(8,128)(2,1)S(1)} %add_convert_fusion), channel_id=1, source_target_pairs={{0,1},{1,2},{2,3},{3,0},{4,5},{5,6},{6,7},{7,4},{8,9},{9,10},{10,1... | collective-permute-start | bytes 49160 | tf_op jit(solution)/shard_map/ppermute | solution.py:533
  215.4 6.5 %collective-permute-start.7 = (bf16[16,512]{1,0:T(8,128)(2,1)S(1)}, bf16[16,512]{1,0:T(8,128)(2,1)S(1)}, u32[]{:S(2)}, u32[]{:S(2)}) collective-permute-start(bf16[16,512]{1,0:T(8,128)(2,1)S(1)} %add_convert_fusion), channel_id=1, source_target_pairs={{0,2},{1,3},{2,0},{3,1},{4,6},{5,7},{6,4},{7,5},{8,10},{9,11},{10,... | collective-permute-start | bytes 49160 | tf_op jit(solution)/shard_map/ppermute | solution.py:533
  218.1 5.8 %collective-permute-start.8 = (bf16[16,512]{1,0:T(8,128)(2,1)S(1)}, bf16[16,512]{1,0:T(8,128)(2,1)S(1)}, u32[]{:S(2)}, u32[]{:S(2)}) collective-permute-start(bf16[16,512]{1,0:T(8,128)(2,1)S(1)} %add_convert_fusion), channel_id=1, source_target_pairs={{0,3},{1,0},{2,1},{3,2},{4,7},{5,4},{6,5},{7,6},{8,11},{9,8},{10,9... | collective-permute-start | bytes 49160 | tf_op jit(solution)/shard_map/ppermute | solution.py:533
  223.9 9.2 %collective-permute-start.9 = (bf16[64,512]{1,0:T(8,128)(2,1)S(1)}, bf16[64,512]{1,0:T(8,128)(2,1)S(1)}, u32[]{:S(2)}, u32[]{:S(2)}) collective-permute-start(bf16[64,512]{1,0:T(8,128)(2,1)S(1)} %get-tuple-element.69), channel_id=1, source_target_pairs={{0,4},{1,5},{2,6},{3,7},{4,8},{5,9},{6,10},{7,11},{8,12},{9,13},{1... | collective-permute-start | bytes 196616 | tf_op jit(solution)/shard_map/ppermute | solution.py:533
  225.8 7.3 %collective-permute-start.10 = (bf16[64,512]{1,0:T(8,128)(2,1)S(1)}, bf16[64,512]{1,0:T(8,128)(2,1)S(1)}, u32[]{:S(2)}, u32[]{:S(2)}) collective-permute-start(bf16[64,512]{1,0:T(8,128)(2,1)S(1)} %get-tuple-element.69), channel_id=1, source_target_pairs={{0,8},{1,9},{2,10},{3,11},{4,12},{5,13},{6,14},{7,15},{8,0},{9,1},... | collective-permute-start | bytes 196616 | tf_op jit(solution)/shard_map/ppermute | solution.py:533
  230.1 5.3 %collective-permute-start.11 = (bf16[64,512]{1,0:T(8,128)(2,1)S(1)}, bf16[64,512]{1,0:T(8,128)(2,1)S(1)}, u32[]{:S(2)}, u32[]{:S(2)}) collective-permute-start(bf16[64,512]{1,0:T(8,128)(2,1)S(1)} %get-tuple-element.69), channel_id=1, source_target_pairs={{0,12},{1,13},{2,14},{3,15},{4,0},{5,1},{6,2},{7,3},{8,4},{9,5},{1... | collective-permute-start | bytes 196616 | tf_op jit(solution)/shard_map/ppermute | solution.py:533
  235.4 9.6 %collective-permute-start.12 = (bf16[256,512]{1,0:T(8,128)(2,1)S(1)}, bf16[256,512]{1,0:T(8,128)(2,1)S(1)}, u32[]{:S(2)}, u32[]{:S(2)}) collective-permute-start(bf16[256,512]{1,0:T(8,128)(2,1)S(1)} %constant_dynamic-update-slice_fusion.4.mine_ref), channel_id=1, source_target_pairs={{0,16},{16,0},{32,48},{48,32},{64,80},{80,64},{96,112},{112,96},{1... | collective-permute-start | bytes 786440 | tf_op jit(solution)/shard_map/ppermute | solution.py:537
  246.7 3.8 %collective-permute-start.13 = (bf16[16,32,512]{2,1,0:T(8,128)(2,1)S(1)}, bf16[16,32,512]{2,1,0:T(8,128)(2,1)S(1)}, u32[]{:S(2)}, u32[]{:S(2)}) collective-permute-start(bf16[16,32,512]{2,1,0:T(8,128)(2,1)S(1)} %all-to-all-done.4.grads_ref), channel_id=1, source_target_pairs={{0,16},{16,0},{32,48},{48,32},{64,80},{80,64},{96,112},{112,96},{1... | collective-permute-start | bytes 1572872 | tf_op jit(solution)/shard_map/ppermute | solution.py:545

commit v6 on v4

--- a/solution.py
+++ b/solution.py
@@ -22,6 +22,8 @@
 SHARED = 16
 LANES = 128
 BLOCKS = D // LANES
+GRANT = 24 * 1024 * 1024
+WIDE_GRANT = 56 * 1024 * 1024
 
 epsilon = 1e-06
 logit_scale = 64.0
@@ -317,15 +319,12 @@
 
 
 def weight_kernel(place_ref, mine_ref, other_ref, out_ref):
-    core, plane_y, plane_x = place_ref[0], place_ref[1], place_ref[2]
+    core, plane = place_ref[0], place_ref[1]
     for ref, half in ((mine_ref, core), (other_ref, 1 - core)):
-        for ky in range(4):
-            for kx in range(4):
-                owner = ((plane_y - ky) & 3) * 4 + ((plane_x - kx) & 3)
-                at = pl.multiple_of(owner * WROWS + half * SHARED, SHARED)
-                first = (ky * 4 + kx) * SHARED
-                rows = ref[first : first + SHARED, :].astype(F32)
-                out_ref[pl.ds(at, SHARED), :] = rows * (1.0 / loss_scale)
+        for p in range(PLANE):
+            at = pl.multiple_of((plane ^ p) * WROWS + half * SHARED, SHARED)
+            rows = ref[p * SHARED : (p + 1) * SHARED, :].astype(F32)
+            out_ref[pl.ds(at, SHARED), :] = rows * (1.0 / loss_scale)
 
 
 def finish_kernel(half_ref, grads_ref, items_ref, *rest):
@@ -345,7 +344,7 @@
     count, width = items.shape
     half_block = pl.BlockSpec((HALF, width), lambda i, half_ref: (half_ref[0], 0))
     operands = [half.reshape(1), grads, items]
-    in_specs = [pl.BlockSpec((CHIPS, PIECE, width), lambda i, half_ref: (0, 0, 0)), half_block]
+    in_specs = [pl.BlockSpec(memory_space=pltpu.VMEM), half_block]
     aliases = {}
     if earlier is not None:
         operands.append(earlier)
@@ -358,12 +357,13 @@
             num_scalar_prefetch=1, grid=(1,), in_specs=in_specs, out_specs=half_block
         ),
         input_output_aliases=aliases,
+        compiler_params=pltpu.CompilerParams(vmem_limit_bytes=GRANT),
         cost_estimate=pl.CostEstimate(flops=0, bytes_accessed=1 << 21, transcendentals=0),
         name="finish",
     )(*operands)
 
 
-def local(kernel, outs, operands, scalars=0, scratch=(), flops=0):
+def local(kernel, outs, operands, scalars=0, scratch=(), grant=GRANT):
     spaces = [pltpu.SMEM] * scalars + [pltpu.VMEM] * (len(operands) - scalars)
     moved = sum(v.size * v.dtype.itemsize for v in operands) + sum(
         v.size * v.dtype.itemsize for v in outs
@@ -374,8 +374,8 @@
         in_specs=[pl.BlockSpec(memory_space=s) for s in spaces],
         out_specs=tuple(pl.BlockSpec(memory_space=pltpu.VMEM) for _ in outs),
         scratch_shapes=list(scratch),
-        compiler_params=pltpu.CompilerParams(vmem_limit_bytes=56 * 1024 * 1024),
-        cost_estimate=pl.CostEstimate(flops=flops, bytes_accessed=moved, transcendentals=0),
+        compiler_params=pltpu.CompilerParams(vmem_limit_bytes=grant),
+        cost_estimate=pl.CostEstimate(flops=0, bytes_accessed=moved, transcendentals=0),
     )(*operands)
 
 
@@ -408,6 +408,7 @@
         ],
         [core_s, index, w_proj, item_rows],
         scalars=1,
+        grant=WIDE_GRANT,
     )
     first_in = exchange(first_out, "shard")
 
@@ -419,6 +420,7 @@
         serve_kernel,
         [shaped((PLANE, CAP, width)), shaped((slots, item_count))],
         [first_in, unit_items],
+        grant=WIDE_GRANT,
     )
     served, first_mine = lax.optimization_barrier((served, first_in))
     looked_up = exchange(served, "shard")
@@ -436,6 +438,7 @@
             pltpu.VMEM((tok_rows, width), BF16),
             pltpu.VMEM((SECTIONS, tok_rows, DH), BF16),
         ],
+        grant=56 * 1024 * 1024,
     )
 
     third_out, grad_out, grad_out_b = local(
@@ -454,6 +457,7 @@
             pltpu.VMEM((tok_rows, width), BF16),
             pltpu.VMEM((tok_rows, width), BF16),
         ],
+        grant=56 * 1024 * 1024,
     )
     third_in = exchange(third_out, "shard")
 
@@ -539,24 +543,19 @@
     )
     mine = exchange(summed, "dp", columns)
 
-    def turned(rows, step_y, step_x):
-        moves = [
-            (y * 4 + x, (y + step_y) % 4 * 4 + (x + step_x) % 4) for y in range(4) for x in range(4)
-        ]
-        return lax.ppermute(rows, "shard", moves)
-
-    w_rows = jnp.concatenate([w_rows] + [turned(w_rows, 0, k) for k in (1, 2, 3)], axis=0)
-    w_rows = jnp.concatenate([w_rows] + [turned(w_rows, k, 0) for k in (1, 2, 3)], axis=0)
+    for k in range(4):
+        others = lax.ppermute(w_rows, "shard", [(i, i ^ (1 << k)) for i in range(PLANE)])
+        w_rows = jnp.concatenate([w_rows, others], axis=0)
     w_other_rows = lax.ppermute(w_rows, "dp", partners)
-    other = lax.ppermute(mine, "dp", partners)
-    item_grads = finish(1 - core, other, item_rows, finish(core, mine, item_rows))
-    w_rows, w_other_rows, item_grads = lax.optimization_barrier((w_rows, w_other_rows, item_grads))
     (weight_grads,) = local(
         weight_kernel,
         [shaped((width, width), F32)],
-        [jnp.stack([core, plane >> 2, plane & 3]), w_rows, w_other_rows],
+        [jnp.stack([core, plane]), w_rows, w_other_rows],
         scalars=1,
     )
+    mine, weight_grads = lax.optimization_barrier((mine, weight_grads))
+    other = lax.ppermute(mine, "dp", partners)
+    item_grads = finish(1 - core, other, item_rows, finish(core, mine, item_rows))
     return (grad_tokens, weight_grads, item_grads)
 
 

time: 245 us -> 229 us (0.935)
  Pallas kernels: 45.5 us -> 30.7 us
  waiting for transfers between devices: 55.4 us -> 67.5 us
  starting transfers between devices: 60.9 us -> 50.8 us
    ppermute x6 -> x4, waiting for transfers between devices: 2.15 us -> 15.1 us  [shards(): lax.ppermute(w_rows, 'shard', [(i, i ^ 1 << k) for i in range(PLANE)])]
    pallas_call x11, Pallas kernels: 40.4 us -> 27.9 us  [local(): pl.pallas_call(kernel, out_shape=tuple(outs), in_specs=[pl.BlockSpec(memo...]
    ppermute x6 -> x4, starting transfers between devices: 17.7 us -> 8.57 us  [shards(): lax.ppermute(w_rows, 'shard', [(i, i ^ 1 << k) for i in range(PLANE)])]
    ppermute x1, starting transfers between devices: 9.13 us -> 2.27 us  [shards(): other = lax.ppermute(mine, 'dp', partners)]
    ppermute x1, starting transfers between devices: 1.92 us -> 7.88 us  [shards(): w_other_rows = lax.ppermute(w_rows, 'dp', partners)]
    all_to_all x4, waiting for transfers between devices: 53.3 us -> 50.4 us  [exchange(): lax.all_to_all(pieces, axis, split_axis=0, concat_axis=0, tiled=True, axi...]
    unnamed x49 -> x42, local copies, waits for them, and re-layouts: 8.42 us -> 6.35 us
  transfers between devices with their start and end apart: 14 -> 12, of which waited for: 5 -> 10; matrix products, arithmetic and copies ran while one was open for 4% -> 5% of each run, Pallas kernels for 6% -> 5%
where the time goes in v6:
time: 229 us; the launch traced here: 228 us
  waiting for transfers between devices  67.5 us (29%)
  starting transfers between devices  50.8 us (22%)
  blocking collectives  47.4 us (21%)
  Pallas kernels  30.7 us (13%)
  matrix products  17.1 us (7%)
  local copies, waits for them, and re-layouts  6.95 us (3%)
  other arithmetic  6.35 us (3%)
    all_to_all x4, waiting for transfers between devices, exchange(): lax.all_to_all(pieces, axis, split_axis=0, concat_axis=0, tiled=True, axi...  50.4 us
    all_to_all x2, blocking collectives, exchange(): lax.all_to_all(pieces, axis, split_axis=0, concat_axis=0, tiled=True, axi...  47.4 us
    pallas_call x11, Pallas kernels, local(): pl.pallas_call(kernel, out_shape=tuple(outs), in_specs=[pl.BlockSpec(memo...  27.9 us
    all_to_all x4, starting transfers between devices, exchange(): lax.all_to_all(pieces, axis, split_axis=0, concat_axis=0, tiled=True, axi...  21.6 us
    dot_general x9, matrix products, dot(): return lax.dot_general(a, b, (contract, batch), preferred_element_type=F32)  17.1 us
    ppermute x4, waiting for transfers between devices, shards(): lax.ppermute(w_rows, 'shard', [(i, i ^ 1 << k) for i in range(PLANE)])  15.1 us
    ppermute x4, starting transfers between devices, shards(): lax.ppermute(w_rows, 'shard', [(i, i ^ 1 << k) for i in range(PLANE)])  8.57 us
    ppermute x1, starting transfers between devices, shards(): w_other_rows = lax.ppermute(w_rows, 'dp', partners)  7.88 us
  transfers between devices with their start and end apart: 12, of which 10 were waited for; matrix products, arithmetic and copies ran while one was open for 5% of the time, Pallas kernels for 5%

profile of v6, /device:TPU:1, one launch (start us, length us, event | category | flops | bytes accessed | tf_op | source)
XLA Modules:
  0.0 227.8 jit_solution(5277467711575125637)
XLA Ops:
  2.7 3.7 %shard_map.103 = (bf16[16,400,128]{2,1,0:T(8,128)(2,1)}, s32[384,1]{1,0:T(8,128)}) custom-call(s32[1]{0:T(128)} %bitcast.core_ref.half_ref, s32[1,832]{1,0:T(1,128)} %reshape.115.index_ref, bf16[512,128]{1,0:T(8,128)(2,1)} %w_ref.1, bf16[1024,512]{1,0:T(8,128)(2,1)} %items_ref.5), custom_call_target="tpu_custom_call" | custom-call | bytes 2822916 | tf_op jit(solution)/shard_map/pallas_call | solution.py:371
  6.4 7.6 %all-to-all-start = ((bf16[16,400,128]{2,1,0:T(8,128)(2,1)}), bf16[16,400,128]{2,1,0:T(8,128)(2,1)S(1)}, u32[]{:S(2)}, u32[]{:S(2)}) async-start(bf16[16,400,128]{2,1,0:T(8,128)(2,1)} %get-tuple-element.31), calls=%async_computation | async-start | bytes 3276800 | tf_op jit(solution)/shard_map/all_to_all | solution.py:64
  14.3 1.3 fusion.4.items_ref
  15.6 18.9 %all-to-all-done.recv_ref.mine_ref = bf16[16,400,128]{2,1,0:T(8,128)(2,1)S(1)} async-done(((bf16[16,400,128]{2,1,0:T(8,128)(2,1)}), bf16[16,400,128]{2,1,0:T(8,128)(2,1)S(1)}, u32[]{:S(2)}, u32[]{:S(2)}) %all-to-all-start) | async-done | bytes 1638432 | tf_op jit(solution)/shard_map/all_to_all | solution.py:64
  34.5 1.2 copy-done.7
  35.7 4.1 %shard_map.104 = (bf16[16,48,512]{2,1,0:T(8,128)(2,1)}, bf16[768,1024]{1,0:T(8,128)(2,1)}) custom-call(bf16[16,400,128]{2,1,0:T(8,128)(2,1)} %copy-done.7, bf16[1024,512]{1,0:T(8,128)(2,1)} %fusion.4.items_ref), custom_call_target="tpu_custom_call" | custom-call | bytes 5046272 | tf_op jit(solution)/shard_map/pallas_call | solution.py:371
  39.8 6.8 %collective-permute-start = (bf16[16,400,128]{2,1,0:T(8,128)(2,1)}, bf16[16,400,128]{2,1,0:T(8,128)(2,1)S(1)}, u32[]{:S(2)}, u32[]{:S(2)}) collective-permute-start(bf16[16,400,128]{2,1,0:T(8,128)(2,1)} %copy-done.7), channel_id=1, source_target_pairs={{0,16},{16,0},{32,48},{48,32},{64,80},{80,64},{96,112},{112,96},{1... | collective-permute-start | bytes 4915208 | tf_op jit(solution)/shard_map/ppermute | solution.py:427
  46.6 3.8 %all-to-all-start.1 = ((bf16[16,48,512]{2,1,0:T(8,128)(2,1)}), bf16[16,48,512]{2,1,0:T(8,128)(2,1)S(1)}, u32[]{:S(2)}, u32[]{:S(2)}) async-start(bf16[16,48,512]{2,1,0:T(8,128)(2,1)} %get-tuple-element.38), calls=%async_computation.1 | async-start | bytes 1572864 | tf_op jit(solution)/shard_map/all_to_all | solution.py:64
  50.7 0.8 fusion.24
  51.5 1.2 copy-done.8
  52.7 7.5 %shard_map.105 = (f32[384,512]{1,0:T(8,128)}, bf16[4,384,128]{2,1,0:T(8,128)(2,1)}, bf16[16,512,128]{2,1,0:T(8,128)(2,1)}) custom-call(s32[1]{0:T(128)} %bitcast.core_ref.half_ref, s32[1,4]{1,0:T(1,128)} %lengths_ref.1, bf16[384,512]{1,0:T(8,128)(2,1)} %tokens_ref.3, bf16[16,400,128]{2,1,0:T(8,128)(2,1)} %copy-done.7, bf16[16,400,128]{2,1,0:T(8,128)(2,1)} %copy-done.8, ...), custom_call_target="tpu_custom_call" | custom-call | bytes 7471124 | tf_op jit(solution)/shard_map/pallas_call | solution.py:371
  60.1 4.8 %all-to-all-done.1.recv_ref = bf16[16,48,512]{2,1,0:T(8,128)(2,1)S(1)} async-done(((bf16[16,48,512]{2,1,0:T(8,128)(2,1)}), bf16[16,48,512]{2,1,0:T(8,128)(2,1)S(1)}, u32[]{:S(2)}, u32[]{:S(2)}) %all-to-all-start.1) | async-done | bytes 786464 | tf_op jit(solution)/shard_map/all_to_all | solution.py:64
  64.9 0.9 copy-done.10
  65.8 8.3 %shard_map.106 = (bf16[16,144,512]{2,1,0:T(8,128)(2,1)}, f32[384,512]{1,0:T(8,128)}, bf16[384,512]{1,0:T(8,128)(2,1)}) custom-call(s32[1]{0:T(128)} %bitcast.core_ref.half_ref, f32[384,512]{1,0:T(8,128)} %get-tuple-element.36.layer_ref, bf16[4,384,128]{2,1,0:T(8,128)(2,1)} %get-tuple-element.37.gated_ref, bf16[16,48,512]{2,1,0:T(8,128)(2,1)} %copy-done.10, ...), custom_call_target="tpu_custom_call" | custom-call | bytes 8783364 | tf_op jit(solution)/shard_map/pallas_call | solution.py:371
  74.1 1.0 copy-done.4
  75.3 3.5 %multiply_convert_fusion = (bf16[16,384,128]{1,2,0:T(8,128)(2,1)S(1)}, f32[16,384,128]{1,2,0:T(8,128)}) fusion(bf16[16,512,128]{2,1,0:T(8,128)(2,1)S(1)} %copy-done.18, bf16[384,512]{1,0:T(8,128)(2,1)S(1)} %shard_map.107), kind=kOutput, calls=%fused_computation.2 | convolution fusion | flops 809238528 | bytes 7208960 | tf_op jit(solution)/shard_map/dot_general | solution.py:38
  78.8 1.1 select_convert_fusion.1
  81.7 1.2 fusion.16
  82.8 1.3 fusion.35
  84.1 2.5 %select_convert_fusion = bf16[4,384,384]{2,1,0:T(8,128)(2,1)} fusion(f32[4,384,384]{2,1,0:T(8,128)S(1)} %get-tuple-element.72, bf16[4,384,128]{1,2,0:T(8,128)(2,1)S(1)} %get-tuple-element.64, pred[384,384]{1,0:T(8,128)(4,1)S(1)} %copy-done.16, bf16[16,384,128]{1,2,0:T(8,128)(2,1)S(1)} %get-tuple-element.69), kind=kOutput, calls=%fused_computation.8 | convolution fusion | flops 158662656 | bytes 4472832 | tf_op jit(solution)/shard_map/dot_general | solution.py:38
  86.6 3.9 %all-to-all-start.2 = ((bf16[16,144,512]{2,1,0:T(8,128)(2,1)}), bf16[16,144,512]{2,1,0:T(8,128)(2,1)S(1)}, u32[]{:S(2)}, u32[]{:S(2)}) async-start(bf16[16,144,512]{2,1,0:T(8,128)(2,1)} %get-tuple-element.40), calls=%async_computation.2 | async-start | bytes 4718592 | tf_op jit(solution)/shard_map/all_to_all | solution.py:64
  90.6 2.0 fusion.29
  92.7 1.4 fusion.25
  94.1 4.2 %fusion.10 = (f32[384]{0:T(512)S(1)}, f32[384]{0:T(512)S(1)}, f32[384,512]{1,0:T(8,128)S(1)}) fusion(bf16[384,512]{1,0:T(8,128)(2,1)S(1)} %copy-done.3, bf16[16,512,128]{2,1,0:T(8,128)(2,1)} %get-tuple-element.47, f32[4,384,128]{1,2,0:T(8,128)S(1)} %fusion.25, f32[4,384,128]{1,2,0:T(8,128)S(1)} %fusion.29, f32[4,384,128]{1,2,0:T(8,128)S(1)} %copy-done.15, ...), kind=kOutput, calls=%fused_computation.23 | convolution fusion | flops 815725824 | bytes 9571328 | tf_op jit(solution)/shard_map/dot_general | solution.py:38
  98.3 1.0 fusion.14
  99.3 26.6 %all-to-all-done.2.recv_ref = bf16[16,144,512]{2,1,0:T(8,128)(2,1)S(1)} async-done(((bf16[16,144,512]{2,1,0:T(8,128)(2,1)}), bf16[16,144,512]{2,1,0:T(8,128)(2,1)S(1)}, u32[]{:S(2)}, u32[]{:S(2)}) %all-to-all-start.2) | async-done | bytes 2359328 | tf_op jit(solution)/shard_map/all_to_all | solution.py:64
  126.0 1.4 copy-done.1
  127.4 0.9 shard_map.108
  128.3 3.6 %collective-permute-start.1 = (bf16[528,512]{1,0:T(8,128)(2,1)S(1)}, bf16[528,512]{1,0:T(8,128)(2,1)S(1)}, u32[]{:S(2)}, u32[]{:S(2)}) collective-permute-start(bf16[528,512]{1,0:T(8,128)(2,1)S(1)} %get-tuple-element.54), channel_id=1, source_target_pairs={{0,16},{16,0},{32,48},{48,32},{64,80},{80,64},{96,112},{112,96},{1... | collective-permute-start | bytes 1622024 | tf_op jit(solution)/shard_map/ppermute | solution.py:526
  132.6 0.8 collective-permute-done.1.other_ref
  133.6 21.6 %all_to_all.30.recv_ref = bf16[4,144,512]{2,1,0:T(8,128)(2,1)S(1)} all-to-all(bf16[4,144,512]{2,1,0:T(8,128)(2,1)S(1)} %shard_map.110), channel_id=1, replica_groups={{0,32,64,96},{16,48,80,112},{128,160,192,224},{144,176,208,240},{256,28..., dimensions={0} | all-to-all | bytes 1179648 | tf_op jit(solution)/shard_map/all_to_all | solution.py:64
  155.3 25.7 %all_to_all.31.recv_ref = bf16[4,48,512]{2,1,0:T(8,128)(2,1)S(1)} all-to-all(bf16[4,48,512]{2,1,0:T(8,128)(2,1)S(1)} %shard_map.111), channel_id=1, replica_groups={{0,128,256,384},{16,144,272,400},{32,160,288,416},{48,176,304,432},{64,..., dimensions={0} | all-to-all | bytes 393216 | tf_op jit(solution)/shard_map/all_to_all | solution.py:64
  181.0 0.9 shard_map.112
  181.8 6.3 %all-to-all-start.5 = ((bf16[16,32,512]{2,1,0:T(8,128)(2,1)}), bf16[16,32,512]{2,1,0:T(8,128)(2,1)S(1)}, u32[]{:S(2)}, u32[]{:S(2)}) async-start(bf16[16,32,512]{2,1,0:T(8,128)(2,1)} %get-tuple-element.55), calls=%async_computation.5 | async-start | bytes 1048576 | tf_op jit(solution)/shard_map/all_to_all | solution.py:64
  188.2 1.9 collective-permute-start.2
  190.1 2.6 %collective-permute-done.2 = bf16[16,512]{1,0:T(8,128)(2,1)S(1)} collective-permute-done((bf16[16,512]{1,0:T(8,128)(2,1)S(1)}, bf16[16,512]{1,0:T(8,128)(2,1)S(1)}, u32[]{:S(2)}, u32[]{:S(2)}) %collective-permute-start.2) | collective-permute-done | bytes 16416 | tf_op jit(solution)/shard_map/ppermute | solution.py:547
  192.7 1.9 collective-permute-start.3
  194.6 4.5 %collective-permute-done.3 = bf16[32,512]{1,0:T(8,128)(2,1)S(1)} collective-permute-done((bf16[32,512]{1,0:T(8,128)(2,1)S(1)}, bf16[32,512]{1,0:T(8,128)(2,1)S(1)}, u32[]{:S(2)}, u32[]{:S(2)}) %collective-permute-start.3) | collective-permute-done | bytes 32800 | tf_op jit(solution)/shard_map/ppermute | solution.py:547
  199.1 1.9 collective-permute-start.4
  201.0 3.4 %collective-permute-done.4 = bf16[64,512]{1,0:T(8,128)(2,1)S(1)} collective-permute-done((bf16[64,512]{1,0:T(8,128)(2,1)S(1)}, bf16[64,512]{1,0:T(8,128)(2,1)S(1)}, u32[]{:S(2)}, u32[]{:S(2)}) %collective-permute-start.4) | collective-permute-done | bytes 65568 | tf_op jit(solution)/shard_map/ppermute | solution.py:547
  204.4 2.8 %collective-permute-start.5 = (bf16[128,512]{1,0:T(8,128)(2,1)S(1)}, bf16[128,512]{1,0:T(8,128)(2,1)S(1)}, u32[]{:S(2)}, u32[]{:S(2)}) collective-permute-start(bf16[128,512]{1,0:T(8,128)(2,1)S(1)} %pad_maximum_fusion), channel_id=1, source_target_pairs={{0,8},{1,9},{2,10},{3,11},{4,12},{5,13},{6,14},{7,15},{8,0},{9,1},... | collective-permute-start | bytes 393224 | tf_op jit(solution)/shard_map/ppermute | solution.py:547
  207.3 4.6 %collective-permute-done.5 = bf16[128,512]{1,0:T(8,128)(2,1)S(1)} collective-permute-done((bf16[128,512]{1,0:T(8,128)(2,1)S(1)}, bf16[128,512]{1,0:T(8,128)(2,1)S(1)}, u32[]{:S(2)}, u32[]{:S(2)}) %collective-permute-start.5) | collective-permute-done | bytes 131104 | tf_op jit(solution)/shard_map/ppermute | solution.py:547
  211.9 7.9 %collective-permute-start.6 = (bf16[256,512]{1,0:T(8,128)(2,1)S(1)}, bf16[256,512]{1,0:T(8,128)(2,1)S(1)}, u32[]{:S(2)}, u32[]{:S(2)}) collective-permute-start(bf16[256,512]{1,0:T(8,128)(2,1)S(1)} %constant_dynamic-update-slice_fusion.mine_ref), channel_id=1, source_target_pairs={{0,16},{16,0},{32,48},{48,32},{64,80},{80,64},{96,112},{112,96},{1... | collective-permute-start | bytes 786440 | tf_op jit(solution)/shard_map/ppermute | solution.py:549
  219.9 1.1 collective-permute-done.6.other_ref
  221.0 1.6 shard_map.113
  222.6 2.3 collective-permute-start.7
  224.9 1.4 finish.2.rest_0_
  226.4 1.4 finish.3
  (62 shorter events, 5.7 us)
Async XLA Ops:
  0.6 13.4 %copy-start = (bf16[1024,512]{1,0:T(8,128)(2,1)S(1)}, bf16[1024,512]{1,0:T(8,128)(2,1)}, u32[]{:S(2)}) copy-start(bf16[1024,512]{1,0:T(8,128)(2,1)} %items_ref.5) | copy-start | bytes 3145732
  6.4 28.1 %all-to-all-start = ((bf16[16,400,128]{2,1,0:T(8,128)(2,1)}), bf16[16,400,128]{2,1,0:T(8,128)(2,1)S(1)}, u32[]{:S(2)}, u32[]{:S(2)}) async-start(bf16[16,400,128]{2,1,0:T(8,128)(2,1)} %get-tuple-element.31), calls=%async_computation | async-start | bytes 3276800 | tf_op jit(solution)/shard_map/all_to_all | solution.py:64
  15.6 34.8 %copy-start.17 = (s32[1,4]{1,0:T(1,128)S(1)}, s32[1,4]{1,0:T(1,128)}, u32[]{:S(2)}) copy-start(s32[1,4]{1,0:T(1,128)} %lengths_ref.1) | copy-start | bytes 52
  34.5 1.2 copy-start.7
  39.8 11.7 %collective-permute-start = (bf16[16,400,128]{2,1,0:T(8,128)(2,1)}, bf16[16,400,128]{2,1,0:T(8,128)(2,1)S(1)}, u32[]{:S(2)}, u32[]{:S(2)}) collective-permute-start(bf16[16,400,128]{2,1,0:T(8,128)(2,1)} %copy-done.7), channel_id=1, source_target_pairs={{0,16},{16,0},{32,48},{48,32},{64,80},{80,64},{96,112},{112,96},{1... | collective-permute-start | bytes 4915208 | tf_op jit(solution)/shard_map/ppermute | solution.py:427
  46.6 18.3 %all-to-all-start.1 = ((bf16[16,48,512]{2,1,0:T(8,128)(2,1)}), bf16[16,48,512]{2,1,0:T(8,128)(2,1)S(1)}, u32[]{:S(2)}, u32[]{:S(2)}) async-start(bf16[16,48,512]{2,1,0:T(8,128)(2,1)} %get-tuple-element.38), calls=%async_computation.1 | async-start | bytes 1572864 | tf_op jit(solution)/shard_map/all_to_all | solution.py:64
  51.5 1.2 copy-start.8
  64.9 0.9 copy-start.10
  65.8 8.3 %copy-start.2 = (bf16[384,512]{1,0:T(8,128)(2,1)S(1)}, bf16[384,512]{1,0:T(8,128)(2,1)}, u32[]{:S(2)}) copy-start(bf16[384,512]{1,0:T(8,128)(2,1)} %tokens_ref.3) | copy-start | bytes 1179652
  65.8 9.4 %copy-start.18 = (bf16[16,512,128]{2,1,0:T(8,128)(2,1)S(1)}, bf16[16,512,128]{2,1,0:T(8,128)(2,1)}, u32[]{:S(2)}) copy-start(bf16[16,512,128]{2,1,0:T(8,128)(2,1)} %get-tuple-element.47) | copy-start | bytes 6291460
  74.1 1.0 copy-start.4
  75.3 3.5 %copy-start.16 = (pred[384,384]{1,0:T(8,128)(4,1)S(1)}, pred[384,384]{1,0:T(8,128)(4,1)}, u32[]{:S(2)}) copy-start(pred[384,384]{1,0:T(8,128)(4,1)} %fusion.24) | copy-start | bytes 442372
  78.8 5.4 %copy-start.12 = (bf16[16,384,128]{1,2,0:T(8,128)(2,1)}, bf16[16,384,128]{1,2,0:T(8,128)(2,1)S(1)}, u32[]{:S(2)}) copy-start(bf16[16,384,128]{1,2,0:T(8,128)(2,1)S(1)} %get-tuple-element.69) | copy-start | bytes 4718596
  78.8 1.3 copy-start.5
  78.8 1.7 copy-start.11
  86.6 39.3 %all-to-all-start.2 = ((bf16[16,144,512]{2,1,0:T(8,128)(2,1)}), bf16[16,144,512]{2,1,0:T(8,128)(2,1)S(1)}, u32[]{:S(2)}, u32[]{:S(2)}) async-start(bf16[16,144,512]{2,1,0:T(8,128)(2,1)} %get-tuple-element.40), calls=%async_computation.2 | async-start | bytes 4718592 | tf_op jit(solution)/shard_map/all_to_all | solution.py:64
  90.6 2.1 copy-start.9
  90.6 3.5 %copy-start.3 = (bf16[384,512]{1,0:T(8,128)(2,1)S(1)}, bf16[384,512]{1,0:T(8,128)(2,1)}, u32[]{:S(2)}) copy-start(bf16[384,512]{1,0:T(8,128)(2,1)} %tokens_ref.3) | copy-start | bytes 1179652
  90.6 3.5 %copy-start.14 = (f32[4,384,128]{1,2,0:T(8,128)S(1)}, f32[4,384,128]{1,2,0:T(8,128)}, u32[]{:S(2)}) copy-start(f32[4,384,128]{1,2,0:T(8,128)} %get-tuple-element.63) | copy-start | bytes 2359300
  90.6 3.5 %copy-start.15 = (f32[4,384,128]{1,2,0:T(8,128)S(1)}, f32[4,384,128]{1,2,0:T(8,128)}, u32[]{:S(2)}) copy-start(f32[4,384,128]{1,2,0:T(8,128)} %fusion.35) | copy-start | bytes 2359300
  94.1 4.2 %copy-start.13 = (f32[384,512]{1,0:T(8,128)S(1)}, f32[384,512]{1,0:T(8,128)}, u32[]{:S(2)}) copy-start(f32[384,512]{1,0:T(8,128)} %get-tuple-element.41) | copy-start | bytes 2359300
  98.3 27.7 %copy-start.6 = (s32[64]{0:T(128)S(1)}, s32[64]{0:T(128)}, u32[]{:S(2)}) copy-start(s32[64]{0:T(128)} %param.15) | copy-start | bytes 772
  126.0 1.4 copy-start.1
  128.3 5.2 %collective-permute-start.1 = (bf16[528,512]{1,0:T(8,128)(2,1)S(1)}, bf16[528,512]{1,0:T(8,128)(2,1)S(1)}, u32[]{:S(2)}, u32[]{:S(2)}) collective-permute-start(bf16[528,512]{1,0:T(8,128)(2,1)S(1)} %get-tuple-element.54), channel_id=1, source_target_pairs={{0,16},{16,0},{32,48},{48,32},{64,80},{80,64},{96,112},{112,96},{1... | collective-permute-start | bytes 1622024 | tf_op jit(solution)/shard_map/ppermute | solution.py:526
  181.8 40.7 %all-to-all-start.5 = ((bf16[16,32,512]{2,1,0:T(8,128)(2,1)}), bf16[16,32,512]{2,1,0:T(8,128)(2,1)S(1)}, u32[]{:S(2)}, u32[]{:S(2)}) async-start(bf16[16,32,512]{2,1,0:T(8,128)(2,1)} %get-tuple-element.55), calls=%async_computation.5 | async-start | bytes 1048576 | tf_op jit(solution)/shard_map/all_to_all | solution.py:64
  188.2 4.5 %collective-permute-start.2 = (bf16[16,512]{1,0:T(8,128)(2,1)S(1)}, bf16[16,512]{1,0:T(8,128)(2,1)S(1)}, u32[]{:S(2)}, u32[]{:S(2)}) collective-permute-start(bf16[16,512]{1,0:T(8,128)(2,1)S(1)} %get-tuple-element.56), channel_id=1, source_target_pairs={{0,1},{1,0},{2,3},{3,2},{4,5},{5,4},{6,7},{7,6},{8,9},{9,8},{10,11... | collective-permute-start | bytes 49160 | tf_op jit(solution)/shard_map/ppermute | solution.py:547
  192.7 6.4 %collective-permute-start.3 = (bf16[32,512]{1,0:T(8,128)(2,1)S(1)}, bf16[32,512]{1,0:T(8,128)(2,1)S(1)}, u32[]{:S(2)}, u32[]{:S(2)}) collective-permute-start(bf16[32,512]{1,0:T(8,128)(2,1)S(1)} %pad_maximum_fusion.2), channel_id=1, source_target_pairs={{0,2},{1,3},{2,0},{3,1},{4,6},{5,7},{6,4},{7,5},{8,10},{9,11},{10,... | collective-permute-start | bytes 98312 | tf_op jit(solution)/shard_map/ppermute | solution.py:547
  199.1 5.3 %collective-permute-start.4 = (bf16[64,512]{1,0:T(8,128)(2,1)S(1)}, bf16[64,512]{1,0:T(8,128)(2,1)S(1)}, u32[]{:S(2)}, u32[]{:S(2)}) collective-permute-start(bf16[64,512]{1,0:T(8,128)(2,1)S(1)} %pad_maximum_fusion.1), channel_id=1, source_target_pairs={{0,4},{1,5},{2,6},{3,7},{4,0},{5,1},{6,2},{7,3},{8,12},{9,13},{10,... | collective-permute-start | bytes 196616 | tf_op jit(solution)/shard_map/ppermute | solution.py:547
  204.4 7.5 %collective-permute-start.5 = (bf16[128,512]{1,0:T(8,128)(2,1)S(1)}, bf16[128,512]{1,0:T(8,128)(2,1)S(1)}, u32[]{:S(2)}, u32[]{:S(2)}) collective-permute-start(bf16[128,512]{1,0:T(8,128)(2,1)S(1)} %pad_maximum_fusion), channel_id=1, source_target_pairs={{0,8},{1,9},{2,10},{3,11},{4,12},{5,13},{6,14},{7,15},{8,0},{9,1},... | collective-permute-start | bytes 393224 | tf_op jit(solution)/shard_map/ppermute | solution.py:547
  211.9 9.0 %collective-permute-start.6 = (bf16[256,512]{1,0:T(8,128)(2,1)S(1)}, bf16[256,512]{1,0:T(8,128)(2,1)S(1)}, u32[]{:S(2)}, u32[]{:S(2)}) collective-permute-start(bf16[256,512]{1,0:T(8,128)(2,1)S(1)} %constant_dynamic-update-slice_fusion.mine_ref), channel_id=1, source_target_pairs={{0,16},{16,0},{32,48},{48,32},{64,80},{80,64},{96,112},{112,96},{1... | collective-permute-start | bytes 786440 | tf_op jit(solution)/shard_map/ppermute | solution.py:549
  222.6 3.8 %collective-permute-start.7 = (bf16[16,32,512]{2,1,0:T(8,128)(2,1)S(1)}, bf16[16,32,512]{2,1,0:T(8,128)(2,1)S(1)}, u32[]{:S(2)}, u32[]{:S(2)}) collective-permute-start(bf16[16,32,512]{2,1,0:T(8,128)(2,1)S(1)} %all-to-all-done.5.grads_ref), channel_id=1, source_target_pairs={{0,16},{16,0},{32,48},{48,32},{64,80},{80,64},{96,112},{112,96},{1... | collective-permute-start | bytes 1572872 | tf_op jit(solution)/shard_map/ppermute | solution.py:557

commit v7 on v6

--- a/solution.py
+++ b/solution.py
@@ -22,6 +22,7 @@
 SHARED = 16
 LANES = 128
 BLOCKS = D // LANES
+CHAIN_BITS = ((1, 2, 4, 8), (4, 8, 1, 2))
 GRANT = 24 * 1024 * 1024
 WIDE_GRANT = 56 * 1024 * 1024
 
@@ -124,8 +125,14 @@
         normed_ref[c : c + step, :] = (wide * scale).astype(BF16)
 
 
-def norm_kernel(tokens_ref, after_ref, normed_ref):
+def norm_kernel(core_ref, tokens_ref, mine_ref, other_ref, after_ref, normed_ref, w_all_ref):
     normalize(tokens_ref, normed_ref)
+    core = core_ref[0]
+    half = w_all_ref.shape[1] // 2
+    for ref, part in ((mine_ref, core), (other_ref, 1 - core)):
+        at = pl.multiple_of(part * half, half)
+        for j in range(SECTIONS):
+            w_all_ref[j, pl.ds(at, half), :] = ref[j, 0:half, :]
 
 
 def forward_kernel(
@@ -137,7 +144,6 @@
     w_out_ref,
     layer_ref,
     gated_ref,
-    w_all_ref,
     normed,
     act,
 ):
@@ -148,10 +154,6 @@
     normalize(tokens_ref, normed)
     left = normed[:, pl.ds(pl.multiple_of(core * half, half), half)]
     right = normed[:, pl.ds(pl.multiple_of((1 - core) * half, half), half)]
-    for ref, part in ((mine_ref, core), (other_ref, 1 - core)):
-        at = pl.multiple_of(part * half, half)
-        for j in range(SECTIONS):
-            w_all_ref[j, pl.ds(at, half), :] = ref[j, 0:half, :]
     for j in range(0, SECTIONS, 2):
         w_left = jnp.concatenate([mine_ref[j, 0:half, :], mine_ref[j + 1, 0:half, :]], axis=1)
         w_right = jnp.concatenate([other_ref[j, 0:half, :], other_ref[j + 1, 0:half, :]], axis=1)
@@ -321,10 +323,13 @@
 def weight_kernel(place_ref, mine_ref, other_ref, out_ref):
     core, plane = place_ref[0], place_ref[1]
     for ref, half in ((mine_ref, core), (other_ref, 1 - core)):
-        for p in range(PLANE):
-            at = pl.multiple_of((plane ^ p) * WROWS + half * SHARED, SHARED)
-            rows = ref[p * SHARED : (p + 1) * SHARED, :].astype(F32)
-            out_ref[pl.ds(at, SHARED), :] = rows * (1.0 / loss_scale)
+        for n, bits in enumerate(CHAIN_BITS):
+            for p in range(PLANE):
+                mask = sum(bit for k, bit in enumerate(bits) if p >> k & 1)
+                at = (plane ^ mask) * WROWS + half * SHARED + n * (SHARED // 2)
+                first = (n * PLANE + p) * (SHARED // 2)
+                rows = ref[first : first + SHARED // 2, :].astype(F32)
+                out_ref[pl.ds(pl.multiple_of(at, 8), SHARED // 2), :] = rows * (1.0 / loss_scale)
 
 
 def finish_kernel(half_ref, grads_ref, items_ref, *rest):
@@ -425,12 +430,11 @@
     served, first_mine = lax.optimization_barrier((served, first_in))
     looked_up = exchange(served, "shard")
     first_other = lax.ppermute(first_mine, "dp", partners)
-    layer_out, gated, w_all = local(
+    layer_out, gated = local(
         forward_kernel,
         [
             shaped((tok_rows, width), F32),
             shaped((HEADS, tok_rows, DH)),
-            shaped((SECTIONS, width, DH)),
         ],
         [core_s, lengths, tokens, first_mine, first_other, w_out],
         scalars=2,
@@ -461,7 +465,12 @@
     )
     third_in = exchange(third_out, "shard")
 
-    (normed,) = local(norm_kernel, [shaped((tok_rows, width))], [tokens, grad_out_b])
+    normed, w_all = local(
+        norm_kernel,
+        [shaped((tok_rows, width)), shaped((SECTIONS, width, DH))],
+        [core_s, tokens, first_mine, first_other, grad_out_b],
+        scalars=1,
+    )
     grad_out_b, w_all, normed, tokens = lax.optimization_barrier(
         (grad_out_b, w_all, normed, tokens)
     )
@@ -543,9 +552,15 @@
     )
     mine = exchange(summed, "dp", columns)
 
+    chains = [w_rows[: SHARED // 2], w_rows[SHARED // 2 :]]
     for k in range(4):
-        others = lax.ppermute(w_rows, "shard", [(i, i ^ (1 << k)) for i in range(PLANE)])
-        w_rows = jnp.concatenate([w_rows, others], axis=0)
+        for n, bits in enumerate(CHAIN_BITS):
+            others = lax.ppermute(
+                chains[n], "shard", [(i, i ^ bits[k]) for i in range(PLANE)]
+            )
+            chains[n] = jnp.concatenate([chains[n], others], axis=0)
+    w_rows = jnp.concatenate(chains, axis=0)
+    mine, w_rows = lax.optimization_barrier((mine, w_rows))
     w_other_rows = lax.ppermute(w_rows, "dp", partners)
     (weight_grads,) = local(
         weight_kernel,
@@ -553,7 +568,6 @@
         [jnp.stack([core, plane]), w_rows, w_other_rows],
         scalars=1,
     )
-    mine, weight_grads = lax.optimization_barrier((mine, weight_grads))
     other = lax.ppermute(mine, "dp", partners)
     item_grads = finish(1 - core, other, item_rows, finish(core, mine, item_rows))
     return (grad_tokens, weight_grads, item_grads)

time: 229 us -> 229 us (level)
  starting transfers between devices: 50.8 us -> 65.3 us
  waiting for transfers between devices: 67.5 us -> 56.8 us
    ppermute x4 -> x8, starting transfers between devices: 8.57 us -> 23.9 us  [shards(): lax.ppermute(chains[n], 'shard', [(i, i ^ bits[k]) for i in range(PLANE)])]
    ppermute x4 -> x8, waiting for transfers between devices: 15.1 us -> 3.75 us  [shards(): lax.ppermute(chains[n], 'shard', [(i, i ^ bits[k]) for i in range(PLANE)])]
    ppermute x1, starting transfers between devices: 7.88 us -> 1.92 us  [shards(): w_other_rows = lax.ppermute(w_rows, 'dp', partners)]
    ppermute x1, starting transfers between devices: 2.27 us -> 6.7 us  [shards(): other = lax.ppermute(mine, 'dp', partners)]
    unnamed x42 -> x44, local copies, waits for them, and re-layouts: 6.35 us -> 4.61 us
  transfers between devices with their start and end apart: 12 -> 16, of which waited for: 10 -> 7; matrix products, arithmetic and copies ran while one was open for 5% -> 5% of each run, Pallas kernels for 5% -> 5%
where the time goes in v7:
time: 229 us; the launch traced here: 228 us
  starting transfers between devices  65.3 us (29%)
  waiting for transfers between devices  56.8 us (25%)
  blocking collectives  47.2 us (21%)
  Pallas kernels  31.7 us (14%)
  matrix products  15.1 us (7%)
  other arithmetic  5.5 us (2%)
  local copies, waits for them, and re-layouts  5.21 us (2%)
    all_to_all x4, waiting for transfers between devices, exchange(): lax.all_to_all(pieces, axis, split_axis=0, concat_axis=0, tiled=True, axi...  52.2 us
    all_to_all x2, blocking collectives, exchange(): lax.all_to_all(pieces, axis, split_axis=0, concat_axis=0, tiled=True, axi...  47.2 us
    pallas_call x11, Pallas kernels, local(): pl.pallas_call(kernel, out_shape=tuple(outs), in_specs=[pl.BlockSpec(memo...  29 us
    ppermute x8, starting transfers between devices, shards(): lax.ppermute(chains[n], 'shard', [(i, i ^ bits[k]) for i in range(PLANE)])  23.9 us
    all_to_all x4, starting transfers between devices, exchange(): lax.all_to_all(pieces, axis, split_axis=0, concat_axis=0, tiled=True, axi...  22.4 us
    dot_general x9, matrix products, dot(): return lax.dot_general(a, b, (contract, batch), preferred_element_type=F32)  15.1 us
    ppermute x1, starting transfers between devices, shards(): first_other = lax.ppermute(first_mine, 'dp', partners)  6.83 us
    ppermute x1, starting transfers between devices, shards(): other = lax.ppermute(mine, 'dp', partners)  6.7 us
  transfers between devices with their start and end apart: 16, of which 7 were waited for; matrix products, arithmetic and copies ran while one was open for 5% of the time, Pallas kernels for 5%

profile of v7, /device:TPU:1, one launch (start us, length us, event | category | flops | bytes accessed | tf_op | source)
XLA Modules:
  0.0 228.1 jit_solution(10955080387327077525)
XLA Ops:
  0.6 0.8 reduce
  2.7 3.7 %shard_map.103 = (bf16[16,400,128]{2,1,0:T(8,128)(2,1)}, s32[384,1]{1,0:T(8,128)}) custom-call(s32[1]{0:T(128)} %bitcast.core_ref.half_ref, s32[1,832]{1,0:T(1,128)} %reshape.115.index_ref, bf16[512,128]{1,0:T(8,128)(2,1)} %w_ref.1, bf16[1024,512]{1,0:T(8,128)(2,1)} %items_ref.5), custom_call_target="tpu_custom_call" | custom-call | bytes 2822916 | tf_op jit(solution)/shard_map/pallas_call | solution.py:376
  6.4 7.6 %all-to-all-start = ((bf16[16,400,128]{2,1,0:T(8,128)(2,1)}), bf16[16,400,128]{2,1,0:T(8,128)(2,1)S(1)}, u32[]{:S(2)}, u32[]{:S(2)}) async-start(bf16[16,400,128]{2,1,0:T(8,128)(2,1)} %get-tuple-element.32), calls=%async_computation | async-start | bytes 3276800 | tf_op jit(solution)/shard_map/all_to_all | solution.py:65
  14.3 1.3 fusion.4.items_ref
  15.6 18.9 %all-to-all-done.recv_ref.mine_ref = bf16[16,400,128]{2,1,0:T(8,128)(2,1)S(1)} async-done(((bf16[16,400,128]{2,1,0:T(8,128)(2,1)}), bf16[16,400,128]{2,1,0:T(8,128)(2,1)S(1)}, u32[]{:S(2)}, u32[]{:S(2)}) %all-to-all-start) | async-done | bytes 1638432 | tf_op jit(solution)/shard_map/all_to_all | solution.py:65
  34.5 1.2 copy-done
  35.7 4.1 %shard_map.104 = (bf16[16,48,512]{2,1,0:T(8,128)(2,1)}, bf16[768,1024]{1,0:T(8,128)(2,1)}) custom-call(bf16[16,400,128]{2,1,0:T(8,128)(2,1)} %copy-done, bf16[1024,512]{1,0:T(8,128)(2,1)} %fusion.4.items_ref), custom_call_target="tpu_custom_call" | custom-call | bytes 5046272 | tf_op jit(solution)/shard_map/pallas_call | solution.py:376
  39.7 6.8 %collective-permute-start = (bf16[16,400,128]{2,1,0:T(8,128)(2,1)}, bf16[16,400,128]{2,1,0:T(8,128)(2,1)S(1)}, u32[]{:S(2)}, u32[]{:S(2)}) collective-permute-start(bf16[16,400,128]{2,1,0:T(8,128)(2,1)} %copy-done), channel_id=1, source_target_pairs={{0,16},{16,0},{32,48},{48,32},{64,80},{80,64},{96,112},{112,96},{1... | collective-permute-start | bytes 4915208 | tf_op jit(solution)/shard_map/ppermute | solution.py:432
  46.5 3.8 %all-to-all-start.1 = ((bf16[16,48,512]{2,1,0:T(8,128)(2,1)}), bf16[16,48,512]{2,1,0:T(8,128)(2,1)S(1)}, u32[]{:S(2)}, u32[]{:S(2)}) async-start(bf16[16,48,512]{2,1,0:T(8,128)(2,1)} %get-tuple-element.39), calls=%async_computation.1 | async-start | bytes 1572864 | tf_op jit(solution)/shard_map/all_to_all | solution.py:65
  50.6 0.8 fusion.24
  51.4 1.2 copy-done.3
  52.7 6.7 %shard_map.105 = (f32[384,512]{1,0:T(8,128)}, bf16[4,384,128]{2,1,0:T(8,128)(2,1)}) custom-call(s32[1]{0:T(128)} %bitcast.core_ref.half_ref, s32[1,4]{1,0:T(1,128)} %lengths_ref.1, bf16[384,512]{1,0:T(8,128)(2,1)} %tokens_ref.3, bf16[16,400,128]{2,1,0:T(8,128)(2,1)} %copy-done, bf16[16,400,128]{2,1,0:T(8,128)(2,1)} %copy-done.3, bf16[512,512]{1,0:T(8,128)(2,1)} %w_out_ref.1), custom_call_target="tpu_custom_call" | custom-call | bytes 5373972 | tf_op jit(solution)/shard_map/pallas_call | solution.py:376
  59.4 5.5 %all-to-all-done.1.recv_ref = bf16[16,48,512]{2,1,0:T(8,128)(2,1)S(1)} async-done(((bf16[16,48,512]{2,1,0:T(8,128)(2,1)}), bf16[16,48,512]{2,1,0:T(8,128)(2,1)S(1)}, u32[]{:S(2)}, u32[]{:S(2)}) %all-to-all-start.1) | async-done | bytes 786464 | tf_op jit(solution)/shard_map/all_to_all | solution.py:65
  64.9 0.9 copy-done.11
  65.8 8.3 %shard_map.106 = (bf16[16,144,512]{2,1,0:T(8,128)(2,1)}, f32[384,512]{1,0:T(8,128)}, bf16[384,512]{1,0:T(8,128)(2,1)}) custom-call(s32[1]{0:T(128)} %bitcast.core_ref.half_ref, f32[384,512]{1,0:T(8,128)} %get-tuple-element.37.layer_ref, bf16[4,384,128]{2,1,0:T(8,128)(2,1)} %get-tuple-element.38.gated_ref, bf16[16,48,512]{2,1,0:T(8,128)(2,1)} %copy-done.11, ...), custom_call_target="tpu_custom_call" | custom-call | bytes 8783364 | tf_op jit(solution)/shard_map/pallas_call | solution.py:376
  74.1 1.0 copy-done.7
  75.4 3.5 %multiply_convert_fusion = (bf16[16,384,128]{1,2,0:T(8,128)(2,1)S(1)}, f32[16,384,128]{1,2,0:T(8,128)}) fusion(bf16[16,512,128]{2,1,0:T(8,128)(2,1)S(1)} %get-tuple-element.49, bf16[384,512]{1,0:T(8,128)(2,1)S(1)} %get-tuple-element.48), kind=kOutput, calls=%fused_computation.2 | convolution fusion | flops 809238528 | bytes 7208960 | tf_op jit(solution)/shard_map/dot_general | solution.py:39
  78.9 1.1 select_convert_fusion.1
  81.7 1.3 fusion.36
  83.0 1.5 select_convert_fusion
  84.5 4.7 %all-to-all-start.2 = ((bf16[16,144,512]{2,1,0:T(8,128)(2,1)}), bf16[16,144,512]{2,1,0:T(8,128)(2,1)}, u32[]{:S(2)}, u32[]{:S(2)}) async-start(bf16[16,144,512]{2,1,0:T(8,128)(2,1)} %get-tuple-element.41), calls=%async_computation.2 | async-start | bytes 4718592 | tf_op jit(solution)/shard_map/all_to_all | solution.py:65
  89.2 1.6 fusion.29
  90.9 1.4 fusion.25
  92.3 3.5 %fusion.10 = (f32[384]{0:T(512)S(1)}, f32[384]{0:T(512)S(1)}, f32[384,512]{1,0:T(8,128)S(1)}) fusion(bf16[384,512]{1,0:T(8,128)(2,1)S(1)} %copy-done.6, bf16[16,512,128]{2,1,0:T(8,128)(2,1)S(1)} %copy-done.10, f32[4,384,128]{1,2,0:T(8,128)S(1)} %fusion.25, f32[4,384,128]{1,2,0:T(8,128)S(1)} %fusion.29, f32[4,384,128]{1,2,0:T(8,128)S(1)} %copy-done.15, ...), kind=kOutput, calls=%fused_computation.23 | convolution fusion | flops 815725824 | bytes 9571328 | tf_op jit(solution)/shard_map/dot_general | solution.py:39
  95.9 1.0 fusion.14
  96.9 27.8 %all-to-all-done.2.recv_ref = bf16[16,144,512]{2,1,0:T(8,128)(2,1)} async-done(((bf16[16,144,512]{2,1,0:T(8,128)(2,1)}), bf16[16,144,512]{2,1,0:T(8,128)(2,1)}, u32[]{:S(2)}, u32[]{:S(2)}) %all-to-all-start.2) | async-done | bytes 2359328 | tf_op jit(solution)/shard_map/all_to_all | solution.py:65
  124.7 2.6 %shard_map.108 = (bf16[528,512]{1,0:T(8,128)(2,1)S(1)}, bf16[768,512]{1,0:T(8,128)(2,1)S(1)}, bf16[64,512]{1,0:T(8,128)(2,1)S(1)}, f32[32,512]{1,0:T(8,128)S(1)}) custom-call(s32[1]{0:T(128)} %bitcast.core_ref.half_ref, bf16[16,144,512]{2,1,0:T(8,128)(2,1)} %all-to-all-done.2.recv_ref, bf16[768,1024]{1,0:T(8,128)(2,1)S(1)} %copy-done.5, s32[1,64]{1,0:T(1,128)S(1)} %bitcast.20), custom_call_target="tpu_custom_call" | custom-call | bytes 5390596 | tf_op jit(solution)/shard_map/pallas_call | solution.py:376
  127.2 3.6 %collective-permute-start.1 = (bf16[528,512]{1,0:T(8,128)(2,1)S(1)}, bf16[528,512]{1,0:T(8,128)(2,1)S(1)}, u32[]{:S(2)}, u32[]{:S(2)}) collective-permute-start(bf16[528,512]{1,0:T(8,128)(2,1)S(1)} %get-tuple-element.56), channel_id=1, source_target_pairs={{0,16},{16,0},{32,48},{48,32},{64,80},{80,64},{96,112},{112,96},{1... | collective-permute-start | bytes 1622024 | tf_op jit(solution)/shard_map/ppermute | solution.py:535
  131.5 0.8 collective-permute-done.1.other_ref
  132.5 21.7 %all_to_all.30.recv_ref = bf16[4,144,512]{2,1,0:T(8,128)(2,1)S(1)} all-to-all(bf16[4,144,512]{2,1,0:T(8,128)(2,1)S(1)} %shard_map.110), channel_id=1, replica_groups={{0,32,64,96},{16,48,80,112},{128,160,192,224},{144,176,208,240},{256,28..., dimensions={0} | all-to-all | bytes 1179648 | tf_op jit(solution)/shard_map/all_to_all | solution.py:65
  154.2 25.6 %all_to_all.31.recv_ref = bf16[4,48,512]{2,1,0:T(8,128)(2,1)S(1)} all-to-all(bf16[4,48,512]{2,1,0:T(8,128)(2,1)S(1)} %shard_map.111), channel_id=1, replica_groups={{0,128,256,384},{16,144,272,400},{32,160,288,416},{48,176,304,432},{64,..., dimensions={0} | all-to-all | bytes 393216 | tf_op jit(solution)/shard_map/all_to_all | solution.py:65
  179.8 0.9 shard_map.112
  180.7 6.3 %all-to-all-start.5 = ((bf16[16,32,512]{2,1,0:T(8,128)(2,1)}), bf16[16,32,512]{2,1,0:T(8,128)(2,1)S(1)}, u32[]{:S(2)}, u32[]{:S(2)}) async-start(bf16[16,32,512]{2,1,0:T(8,128)(2,1)} %get-tuple-element.57), calls=%async_computation.5 | async-start | bytes 1048576 | tf_op jit(solution)/shard_map/all_to_all | solution.py:65
  187.0 1.9 collective-permute-start.6
  188.9 1.9 collective-permute-start.2
  191.4 3.8 %collective-permute-start.7 = (bf16[16,512]{1,0:T(8,128)(2,1)S(1)}, bf16[16,512]{1,0:T(8,128)(2,1)S(1)}, u32[]{:S(2)}, u32[]{:S(2)}) collective-permute-start(bf16[16,512]{1,0:T(8,128)(2,1)S(1)} %pad_maximum_fusion.5), channel_id=1, source_target_pairs={{0,8},{1,9},{2,10},{3,11},{4,12},{5,13},{6,14},{7,15},{8,0},{9,1},... | collective-permute-start | bytes 49160 | tf_op jit(solution)/shard_map/ppermute | solution.py:558
  195.2 2.7 %collective-permute-start.3 = (bf16[16,512]{1,0:T(8,128)(2,1)S(1)}, bf16[16,512]{1,0:T(8,128)(2,1)S(1)}, u32[]{:S(2)}, u32[]{:S(2)}) collective-permute-start(bf16[16,512]{1,0:T(8,128)(2,1)S(1)} %pad_maximum_fusion.4), channel_id=1, source_target_pairs={{0,2},{1,3},{2,0},{3,1},{4,6},{5,7},{6,4},{7,5},{8,10},{9,11},{10,... | collective-permute-start | bytes 49160 | tf_op jit(solution)/shard_map/ppermute | solution.py:558
  198.0 2.6 %collective-permute-start.8 = (bf16[32,512]{1,0:T(8,128)(2,1)S(1)}, bf16[32,512]{1,0:T(8,128)(2,1)S(1)}, u32[]{:S(2)}, u32[]{:S(2)}) collective-permute-start(bf16[32,512]{1,0:T(8,128)(2,1)S(1)} %pad_maximum_fusion.3), channel_id=1, source_target_pairs={{0,1},{1,0},{2,3},{3,2},{4,5},{5,4},{6,7},{7,6},{8,9},{9,8},{10,11... | collective-permute-start | bytes 98312 | tf_op jit(solution)/shard_map/ppermute | solution.py:558
  200.6 0.9 collective-permute-done.3
  201.5 2.4 %collective-permute-start.4 = (bf16[32,512]{1,0:T(8,128)(2,1)S(1)}, bf16[32,512]{1,0:T(8,128)(2,1)S(1)}, u32[]{:S(2)}, u32[]{:S(2)}) collective-permute-start(bf16[32,512]{1,0:T(8,128)(2,1)S(1)} %pad_maximum_fusion.2), channel_id=1, source_target_pairs={{0,4},{1,5},{2,6},{3,7},{4,0},{5,1},{6,2},{7,3},{8,12},{9,13},{10,... | collective-permute-start | bytes 98312 | tf_op jit(solution)/shard_map/ppermute | solution.py:558
  204.0 4.0 %collective-permute-start.9 = (bf16[64,512]{1,0:T(8,128)(2,1)S(1)}, bf16[64,512]{1,0:T(8,128)(2,1)S(1)}, u32[]{:S(2)}, u32[]{:S(2)}) collective-permute-start(bf16[64,512]{1,0:T(8,128)(2,1)S(1)} %pad_maximum_fusion.1), channel_id=1, source_target_pairs={{0,2},{1,3},{2,0},{3,1},{4,6},{5,7},{6,4},{7,5},{8,10},{9,11},{10,... | collective-permute-start | bytes 196616 | tf_op jit(solution)/shard_map/ppermute | solution.py:558
  208.0 4.5 %collective-permute-start.5 = (bf16[64,512]{1,0:T(8,128)(2,1)S(1)}, bf16[64,512]{1,0:T(8,128)(2,1)S(1)}, u32[]{:S(2)}, u32[]{:S(2)}) collective-permute-start(bf16[64,512]{1,0:T(8,128)(2,1)S(1)} %pad_maximum_fusion), channel_id=1, source_target_pairs={{0,8},{1,9},{2,10},{3,11},{4,12},{5,13},{6,14},{7,15},{8,0},{9,1},... | collective-permute-start | bytes 196616 | tf_op jit(solution)/shard_map/ppermute | solution.py:558
  212.6 2.2 collective-permute-done.5
  214.9 6.7 %collective-permute-start.11 = (bf16[16,32,512]{2,1,0:T(8,128)(2,1)S(1)}, bf16[16,32,512]{2,1,0:T(8,128)(2,1)S(1)}, u32[]{:S(2)}, u32[]{:S(2)}) collective-permute-start(bf16[16,32,512]{2,1,0:T(8,128)(2,1)S(1)} %all-to-all-done.5.grads_ref), channel_id=1, source_target_pairs={{0,16},{16,0},{32,48},{48,32},{64,80},{80,64},{96,112},{112,96},{1... | collective-permute-start | bytes 1572872 | tf_op jit(solution)/shard_map/ppermute | solution.py:571
  221.6 1.9 collective-permute-start.10
  223.7 1.4 finish.2.rest_0_
  225.1 1.6 shard_map.113
  226.7 1.4 finish.3
  (76 shorter events, 5.5 us)
Async XLA Ops:
  0.6 13.4 %copy-start.2 = (bf16[1024,512]{1,0:T(8,128)(2,1)S(1)}, bf16[1024,512]{1,0:T(8,128)(2,1)}, u32[]{:S(2)}) copy-start(bf16[1024,512]{1,0:T(8,128)(2,1)} %items_ref.5) | copy-start | bytes 3145732
  6.4 28.1 %all-to-all-start = ((bf16[16,400,128]{2,1,0:T(8,128)(2,1)}), bf16[16,400,128]{2,1,0:T(8,128)(2,1)S(1)}, u32[]{:S(2)}, u32[]{:S(2)}) async-start(bf16[16,400,128]{2,1,0:T(8,128)(2,1)} %get-tuple-element.32), calls=%async_computation | async-start | bytes 3276800 | tf_op jit(solution)/shard_map/all_to_all | solution.py:65
  15.6 34.8 %copy-start.17 = (s32[1,4]{1,0:T(1,128)S(1)}, s32[1,4]{1,0:T(1,128)}, u32[]{:S(2)}) copy-start(s32[1,4]{1,0:T(1,128)} %lengths_ref.1) | copy-start | bytes 52
  34.5 1.2 copy-start
  39.7 11.7 %collective-permute-start = (bf16[16,400,128]{2,1,0:T(8,128)(2,1)}, bf16[16,400,128]{2,1,0:T(8,128)(2,1)S(1)}, u32[]{:S(2)}, u32[]{:S(2)}) collective-permute-start(bf16[16,400,128]{2,1,0:T(8,128)(2,1)} %copy-done), channel_id=1, source_target_pairs={{0,16},{16,0},{32,48},{48,32},{64,80},{80,64},{96,112},{112,96},{1... | collective-permute-start | bytes 4915208 | tf_op jit(solution)/shard_map/ppermute | solution.py:432
  46.5 18.3 %all-to-all-start.1 = ((bf16[16,48,512]{2,1,0:T(8,128)(2,1)}), bf16[16,48,512]{2,1,0:T(8,128)(2,1)S(1)}, u32[]{:S(2)}, u32[]{:S(2)}) async-start(bf16[16,48,512]{2,1,0:T(8,128)(2,1)} %get-tuple-element.39), calls=%async_computation.1 | async-start | bytes 1572864 | tf_op jit(solution)/shard_map/all_to_all | solution.py:65
  51.4 1.2 copy-start.3
  64.9 0.9 copy-start.11
  65.8 8.3 %copy-start.1 = (bf16[16,400,128]{2,1,0:T(8,128)(2,1)S(1)}, bf16[16,400,128]{2,1,0:T(8,128)(2,1)}, u32[]{:S(2)}) copy-start(bf16[16,400,128]{2,1,0:T(8,128)(2,1)} %copy-done) | copy-start | bytes 4915204
  65.8 8.3 %copy-start.4 = (bf16[16,400,128]{2,1,0:T(8,128)(2,1)S(1)}, bf16[16,400,128]{2,1,0:T(8,128)(2,1)}, u32[]{:S(2)}) copy-start(bf16[16,400,128]{2,1,0:T(8,128)(2,1)} %copy-done.3) | copy-start | bytes 4915204
  65.8 8.3 %copy-start.6 = (bf16[384,512]{1,0:T(8,128)(2,1)S(1)}, bf16[384,512]{1,0:T(8,128)(2,1)}, u32[]{:S(2)}) copy-start(bf16[384,512]{1,0:T(8,128)(2,1)} %tokens_ref.3) | copy-start | bytes 1179652
  74.1 1.0 copy-start.7
  75.3 3.5 %copy-start.9 = (bf16[16,512,128]{2,1,0:T(8,128)(2,1)}, bf16[16,512,128]{2,1,0:T(8,128)(2,1)S(1)}, u32[]{:S(2)}) copy-start(bf16[16,512,128]{2,1,0:T(8,128)(2,1)S(1)} %get-tuple-element.49) | copy-start | bytes 6291460
  75.4 3.5 %copy-start.16 = (pred[384,384]{1,0:T(8,128)(4,1)S(1)}, pred[384,384]{1,0:T(8,128)(4,1)}, u32[]{:S(2)}) copy-start(pred[384,384]{1,0:T(8,128)(4,1)} %fusion.24) | copy-start | bytes 442372
  78.9 4.2 %copy-start.13 = (bf16[16,384,128]{1,2,0:T(8,128)(2,1)}, bf16[16,384,128]{1,2,0:T(8,128)(2,1)S(1)}, u32[]{:S(2)}) copy-start(bf16[16,384,128]{1,2,0:T(8,128)(2,1)S(1)} %get-tuple-element.74) | copy-start | bytes 4718596
  78.9 1.4 copy-start.12
  84.5 40.2 %all-to-all-start.2 = ((bf16[16,144,512]{2,1,0:T(8,128)(2,1)}), bf16[16,144,512]{2,1,0:T(8,128)(2,1)}, u32[]{:S(2)}, u32[]{:S(2)}) async-start(bf16[16,144,512]{2,1,0:T(8,128)(2,1)} %get-tuple-element.41), calls=%async_computation.2 | async-start | bytes 4718592 | tf_op jit(solution)/shard_map/all_to_all | solution.py:65
  89.2 3.1 %copy-start.10 = (bf16[16,512,128]{2,1,0:T(8,128)(2,1)S(1)}, bf16[16,512,128]{2,1,0:T(8,128)(2,1)}, u32[]{:S(2)}) copy-start(bf16[16,512,128]{2,1,0:T(8,128)(2,1)} %copy-done.9) | copy-start | bytes 6291460
  89.2 3.1 %copy-start.15 = (f32[4,384,128]{1,2,0:T(8,128)S(1)}, f32[4,384,128]{1,2,0:T(8,128)}, u32[]{:S(2)}) copy-start(f32[4,384,128]{1,2,0:T(8,128)} %fusion.36) | copy-start | bytes 2359300
  92.3 3.6 %copy-start.14 = (f32[384,512]{1,0:T(8,128)S(1)}, f32[384,512]{1,0:T(8,128)}, u32[]{:S(2)}) copy-start(f32[384,512]{1,0:T(8,128)} %get-tuple-element.42) | copy-start | bytes 2359300
  95.8 28.8 %copy-start.5 = (bf16[768,1024]{1,0:T(8,128)(2,1)S(1)}, bf16[768,1024]{1,0:T(8,128)(2,1)}, u32[]{:S(2)}) copy-start(bf16[768,1024]{1,0:T(8,128)(2,1)} %get-tuple-element.51.pick_ref) | copy-start | bytes 4718596
  95.8 28.8 %copy-start.8 = (s32[64]{0:T(128)S(1)}, s32[64]{0:T(128)}, u32[]{:S(2)}) copy-start(s32[64]{0:T(128)} %param.15) | copy-start | bytes 772
  127.2 5.2 %collective-permute-start.1 = (bf16[528,512]{1,0:T(8,128)(2,1)S(1)}, bf16[528,512]{1,0:T(8,128)(2,1)S(1)}, u32[]{:S(2)}, u32[]{:S(2)}) collective-permute-start(bf16[528,512]{1,0:T(8,128)(2,1)S(1)} %get-tuple-element.56), channel_id=1, source_target_pairs={{0,16},{16,0},{32,48},{48,32},{64,80},{80,64},{96,112},{112,96},{1... | collective-permute-start | bytes 1622024 | tf_op jit(solution)/shard_map/ppermute | solution.py:535
  180.7 34.2 %all-to-all-start.5 = ((bf16[16,32,512]{2,1,0:T(8,128)(2,1)}), bf16[16,32,512]{2,1,0:T(8,128)(2,1)S(1)}, u32[]{:S(2)}, u32[]{:S(2)}) async-start(bf16[16,32,512]{2,1,0:T(8,128)(2,1)} %get-tuple-element.57), calls=%async_computation.5 | async-start | bytes 1048576 | tf_op jit(solution)/shard_map/all_to_all | solution.py:65
  187.0 4.4 %collective-permute-start.6 = (bf16[8,512]{1,0:T(8,128)(2,1)S(1)}, bf16[8,512]{1,0:T(8,128)(2,1)S(1)}, u32[]{:S(2)}, u32[]{:S(2)}) collective-permute-start(bf16[8,512]{1,0:T(8,128)(2,1)S(1)} %get-tuple-element.67), channel_id=1, source_target_pairs={{0,4},{1,5},{2,6},{3,7},{4,0},{5,1},{6,2},{7,3},{8,12},{9,13},{10,... | collective-permute-start | bytes 24584 | tf_op jit(solution)/shard_map/ppermute | solution.py:558
  188.9 6.3 %collective-permute-start.2 = (bf16[8,512]{1,0:T(8,128)(2,1)S(1)}, bf16[8,512]{1,0:T(8,128)(2,1)S(1)}, u32[]{:S(2)}, u32[]{:S(2)}) collective-permute-start(bf16[8,512]{1,0:T(8,128)(2,1)S(1)} %get-tuple-element.69), channel_id=1, source_target_pairs={{0,1},{1,0},{2,3},{3,2},{4,5},{5,4},{6,7},{7,6},{8,9},{9,8},{10,11... | collective-permute-start | bytes 24584 | tf_op jit(solution)/shard_map/ppermute | solution.py:558
  191.4 6.5 %collective-permute-start.7 = (bf16[16,512]{1,0:T(8,128)(2,1)S(1)}, bf16[16,512]{1,0:T(8,128)(2,1)S(1)}, u32[]{:S(2)}, u32[]{:S(2)}) collective-permute-start(bf16[16,512]{1,0:T(8,128)(2,1)S(1)} %pad_maximum_fusion.5), channel_id=1, source_target_pairs={{0,8},{1,9},{2,10},{3,11},{4,12},{5,13},{6,14},{7,15},{8,0},{9,1},... | collective-permute-start | bytes 49160 | tf_op jit(solution)/shard_map/ppermute | solution.py:558
  195.2 6.3 %collective-permute-start.3 = (bf16[16,512]{1,0:T(8,128)(2,1)S(1)}, bf16[16,512]{1,0:T(8,128)(2,1)S(1)}, u32[]{:S(2)}, u32[]{:S(2)}) collective-permute-start(bf16[16,512]{1,0:T(8,128)(2,1)S(1)} %pad_maximum_fusion.4), channel_id=1, source_target_pairs={{0,2},{1,3},{2,0},{3,1},{4,6},{5,7},{6,4},{7,5},{8,10},{9,11},{10,... | collective-permute-start | bytes 49160 | tf_op jit(solution)/shard_map/ppermute | solution.py:558
  198.0 6.0 %collective-permute-start.8 = (bf16[32,512]{1,0:T(8,128)(2,1)S(1)}, bf16[32,512]{1,0:T(8,128)(2,1)S(1)}, u32[]{:S(2)}, u32[]{:S(2)}) collective-permute-start(bf16[32,512]{1,0:T(8,128)(2,1)S(1)} %pad_maximum_fusion.3), channel_id=1, source_target_pairs={{0,1},{1,0},{2,3},{3,2},{4,5},{5,4},{6,7},{7,6},{8,9},{9,8},{10,11... | collective-permute-start | bytes 98312 | tf_op jit(solution)/shard_map/ppermute | solution.py:558
  201.5 6.5 %collective-permute-start.4 = (bf16[32,512]{1,0:T(8,128)(2,1)S(1)}, bf16[32,512]{1,0:T(8,128)(2,1)S(1)}, u32[]{:S(2)}, u32[]{:S(2)}) collective-permute-start(bf16[32,512]{1,0:T(8,128)(2,1)S(1)} %pad_maximum_fusion.2), channel_id=1, source_target_pairs={{0,4},{1,5},{2,6},{3,7},{4,0},{5,1},{6,2},{7,3},{8,12},{9,13},{10,... | collective-permute-start | bytes 98312 | tf_op jit(solution)/shard_map/ppermute | solution.py:558
  204.0 10.9 %collective-permute-start.9 = (bf16[64,512]{1,0:T(8,128)(2,1)S(1)}, bf16[64,512]{1,0:T(8,128)(2,1)S(1)}, u32[]{:S(2)}, u32[]{:S(2)}) collective-permute-start(bf16[64,512]{1,0:T(8,128)(2,1)S(1)} %pad_maximum_fusion.1), channel_id=1, source_target_pairs={{0,2},{1,3},{2,0},{3,1},{4,6},{5,7},{6,4},{7,5},{8,10},{9,11},{10,... | collective-permute-start | bytes 196616 | tf_op jit(solution)/shard_map/ppermute | solution.py:558
  208.0 6.8 %collective-permute-start.5 = (bf16[64,512]{1,0:T(8,128)(2,1)S(1)}, bf16[64,512]{1,0:T(8,128)(2,1)S(1)}, u32[]{:S(2)}, u32[]{:S(2)}) collective-permute-start(bf16[64,512]{1,0:T(8,128)(2,1)S(1)} %pad_maximum_fusion), channel_id=1, source_target_pairs={{0,8},{1,9},{2,10},{3,11},{4,12},{5,13},{6,14},{7,15},{8,0},{9,1},... | collective-permute-start | bytes 196616 | tf_op jit(solution)/shard_map/ppermute | solution.py:558
  214.9 11.8 %collective-permute-start.11 = (bf16[16,32,512]{2,1,0:T(8,128)(2,1)S(1)}, bf16[16,32,512]{2,1,0:T(8,128)(2,1)S(1)}, u32[]{:S(2)}, u32[]{:S(2)}) collective-permute-start(bf16[16,32,512]{2,1,0:T(8,128)(2,1)S(1)} %all-to-all-done.5.grads_ref), channel_id=1, source_target_pairs={{0,16},{16,0},{32,48},{48,32},{64,80},{80,64},{96,112},{112,96},{1... | collective-permute-start | bytes 1572872 | tf_op jit(solution)/shard_map/ppermute | solution.py:571
  221.6 3.4 %collective-permute-start.10 = (bf16[256,512]{1,0:T(8,128)(2,1)S(1)}, bf16[256,512]{1,0:T(8,128)(2,1)S(1)}, u32[]{:S(2)}, u32[]{:S(2)}) collective-permute-start(bf16[256,512]{1,0:T(8,128)(2,1)S(1)} %constant_dynamic-update-slice_fusion.mine_ref), channel_id=1, source_target_pairs={{0,16},{16,0},{32,48},{48,32},{64,80},{80,64},{96,112},{112,96},{1... | collective-permute-start | bytes 786440 | tf_op jit(solution)/shard_map/ppermute | solution.py:564

commit v8 on v4

--- a/solution.py
+++ b/solution.py
@@ -22,6 +22,8 @@
 SHARED = 16
 LANES = 128
 BLOCKS = D // LANES
+GRANT = 24 * 1024 * 1024
+WIDE_GRANT = 56 * 1024 * 1024
 
 epsilon = 1e-06
 logit_scale = 64.0
@@ -122,8 +124,14 @@
         normed_ref[c : c + step, :] = (wide * scale).astype(BF16)
 
 
-def norm_kernel(tokens_ref, after_ref, normed_ref):
+def norm_kernel(core_ref, tokens_ref, mine_ref, other_ref, after_ref, normed_ref, w_all_ref):
     normalize(tokens_ref, normed_ref)
+    core = core_ref[0]
+    half = w_all_ref.shape[1] // 2
+    for ref, part in ((mine_ref, core), (other_ref, 1 - core)):
+        at = pl.multiple_of(part * half, half)
+        for j in range(SECTIONS):
+            w_all_ref[j, pl.ds(at, half), :] = ref[j, 0:half, :]
 
 
 def forward_kernel(
@@ -135,7 +143,6 @@
     w_out_ref,
     layer_ref,
     gated_ref,
-    w_all_ref,
     normed,
     act,
 ):
@@ -146,10 +153,6 @@
     normalize(tokens_ref, normed)
     left = normed[:, pl.ds(pl.multiple_of(core * half, half), half)]
     right = normed[:, pl.ds(pl.multiple_of((1 - core) * half, half), half)]
-    for ref, part in ((mine_ref, core), (other_ref, 1 - core)):
-        at = pl.multiple_of(part * half, half)
-        for j in range(SECTIONS):
-            w_all_ref[j, pl.ds(at, half), :] = ref[j, 0:half, :]
     for j in range(0, SECTIONS, 2):
         w_left = jnp.concatenate([mine_ref[j, 0:half, :], mine_ref[j + 1, 0:half, :]], axis=1)
         w_right = jnp.concatenate([other_ref[j, 0:half, :], other_ref[j + 1, 0:half, :]], axis=1)
@@ -345,7 +348,7 @@
     count, width = items.shape
     half_block = pl.BlockSpec((HALF, width), lambda i, half_ref: (half_ref[0], 0))
     operands = [half.reshape(1), grads, items]
-    in_specs = [pl.BlockSpec((CHIPS, PIECE, width), lambda i, half_ref: (0, 0, 0)), half_block]
+    in_specs = [pl.BlockSpec(memory_space=pltpu.VMEM), half_block]
     aliases = {}
     if earlier is not None:
         operands.append(earlier)
@@ -358,12 +361,13 @@
             num_scalar_prefetch=1, grid=(1,), in_specs=in_specs, out_specs=half_block
         ),
         input_output_aliases=aliases,
+        compiler_params=pltpu.CompilerParams(vmem_limit_bytes=GRANT),
         cost_estimate=pl.CostEstimate(flops=0, bytes_accessed=1 << 21, transcendentals=0),
         name="finish",
     )(*operands)
 
 
-def local(kernel, outs, operands, scalars=0, scratch=(), flops=0):
+def local(kernel, outs, operands, scalars=0, scratch=(), grant=GRANT):
     spaces = [pltpu.SMEM] * scalars + [pltpu.VMEM] * (len(operands) - scalars)
     moved = sum(v.size * v.dtype.itemsize for v in operands) + sum(
         v.size * v.dtype.itemsize for v in outs
@@ -374,8 +378,8 @@
         in_specs=[pl.BlockSpec(memory_space=s) for s in spaces],
         out_specs=tuple(pl.BlockSpec(memory_space=pltpu.VMEM) for _ in outs),
         scratch_shapes=list(scratch),
-        compiler_params=pltpu.CompilerParams(vmem_limit_bytes=56 * 1024 * 1024),
-        cost_estimate=pl.CostEstimate(flops=flops, bytes_accessed=moved, transcendentals=0),
+        compiler_params=pltpu.CompilerParams(vmem_limit_bytes=grant),
+        cost_estimate=pl.CostEstimate(flops=0, bytes_accessed=moved, transcendentals=0),
     )(*operands)
 
 
@@ -408,6 +412,7 @@
         ],
         [core_s, index, w_proj, item_rows],
         scalars=1,
+        grant=WIDE_GRANT,
     )
     first_in = exchange(first_out, "shard")
 
@@ -419,16 +424,16 @@
         serve_kernel,
         [shaped((PLANE, CAP, width)), shaped((slots, item_count))],
         [first_in, unit_items],
+        grant=WIDE_GRANT,
     )
     served, first_mine = lax.optimization_barrier((served, first_in))
     looked_up = exchange(served, "shard")
     first_other = lax.ppermute(first_mine, "dp", partners)
-    layer_out, gated, w_all = local(
+    layer_out, gated = local(
         forward_kernel,
         [
             shaped((tok_rows, width), F32),
             shaped((HEADS, tok_rows, DH)),
-            shaped((SECTIONS, width, DH)),
         ],
         [core_s, lengths, tokens, first_mine, first_other, w_out],
         scalars=2,
@@ -436,6 +441,7 @@
             pltpu.VMEM((tok_rows, width), BF16),
             pltpu.VMEM((SECTIONS, tok_rows, DH), BF16),
         ],
+        grant=24 * 1024 * 1024,
     )
 
     third_out, grad_out, grad_out_b = local(
@@ -454,10 +460,16 @@
             pltpu.VMEM((tok_rows, width), BF16),
             pltpu.VMEM((tok_rows, width), BF16),
         ],
+        grant=24 * 1024 * 1024,
     )
     third_in = exchange(third_out, "shard")
 
-    (normed,) = local(norm_kernel, [shaped((tok_rows, width))], [tokens, grad_out_b])
+    normed, w_all = local(
+        norm_kernel,
+        [shaped((tok_rows, width)), shaped((SECTIONS, width, DH))],
+        [core_s, tokens, first_mine, first_other, grad_out_b],
+        scalars=1,
+    )
     grad_out_b, w_all, normed, tokens = lax.optimization_barrier(
         (grad_out_b, w_all, normed, tokens)
     )

time: 245 us -> 227 us (0.927)
  Pallas kernels: 45.5 us -> 29.4 us
  waiting for transfers between devices: 55.4 us -> 58.7 us
    pallas_call x11, Pallas kernels: 40.4 us -> 26.7 us  [local(): pl.pallas_call(kernel, out_shape=tuple(outs), in_specs=[pl.BlockSpec(memo...]
    all_to_all x4, waiting for transfers between devices: 53.3 us -> 56 us  [exchange(): lax.all_to_all(pieces, axis, split_axis=0, concat_axis=0, tiled=True, axi...]
    unnamed x49 -> x45, local copies, waits for them, and re-layouts: 8.42 us -> 6.89 us
  transfers between devices with their start and end apart: 14 -> 14, of which waited for: 5 -> 6; matrix products, arithmetic and copies ran while one was open for 4% -> 5% of each run, Pallas kernels for 6% -> 4%
where the time goes in v8:
time: 227 us; the launch traced here: 226 us
  starting transfers between devices  61.5 us (27%)
  waiting for transfers between devices  58.7 us (26%)
  blocking collectives  47.2 us (21%)
  Pallas kernels  29.4 us (13%)
  matrix products  15.1 us (7%)
  local copies, waits for them, and re-layouts  7.49 us (3%)
  other arithmetic  5.48 us (2%)
    all_to_all x4, waiting for transfers between devices, exchange(): lax.all_to_all(pieces, axis, split_axis=0, concat_axis=0, tiled=True, axi...  56 us
    all_to_all x2, blocking collectives, exchange(): lax.all_to_all(pieces, axis, split_axis=0, concat_axis=0, tiled=True, axi...  47.2 us
    pallas_call x11, Pallas kernels, local(): pl.pallas_call(kernel, out_shape=tuple(outs), in_specs=[pl.BlockSpec(memo...  26.7 us
    all_to_all x4, starting transfers between devices, exchange(): lax.all_to_all(pieces, axis, split_axis=0, concat_axis=0, tiled=True, axi...  23.1 us
    ppermute x6, starting transfers between devices, turned(): return lax.ppermute(rows, 'shard', moves)  17.6 us
    dot_general x9, matrix products, dot(): return lax.dot_general(a, b, (contract, batch), preferred_element_type=F32)  15.1 us
    ppermute x1, starting transfers between devices, shards(): other = lax.ppermute(mine, 'dp', partners)  8.39 us
    ppermute x1, starting transfers between devices, shards(): first_other = lax.ppermute(first_mine, 'dp', partners)  6.96 us
  transfers between devices with their start and end apart: 14, of which 6 were waited for; matrix products, arithmetic and copies ran while one was open for 5% of the time, Pallas kernels for 4%

profile of v8, /device:TPU:1, one launch (start us, length us, event | category | flops | bytes accessed | tf_op | source)
XLA Modules:
  0.0 226.1 jit_solution(17261812402476413667)
XLA Ops:
  2.7 3.7 %shard_map.103 = (bf16[16,400,128]{2,1,0:T(8,128)(2,1)}, s32[384,1]{1,0:T(8,128)}) custom-call(s32[1]{0:T(128)} %bitcast.core_ref.half_ref, s32[1,832]{1,0:T(1,128)} %reshape.115.index_ref, bf16[512,128]{1,0:T(8,128)(2,1)} %w_ref.1, bf16[1024,512]{1,0:T(8,128)(2,1)} %items_ref.5), custom_call_target="tpu_custom_call" | custom-call | bytes 2822916 | tf_op jit(solution)/shard_map/pallas_call | solution.py:375
  6.4 7.6 %all-to-all-start = ((bf16[16,400,128]{2,1,0:T(8,128)(2,1)}), bf16[16,400,128]{2,1,0:T(8,128)(2,1)S(1)}, u32[]{:S(2)}, u32[]{:S(2)}) async-start(bf16[16,400,128]{2,1,0:T(8,128)(2,1)} %get-tuple-element.33), calls=%async_computation | async-start | bytes 3276800 | tf_op jit(solution)/shard_map/all_to_all | solution.py:64
  14.3 1.3 fusion.4.items_ref
  15.6 18.9 %all-to-all-done.recv_ref.mine_ref = bf16[16,400,128]{2,1,0:T(8,128)(2,1)S(1)} async-done(((bf16[16,400,128]{2,1,0:T(8,128)(2,1)}), bf16[16,400,128]{2,1,0:T(8,128)(2,1)S(1)}, u32[]{:S(2)}, u32[]{:S(2)}) %all-to-all-start) | async-done | bytes 1638432 | tf_op jit(solution)/shard_map/all_to_all | solution.py:64
  34.5 1.2 copy-done
  35.7 4.1 %shard_map.104 = (bf16[16,48,512]{2,1,0:T(8,128)(2,1)}, bf16[768,1024]{1,0:T(8,128)(2,1)}) custom-call(bf16[16,400,128]{2,1,0:T(8,128)(2,1)} %copy-done, bf16[1024,512]{1,0:T(8,128)(2,1)} %fusion.4.items_ref), custom_call_target="tpu_custom_call" | custom-call | bytes 5046272 | tf_op jit(solution)/shard_map/pallas_call | solution.py:375
  39.7 7.0 %collective-permute-start = (bf16[16,400,128]{2,1,0:T(8,128)(2,1)}, bf16[16,400,128]{2,1,0:T(8,128)(2,1)}, u32[]{:S(2)}, u32[]{:S(2)}) collective-permute-start(bf16[16,400,128]{2,1,0:T(8,128)(2,1)} %copy-done), channel_id=1, source_target_pairs={{0,16},{16,0},{32,48},{48,32},{64,80},{80,64},{96,112},{112,96},{1... | collective-permute-start | bytes 4915208 | tf_op jit(solution)/shard_map/ppermute | solution.py:431
  46.7 4.5 %all-to-all-start.1 = ((bf16[16,48,512]{2,1,0:T(8,128)(2,1)}), bf16[16,48,512]{2,1,0:T(8,128)(2,1)}, u32[]{:S(2)}, u32[]{:S(2)}) async-start(bf16[16,48,512]{2,1,0:T(8,128)(2,1)} %get-tuple-element.40), calls=%async_computation.1 | async-start | bytes 1572864 | tf_op jit(solution)/shard_map/all_to_all | solution.py:64
  51.4 0.8 fusion.24
  52.3 1.0 copy-done.6
  53.3 5.1 %shard_map.105 = (f32[384,512]{1,0:T(8,128)S(1)}, bf16[4,384,128]{2,1,0:T(8,128)(2,1)S(1)}) custom-call(s32[1]{0:T(128)} %bitcast.core_ref.half_ref, s32[1,4]{1,0:T(1,128)S(1)} %copy-done.14, bf16[384,512]{1,0:T(8,128)(2,1)S(1)} %copy-done.4, bf16[16,400,128]{2,1,0:T(8,128)(2,1)S(1)} %copy-done.1, bf16[16,400,128]{2,1,0:T(8,128)(2,1)} %collective-permute-done.other_ref, ...), custom_call_target="tpu_custom_call" | custom-call | bytes 5373972 | tf_op jit(solution)/shard_map/pallas_call | solution.py:375
  58.5 0.9 copy-done.10
  59.3 6.4 %all-to-all-done.1.recv_ref = bf16[16,48,512]{2,1,0:T(8,128)(2,1)} async-done(((bf16[16,48,512]{2,1,0:T(8,128)(2,1)}), bf16[16,48,512]{2,1,0:T(8,128)(2,1)}, u32[]{:S(2)}, u32[]{:S(2)}) %all-to-all-start.1) | async-done | bytes 786464 | tf_op jit(solution)/shard_map/all_to_all | solution.py:64
  65.7 1.1 copy-done.11
  66.9 0.9 copy-done.12
  67.8 5.8 %shard_map.106 = (bf16[16,144,512]{2,1,0:T(8,128)(2,1)S(1)}, f32[384,512]{1,0:T(8,128)S(1)}, bf16[384,512]{1,0:T(8,128)(2,1)S(1)}) custom-call(s32[1]{0:T(128)} %bitcast.core_ref.half_ref, f32[384,512]{1,0:T(8,128)S(1)} %copy-done.11, bf16[4,384,128]{2,1,0:T(8,128)(2,1)S(1)} %get-tuple-element.39.gated_ref, bf16[16,48,512]{2,1,0:T(8,128)(2,1)} %all-to-all-done.1.recv_ref, ...), custom_call_target="tpu_custom_call" | custom-call | bytes 8783364 | tf_op jit(solution)/shard_map/pallas_call | solution.py:375
  73.7 1.4 copy-done.5
  75.1 2.0 shard_map.107
  77.1 3.5 %multiply_convert_fusion = (bf16[16,384,128]{1,2,0:T(8,128)(2,1)S(1)}, f32[16,384,128]{1,2,0:T(8,128)}) fusion(bf16[16,512,128]{2,1,0:T(8,128)(2,1)S(1)} %get-tuple-element.50, bf16[384,512]{1,0:T(8,128)(2,1)S(1)} %get-tuple-element.49), kind=kOutput, calls=%fused_computation.2 | convolution fusion | flops 809238528 | bytes 7208960 | tf_op jit(solution)/shard_map/dot_general | solution.py:38
  80.6 1.1 select_convert_fusion.1
  83.5 1.3 fusion.35
  84.8 1.5 select_convert_fusion
  86.3 4.7 %all-to-all-start.2 = ((bf16[16,144,512]{2,1,0:T(8,128)(2,1)}), bf16[16,144,512]{2,1,0:T(8,128)(2,1)}, u32[]{:S(2)}, u32[]{:S(2)}) async-start(bf16[16,144,512]{2,1,0:T(8,128)(2,1)} %copy-done.5), calls=%async_computation.2 | async-start | bytes 4718592 | tf_op jit(solution)/shard_map/all_to_all | solution.py:64
  91.0 1.6 fusion.29
  92.6 1.4 fusion.25
  94.1 3.5 %fusion.10 = (f32[384]{0:T(512)S(1)}, f32[384]{0:T(512)S(1)}, f32[384,512]{1,0:T(8,128)S(1)}) fusion(bf16[384,512]{1,0:T(8,128)(2,1)S(1)} %copy-done.4, bf16[16,512,128]{2,1,0:T(8,128)(2,1)S(1)} %copy-done.16, f32[4,384,128]{1,2,0:T(8,128)S(1)} %fusion.25, f32[4,384,128]{1,2,0:T(8,128)S(1)} %fusion.29, f32[4,384,128]{1,2,0:T(8,128)S(1)} %copy-done.18, ...), kind=kOutput, calls=%fused_computation.23 | convolution fusion | flops 815725824 | bytes 9571328 | tf_op jit(solution)/shard_map/dot_general | solution.py:38
  97.6 1.0 fusion.14
  98.6 27.8 %all-to-all-done.2.recv_ref = bf16[16,144,512]{2,1,0:T(8,128)(2,1)} async-done(((bf16[16,144,512]{2,1,0:T(8,128)(2,1)}), bf16[16,144,512]{2,1,0:T(8,128)(2,1)}, u32[]{:S(2)}, u32[]{:S(2)}) %all-to-all-start.2) | async-done | bytes 2359328 | tf_op jit(solution)/shard_map/all_to_all | solution.py:64
  126.4 2.6 %shard_map.108 = (bf16[528,512]{1,0:T(8,128)(2,1)S(1)}, bf16[768,512]{1,0:T(8,128)(2,1)S(1)}, bf16[64,512]{1,0:T(8,128)(2,1)S(1)}, f32[32,512]{1,0:T(8,128)S(1)}) custom-call(s32[1]{0:T(128)} %bitcast.core_ref.half_ref, bf16[16,144,512]{2,1,0:T(8,128)(2,1)} %all-to-all-done.2.recv_ref, bf16[768,1024]{1,0:T(8,128)(2,1)S(1)} %copy-done.3, s32[1,64]{1,0:T(1,128)S(1)} %bitcast.22), custom_call_target="tpu_custom_call" | custom-call | bytes 5390596 | tf_op jit(solution)/shard_map/pallas_call | solution.py:375
  129.0 3.6 %collective-permute-start.1 = (bf16[528,512]{1,0:T(8,128)(2,1)S(1)}, bf16[528,512]{1,0:T(8,128)(2,1)S(1)}, u32[]{:S(2)}, u32[]{:S(2)}) collective-permute-start(bf16[528,512]{1,0:T(8,128)(2,1)S(1)} %get-tuple-element.57), channel_id=1, source_target_pairs={{0,16},{16,0},{32,48},{48,32},{64,80},{80,64},{96,112},{112,96},{1... | collective-permute-start | bytes 1622024 | tf_op jit(solution)/shard_map/ppermute | solution.py:534
  133.3 0.8 collective-permute-done.1.other_ref
  134.3 21.7 %all_to_all.30.recv_ref = bf16[4,144,512]{2,1,0:T(8,128)(2,1)S(1)} all-to-all(bf16[4,144,512]{2,1,0:T(8,128)(2,1)S(1)} %shard_map.110), channel_id=1, replica_groups={{0,32,64,96},{16,48,80,112},{128,160,192,224},{144,176,208,240},{256,28..., dimensions={0} | all-to-all | bytes 1179648 | tf_op jit(solution)/shard_map/all_to_all | solution.py:64
  156.0 25.6 %all_to_all.31.recv_ref = bf16[4,48,512]{2,1,0:T(8,128)(2,1)S(1)} all-to-all(bf16[4,48,512]{2,1,0:T(8,128)(2,1)S(1)} %shard_map.111), channel_id=1, replica_groups={{0,128,256,384},{16,144,272,400},{32,160,288,416},{48,176,304,432},{64,..., dimensions={0} | all-to-all | bytes 393216 | tf_op jit(solution)/shard_map/all_to_all | solution.py:64
  181.6 0.9 shard_map.112
  182.5 6.3 %all-to-all-start.5 = ((bf16[16,32,512]{2,1,0:T(8,128)(2,1)}), bf16[16,32,512]{2,1,0:T(8,128)(2,1)S(1)}, u32[]{:S(2)}, u32[]{:S(2)}) async-start(bf16[16,32,512]{2,1,0:T(8,128)(2,1)} %get-tuple-element.59), calls=%async_computation.5 | async-start | bytes 1048576 | tf_op jit(solution)/shard_map/all_to_all | solution.py:64
  188.8 1.9 collective-permute-start.2
  190.7 2.6 %collective-permute-start.3 = (bf16[16,512]{1,0:T(8,128)(2,1)S(1)}, bf16[16,512]{1,0:T(8,128)(2,1)S(1)}, u32[]{:S(2)}, u32[]{:S(2)}) collective-permute-start(bf16[16,512]{1,0:T(8,128)(2,1)S(1)} %get-tuple-element.58), channel_id=1, source_target_pairs={{0,2},{1,3},{2,0},{3,1},{4,6},{5,7},{6,4},{7,5},{8,10},{9,11},{10,... | collective-permute-start | bytes 49160 | tf_op jit(solution)/shard_map/ppermute | solution.py:558
  193.4 3.8 %collective-permute-start.4 = (bf16[16,512]{1,0:T(8,128)(2,1)S(1)}, bf16[16,512]{1,0:T(8,128)(2,1)S(1)}, u32[]{:S(2)}, u32[]{:S(2)}) collective-permute-start(bf16[16,512]{1,0:T(8,128)(2,1)S(1)} %get-tuple-element.58), channel_id=1, source_target_pairs={{0,3},{1,0},{2,1},{3,2},{4,7},{5,4},{6,5},{7,6},{8,11},{9,8},{10,9... | collective-permute-start | bytes 49160 | tf_op jit(solution)/shard_map/ppermute | solution.py:558
  197.3 1.9 collective-permute-done.4
  199.2 1.9 collective-permute-start.5
  201.1 4.3 %collective-permute-start.6 = (bf16[64,512]{1,0:T(8,128)(2,1)S(1)}, bf16[64,512]{1,0:T(8,128)(2,1)S(1)}, u32[]{:S(2)}, u32[]{:S(2)}) collective-permute-start(bf16[64,512]{1,0:T(8,128)(2,1)S(1)} %get-tuple-element.69), channel_id=1, source_target_pairs={{0,8},{1,9},{2,10},{3,11},{4,12},{5,13},{6,14},{7,15},{8,0},{9,1},... | collective-permute-start | bytes 196616 | tf_op jit(solution)/shard_map/ppermute | solution.py:558
  205.4 3.0 %collective-permute-start.7 = (bf16[64,512]{1,0:T(8,128)(2,1)S(1)}, bf16[64,512]{1,0:T(8,128)(2,1)S(1)}, u32[]{:S(2)}, u32[]{:S(2)}) collective-permute-start(bf16[64,512]{1,0:T(8,128)(2,1)S(1)} %get-tuple-element.69), channel_id=1, source_target_pairs={{0,12},{1,13},{2,14},{3,15},{4,0},{5,1},{6,2},{7,3},{8,4},{9,5},{1... | collective-permute-start | bytes 196616 | tf_op jit(solution)/shard_map/ppermute | solution.py:558
  208.4 2.8 %all-to-all-done.5.grads_ref = bf16[16,32,512]{2,1,0:T(8,128)(2,1)S(1)} async-done(((bf16[16,32,512]{2,1,0:T(8,128)(2,1)}), bf16[16,32,512]{2,1,0:T(8,128)(2,1)S(1)}, u32[]{:S(2)}, u32[]{:S(2)}) %all-to-all-start.5) | async-done | bytes 524320 | tf_op jit(solution)/shard_map/all_to_all | solution.py:64
  211.3 8.4 %collective-permute-start.9 = (bf16[16,32,512]{2,1,0:T(8,128)(2,1)S(1)}, bf16[16,32,512]{2,1,0:T(8,128)(2,1)S(1)}, u32[]{:S(2)}, u32[]{:S(2)}) collective-permute-start(bf16[16,32,512]{2,1,0:T(8,128)(2,1)S(1)} %all-to-all-done.5.grads_ref), channel_id=1, source_target_pairs={{0,16},{16,0},{32,48},{48,32},{64,80},{80,64},{96,112},{112,96},{1... | collective-permute-start | bytes 1572872 | tf_op jit(solution)/shard_map/ppermute | solution.py:563
  219.7 1.9 collective-permute-start.8
  221.8 1.4 finish.2.rest_0_
  223.1 1.4 finish.3
  224.5 1.6 shard_map.113
  (67 shorter events, 5.4 us)
Async XLA Ops:
  0.6 13.4 %copy-start.2 = (bf16[1024,512]{1,0:T(8,128)(2,1)S(1)}, bf16[1024,512]{1,0:T(8,128)(2,1)}, u32[]{:S(2)}) copy-start(bf16[1024,512]{1,0:T(8,128)(2,1)} %items_ref.5) | copy-start | bytes 3145732
  6.4 28.1 %all-to-all-start = ((bf16[16,400,128]{2,1,0:T(8,128)(2,1)}), bf16[16,400,128]{2,1,0:T(8,128)(2,1)S(1)}, u32[]{:S(2)}, u32[]{:S(2)}) async-start(bf16[16,400,128]{2,1,0:T(8,128)(2,1)} %get-tuple-element.33), calls=%async_computation | async-start | bytes 3276800 | tf_op jit(solution)/shard_map/all_to_all | solution.py:64
  15.6 35.6 %copy-start.14 = (s32[1,4]{1,0:T(1,128)S(1)}, s32[1,4]{1,0:T(1,128)}, u32[]{:S(2)}) copy-start(s32[1,4]{1,0:T(1,128)} %lengths_ref.1) | copy-start | bytes 52
  15.6 36.7 %copy-start.4 = (bf16[384,512]{1,0:T(8,128)(2,1)S(1)}, bf16[384,512]{1,0:T(8,128)(2,1)}, u32[]{:S(2)}) copy-start(bf16[384,512]{1,0:T(8,128)(2,1)} %tokens_ref.3) | copy-start | bytes 1179652
  34.5 1.2 copy-start
  39.7 12.6 %copy-start.1 = (bf16[16,400,128]{2,1,0:T(8,128)(2,1)S(1)}, bf16[16,400,128]{2,1,0:T(8,128)(2,1)}, u32[]{:S(2)}) copy-start(bf16[16,400,128]{2,1,0:T(8,128)(2,1)} %copy-done) | copy-start | bytes 4915204
  39.7 12.5 %collective-permute-start = (bf16[16,400,128]{2,1,0:T(8,128)(2,1)}, bf16[16,400,128]{2,1,0:T(8,128)(2,1)}, u32[]{:S(2)}, u32[]{:S(2)}) collective-permute-start(bf16[16,400,128]{2,1,0:T(8,128)(2,1)} %copy-done), channel_id=1, source_target_pairs={{0,16},{16,0},{32,48},{48,32},{64,80},{80,64},{96,112},{112,96},{1... | collective-permute-start | bytes 4915208 | tf_op jit(solution)/shard_map/ppermute | solution.py:431
  46.7 19.1 %all-to-all-start.1 = ((bf16[16,48,512]{2,1,0:T(8,128)(2,1)}), bf16[16,48,512]{2,1,0:T(8,128)(2,1)}, u32[]{:S(2)}, u32[]{:S(2)}) async-start(bf16[16,48,512]{2,1,0:T(8,128)(2,1)} %get-tuple-element.40), calls=%async_computation.1 | async-start | bytes 1572864 | tf_op jit(solution)/shard_map/all_to_all | solution.py:64
  52.3 1.0 copy-start.6
  58.4 0.9 copy-start.10
  65.7 1.1 copy-start.11
  66.9 0.9 copy-start.12
  73.7 1.4 copy-start.5
  75.1 2.0 copy-start.8
  77.1 3.5 %copy-start.15 = (bf16[16,512,128]{2,1,0:T(8,128)(2,1)}, bf16[16,512,128]{2,1,0:T(8,128)(2,1)S(1)}, u32[]{:S(2)}) copy-start(bf16[16,512,128]{2,1,0:T(8,128)(2,1)S(1)} %get-tuple-element.50) | copy-start | bytes 6291460
  77.1 3.5 %copy-start.19 = (pred[384,384]{1,0:T(8,128)(4,1)S(1)}, pred[384,384]{1,0:T(8,128)(4,1)}, u32[]{:S(2)}) copy-start(pred[384,384]{1,0:T(8,128)(4,1)} %fusion.24) | copy-start | bytes 442372
  80.6 4.2 %copy-start.17 = (bf16[16,384,128]{1,2,0:T(8,128)(2,1)}, bf16[16,384,128]{1,2,0:T(8,128)(2,1)S(1)}, u32[]{:S(2)}) copy-start(bf16[16,384,128]{1,2,0:T(8,128)(2,1)S(1)} %get-tuple-element.81) | copy-start | bytes 4718596
  80.6 1.4 copy-start.7
  86.3 40.2 %all-to-all-start.2 = ((bf16[16,144,512]{2,1,0:T(8,128)(2,1)}), bf16[16,144,512]{2,1,0:T(8,128)(2,1)}, u32[]{:S(2)}, u32[]{:S(2)}) async-start(bf16[16,144,512]{2,1,0:T(8,128)(2,1)} %copy-done.5), calls=%async_computation.2 | async-start | bytes 4718592 | tf_op jit(solution)/shard_map/all_to_all | solution.py:64
  91.0 3.1 %copy-start.16 = (bf16[16,512,128]{2,1,0:T(8,128)(2,1)S(1)}, bf16[16,512,128]{2,1,0:T(8,128)(2,1)}, u32[]{:S(2)}) copy-start(bf16[16,512,128]{2,1,0:T(8,128)(2,1)} %copy-done.15) | copy-start | bytes 6291460
  91.0 3.1 %copy-start.18 = (f32[4,384,128]{1,2,0:T(8,128)S(1)}, f32[4,384,128]{1,2,0:T(8,128)}, u32[]{:S(2)}) copy-start(f32[4,384,128]{1,2,0:T(8,128)} %fusion.35) | copy-start | bytes 2359300
  94.1 3.6 %copy-start.9 = (f32[384,512]{1,0:T(8,128)S(1)}, f32[384,512]{1,0:T(8,128)}, u32[]{:S(2)}) copy-start(f32[384,512]{1,0:T(8,128)} %copy-done.8) | copy-start | bytes 2359300
  97.6 28.8 %copy-start.3 = (bf16[768,1024]{1,0:T(8,128)(2,1)S(1)}, bf16[768,1024]{1,0:T(8,128)(2,1)}, u32[]{:S(2)}) copy-start(bf16[768,1024]{1,0:T(8,128)(2,1)} %get-tuple-element.52.pick_ref) | copy-start | bytes 4718596
  97.6 28.8 %copy-start.13 = (s32[64]{0:T(128)S(1)}, s32[64]{0:T(128)}, u32[]{:S(2)}) copy-start(s32[64]{0:T(128)} %param.15) | copy-start | bytes 772
  129.0 5.2 %collective-permute-start.1 = (bf16[528,512]{1,0:T(8,128)(2,1)S(1)}, bf16[528,512]{1,0:T(8,128)(2,1)S(1)}, u32[]{:S(2)}, u32[]{:S(2)}) collective-permute-start(bf16[528,512]{1,0:T(8,128)(2,1)S(1)} %get-tuple-element.57), channel_id=1, source_target_pairs={{0,16},{16,0},{32,48},{48,32},{64,80},{80,64},{96,112},{112,96},{1... | collective-permute-start | bytes 1622024 | tf_op jit(solution)/shard_map/ppermute | solution.py:534
  182.5 28.8 %all-to-all-start.5 = ((bf16[16,32,512]{2,1,0:T(8,128)(2,1)}), bf16[16,32,512]{2,1,0:T(8,128)(2,1)S(1)}, u32[]{:S(2)}, u32[]{:S(2)}) async-start(bf16[16,32,512]{2,1,0:T(8,128)(2,1)} %get-tuple-element.59), calls=%async_computation.5 | async-start | bytes 1048576 | tf_op jit(solution)/shard_map/all_to_all | solution.py:64
  188.8 8.5 %collective-permute-start.2 = (bf16[16,512]{1,0:T(8,128)(2,1)S(1)}, bf16[16,512]{1,0:T(8,128)(2,1)S(1)}, u32[]{:S(2)}, u32[]{:S(2)}) collective-permute-start(bf16[16,512]{1,0:T(8,128)(2,1)S(1)} %get-tuple-element.58), channel_id=1, source_target_pairs={{0,1},{1,2},{2,3},{3,0},{4,5},{5,6},{6,7},{7,4},{8,9},{9,10},{10,1... | collective-permute-start | bytes 49160 | tf_op jit(solution)/shard_map/ppermute | solution.py:558
  190.7 6.5 %collective-permute-start.3 = (bf16[16,512]{1,0:T(8,128)(2,1)S(1)}, bf16[16,512]{1,0:T(8,128)(2,1)S(1)}, u32[]{:S(2)}, u32[]{:S(2)}) collective-permute-start(bf16[16,512]{1,0:T(8,128)(2,1)S(1)} %get-tuple-element.58), channel_id=1, source_target_pairs={{0,2},{1,3},{2,0},{3,1},{4,6},{5,7},{6,4},{7,5},{8,10},{9,11},{10,... | collective-permute-start | bytes 49160 | tf_op jit(solution)/shard_map/ppermute | solution.py:558
  193.4 5.8 %collective-permute-start.4 = (bf16[16,512]{1,0:T(8,128)(2,1)S(1)}, bf16[16,512]{1,0:T(8,128)(2,1)S(1)}, u32[]{:S(2)}, u32[]{:S(2)}) collective-permute-start(bf16[16,512]{1,0:T(8,128)(2,1)S(1)} %get-tuple-element.58), channel_id=1, source_target_pairs={{0,3},{1,0},{2,1},{3,2},{4,7},{5,4},{6,5},{7,6},{8,11},{9,8},{10,9... | collective-permute-start | bytes 49160 | tf_op jit(solution)/shard_map/ppermute | solution.py:558
  199.2 20.5 %collective-permute-start.5 = (bf16[64,512]{1,0:T(8,128)(2,1)S(1)}, bf16[64,512]{1,0:T(8,128)(2,1)S(1)}, u32[]{:S(2)}, u32[]{:S(2)}) collective-permute-start(bf16[64,512]{1,0:T(8,128)(2,1)S(1)} %get-tuple-element.69), channel_id=1, source_target_pairs={{0,4},{1,5},{2,6},{3,7},{4,8},{5,9},{6,10},{7,11},{8,12},{9,13},{1... | collective-permute-start | bytes 196616 | tf_op jit(solution)/shard_map/ppermute | solution.py:558
  201.1 18.6 %collective-permute-start.6 = (bf16[64,512]{1,0:T(8,128)(2,1)S(1)}, bf16[64,512]{1,0:T(8,128)(2,1)S(1)}, u32[]{:S(2)}, u32[]{:S(2)}) collective-permute-start(bf16[64,512]{1,0:T(8,128)(2,1)S(1)} %get-tuple-element.69), channel_id=1, source_target_pairs={{0,8},{1,9},{2,10},{3,11},{4,12},{5,13},{6,14},{7,15},{8,0},{9,1},... | collective-permute-start | bytes 196616 | tf_op jit(solution)/shard_map/ppermute | solution.py:558
  205.4 14.3 %collective-permute-start.7 = (bf16[64,512]{1,0:T(8,128)(2,1)S(1)}, bf16[64,512]{1,0:T(8,128)(2,1)S(1)}, u32[]{:S(2)}, u32[]{:S(2)}) collective-permute-start(bf16[64,512]{1,0:T(8,128)(2,1)S(1)} %get-tuple-element.69), channel_id=1, source_target_pairs={{0,12},{1,13},{2,14},{3,15},{4,0},{5,1},{6,2},{7,3},{8,4},{9,5},{1... | collective-permute-start | bytes 196616 | tf_op jit(solution)/shard_map/ppermute | solution.py:558
  211.3 11.9 %collective-permute-start.9 = (bf16[16,32,512]{2,1,0:T(8,128)(2,1)S(1)}, bf16[16,32,512]{2,1,0:T(8,128)(2,1)S(1)}, u32[]{:S(2)}, u32[]{:S(2)}) collective-permute-start(bf16[16,32,512]{2,1,0:T(8,128)(2,1)S(1)} %all-to-all-done.5.grads_ref), channel_id=1, source_target_pairs={{0,16},{16,0},{32,48},{48,32},{64,80},{80,64},{96,112},{112,96},{1... | collective-permute-start | bytes 1572872 | tf_op jit(solution)/shard_map/ppermute | solution.py:563
  219.7 4.8 %collective-permute-start.8 = (bf16[256,512]{1,0:T(8,128)(2,1)S(1)}, bf16[256,512]{1,0:T(8,128)(2,1)S(1)}, u32[]{:S(2)}, u32[]{:S(2)}) collective-permute-start(bf16[256,512]{1,0:T(8,128)(2,1)S(1)} %constant_dynamic-update-slice_fusion.4.mine_ref), channel_id=1, source_target_pairs={{0,16},{16,0},{32,48},{48,32},{64,80},{80,64},{96,112},{112,96},{1... | collective-permute-start | bytes 786440 | tf_op jit(solution)/shard_map/ppermute | solution.py:562
